TPU v7x, 32 devices: a whole 2x2x4 slice. The times are simulated.
32 devices in a mesh: dp: 4 (over y, x), fsdp: 8 (over z, core).
Axes of the slice: x: 2, y: 2, z: 4, core: 2. Of those that a mesh axis runs over, the one named last changes fastest.
Arguments:
- stream_x: bfloat16 [32768, 512], P(('dp', 'fsdp')), may hold values from -6 to 6
- stream_y: bfloat16 [32768, 512], P(('dp', 'fsdp')), may hold values from -6 to 6
- cotangent: bfloat16 [32768, 512], P(('dp', 'fsdp')), may hold values from -6 to 6
- doc_lengths: int32 [32, 16], P(('dp', 'fsdp')), may hold values from 1 to 512, 1024 in all within a row
- query_weight: bfloat16 [512, 512], P(('dp', 'fsdp')), may hold values from -0.25 to 0.25
- query_bias: bfloat16 [512], P(('dp', 'fsdp')), may hold values from -2.5 to 2.5
- key_weight: bfloat16 [512, 512], P(('dp', 'fsdp')), may hold values from -0.25 to 0.25
- value_weight: bfloat16 [512, 512], P(('dp', 'fsdp')), may hold values from -0.25 to 0.25
- value_bias: bfloat16 [512], P(('dp', 'fsdp')), may hold values from -3 to 3
- output_weight: bfloat16 [512, 512], P(('dp', 'fsdp')), may hold values from -1 to 1
- output_bias: bfloat16 [512], P(('dp', 'fsdp')), may hold values from -2.5 to 2.5
- first_gain: bfloat16 [512], P(('dp', 'fsdp')), may hold values from 0.099609375 to 1.8984375
- first_shift: bfloat16 [512], P(('dp', 'fsdp')), may hold values from -2.5 to 2.5
- up_weight: bfloat16 [512, 2048], P(('dp', 'fsdp')), may hold values from -0.25 to 0.25
- up_bias: bfloat16 [2048], P(('dp', 'fsdp')), may hold values from -3 to 3
- down_weight: bfloat16 [2048, 512], P(('dp', 'fsdp')), may hold values from -0.1875 to 0.1875
- down_bias: bfloat16 [512], P(('dp', 'fsdp')), may hold values from -2.5 to 2.5
- second_gain: bfloat16 [512], P(('dp', 'fsdp')), may hold values from 0.099609375 to 1.8984375
- second_shift: bfloat16 [512], P(('dp', 'fsdp')), may hold values from -2.5 to 2.5
- final_gain: bfloat16 [512], P(('dp', 'fsdp')), may hold values from 0.099609375 to 1.8984375
- final_shift: bfloat16 [512], P(('dp', 'fsdp')), may hold values from -2.5 to 2.5
Outputs:
- block_out: bfloat16 [32768, 512], P(('dp', 'fsdp'))
- grad_x: float32 [32768, 512], P(('dp', 'fsdp'))
- grad_y: float32 [32768, 512], P(('dp', 'fsdp'))
- query_weight_grad: float32 [512, 512], P(('dp', 'fsdp'))
- query_bias_grad: float32 [512], P(('dp', 'fsdp'))
- key_weight_grad: float32 [512, 512], P(('dp', 'fsdp'))
- value_weight_grad: float32 [512, 512], P(('dp', 'fsdp'))
- value_bias_grad: float32 [512], P(('dp', 'fsdp'))
- output_weight_grad: float32 [512, 512], P(('dp', 'fsdp'))
- output_bias_grad: float32 [512], P(('dp', 'fsdp'))
- first_gain_grad: float32 [512], P(('dp', 'fsdp'))
- first_shift_grad: float32 [512], P(('dp', 'fsdp'))
- up_weight_grad: float32 [512, 2048], P(('dp', 'fsdp'))
- up_bias_grad: float32 [2048], P(('dp', 'fsdp'))
- down_weight_grad: float32 [2048, 512], P(('dp', 'fsdp'))
- down_bias_grad: float32 [512], P(('dp', 'fsdp'))
- second_gain_grad: float32 [512], P(('dp', 'fsdp'))
- second_shift_grad: float32 [512], P(('dp', 'fsdp'))
- final_gain_grad: float32 [512], P(('dp', 'fsdp'))
- final_shift_grad: float32 [512], P(('dp', 'fsdp'))
Inputs may be any that keep to these rules, and one draw needn't show every extreme that they name: `doc_lengths`: row p lists the lengths of the 16 sequences packed in order into the 1024 tokens of pack p; each row sums to 1024, and the longest of every row is exactly 512.
All inputs are finite; a program needn't handle non-finite values.
Results may differ from a plain program's by a relative error of at most 0.012.
The roundings to bfloat16 on the way count: a program that leaves them out, or rounds other values in their place, can miss the bound.
Values may be sent and summed in bfloat16 or wider, within the bound.
No kernel may reach another device: no remote copies, remote signals or barrier semaphores. Data moves between devices by JAX's collectives and lax.ppermute only.
A program may use at most 128 MiB of HBM per device.

v0:
```python
import functools
import math

import jax
import jax.numpy as jnp
from jax import lax
from jax.experimental import pallas as pl
from jax.experimental.pallas import tpu as pltpu
from jax.sharding import PartitionSpec as P

HEADS = 8
LONGEST = 512
BLOCK = 256
TILE = 512
LANES = 128
AXES = ("dp", "fsdp")
SHARD = 16
VECTORS = 8

epsilon = 1e-05
neg_large = -1e30
log2_e = 1.4426950408889634
low = jnp.bfloat16
wide = jnp.float32

BIAS_QUERY, BIAS_VALUE, BIAS_OUTPUT, GAIN_FIRST, SHIFT_FIRST, BIAS_DOWN = range(6)
GAIN_SECOND, SHIFT_SECOND, GAIN_FINAL, SHIFT_FINAL, BIAS_UP = 6, 7, 8, 9, 16


def nn(left, right):
    return lax.dot_general(left, right, (((1,), (0,)), ((), ())), preferred_element_type=wide)


def nt(left, right):
    return lax.dot_general(left, right, (((1,), (1,)), ((), ())), preferred_element_type=wide)


def tn(left, right):
    return lax.dot_general(left, right, (((0,), (0,)), ((), ())), preferred_element_type=wide)


def column_sum(values):
    return jnp.sum(values.astype(wide), axis=0, keepdims=True)


def normalize(values):
    centre = jnp.mean(values, axis=-1, keepdims=True)
    shifted = values - centre
    spread = jnp.mean(shifted * shifted, axis=-1, keepdims=True)
    scaler = lax.rsqrt(spread + epsilon)
    return (shifted * scaler, scaler)


def norm_back(upstream, normed, scaler):
    return scaler * (
        upstream
        - jnp.mean(upstream, axis=-1, keepdims=True)
        - normed * jnp.mean(upstream * normed, axis=-1, keepdims=True)
    )


def call(kernel, name, weight, mebibytes, **settings):
    return pl.pallas_call(
        kernel,
        name=name,
        compiler_params=pltpu.CompilerParams(vmem_limit_bytes=mebibytes << 20),
        cost_estimate=pl.CostEstimate(
            flops=weight * 250_000_000, transcendentals=0, bytes_accessed=1 << 10
        ),
        **settings,
    )


SCALARS = pl.BlockSpec(memory_space=pltpu.SMEM)
ANYWHERE = pl.BlockSpec(memory_space=pl.ANY)


def fetch(ids_ref, parts, others, whole, semaphores, rows):
    digit, core = ids_ref[0], ids_ref[1]
    copies = []
    for k, (part, other) in enumerate(zip(parts, others)):
        for n, (source, which) in enumerate(((part, core), (other, 1 - core))):
            copies.append(
                pltpu.make_async_copy(
                    source.at[:, rows],
                    whole.at[digit ^ k, :, which, rows],
                    semaphores.at[2 * k + n],
                )
            )
    return copies


def deliver(ids_ref, whole, kept, away, semaphores):
    digit, core = ids_ref[0], ids_ref[1]
    copies = []
    for k in range(whole.shape[0]):
        for n, (target, which) in enumerate(((kept, core), (away, 1 - core))):
            copies.append(
                pltpu.make_async_copy(
                    whole.at[digit ^ k, :, which], target.at[k], semaphores.at[2 * k + n]
                )
            )
    for copy in copies:
        copy.start()
    for copy in copies:
        copy.wait()


def pack_vectors(sums, shards, size, tail_sums, tail_size):
    lane = lax.broadcasted_iota(jnp.int32, (VECTORS, LANES), 1)
    row = lax.broadcasted_iota(jnp.int32, (VECTORS, LANES), 0)
    tiles = []
    for j in range(shards):
        place, shift = divmod(j * size, LANES)
        tile = sums[:, place * LANES : (place + 1) * LANES]
        tile = pltpu.roll(tile, (LANES - shift) % LANES, 1) if shift else tile
        tile = jnp.where(lane < size, tile, 0.0)
        if tail_sums is not None:
            width = sums.shape[1]
            line, place = divmod(j * tail_size, width)
            place, shift = divmod(place, LANES)
            last = tail_sums[:, place * LANES : (place + 1) * LANES]
            last = pltpu.roll(last, (LANES - shift) % LANES, 1) if shift else last
            last = jnp.where(lane < tail_size, last[line : line + 1, :], 0.0)
            tile = jnp.where(row == VECTORS - 1, last, tile)
        tiles.append(tile)
    return tiles


def fixed(shape):
    zeros = (0,) * len(shape)
    return pl.BlockSpec(shape, lambda p: zeros)


def one_head(values, number, size):
    lane = lax.broadcasted_iota(jnp.int32, values.shape, 1)
    mine = (lane >= number * size) & (lane < (number + 1) * size)
    return jnp.where(mine, values, jnp.zeros_like(values))


def key_span(number):
    return max(0, (number * BLOCK - (LONGEST - 1)) // BLOCK * BLOCK), (number + 1) * BLOCK


def probabilities(scores):
    peak = jnp.max(scores, axis=0, keepdims=True)
    expon = jnp.exp2((scores - peak) * log2_e)
    return expon * (1.0 / jnp.sum(expon, axis=0, keepdims=True))


def unpack_vectors(tile, shards, size, tail_size):
    width = shards * size
    groups = [[jnp.zeros((VECTORS, LANES), wide) for _ in range(width // LANES)] for _ in range(2)]
    tails = [jnp.zeros((VECTORS, LANES), wide) for _ in range(shards * tail_size // LANES)]
    for j in range(shards):
        packed = tile(j).astype(wide)
        place, shift = divmod(j * size, LANES)
        for n, group in enumerate(groups):
            part = packed[:, n * LANES : (n + 1) * LANES]
            group[place] += pltpu.roll(part, shift, 1) if shift else part
        place, shift = divmod(j * tail_size, LANES)
        part = packed[:, 2 * LANES : 3 * LANES]
        tails[place] += pltpu.roll(part, shift, 1) if shift else part
    per = width // LANES
    lines = [
        jnp.concatenate([tail[:1] for tail in tails[n * per : (n + 1) * per]], axis=1)
        for n in range(len(tails) // per)
    ]
    lines.append(jnp.zeros((VECTORS - len(lines), width), wide))
    return jnp.concatenate(
        [jnp.concatenate(group, axis=1) for group in groups] + lines, axis=0
    )


def attend_kernel(size, tail_size, ids_ref, x_ref, hide_ref, *refs):
    parts, others = refs[:4], refs[4:8]
    q_ref, k_ref, v_ref, context_ref, table_ref, whole, semaphores = refs[8:]
    pair = pl.program_id(0)
    x = x_ref[...]
    length, width = x.shape

    @pl.when(pair == 0)
    def _():
        copies = fetch(ids_ref, parts, others, whole, semaphores, slice(None))
        for copy in copies:
            copy.start()
        for copy in copies:
            copy.wait()
        chips = whole.shape[1]

        def tile(j):
            return whole[j // (2 * chips), j // 2 % chips, j % 2, 3 * SHARD :, :]

        table_ref[...] = unpack_vectors(tile, width // SHARD, SHARD, tail_size)

    here = pl.ds(pl.multiple_of(pair * LANES, LANES), LANES)

    def projected(n):
        return nn(x, whole[:, :, :, n * SHARD : (n + 1) * SHARD, here].reshape(width, LANES))

    queries = (projected(0) + table_ref[BIAS_QUERY : BIAS_QUERY + 1, here]).astype(low)
    queries = (queries * (1.0 / math.sqrt(size))).astype(low)
    keys = projected(1).astype(low)
    values = (projected(2) + table_ref[BIAS_VALUE : BIAS_VALUE + 1, here]).astype(low)
    q_ref[...] = queries
    k_ref[...] = keys
    v_ref[...] = values
    turned = values.T
    for number in range(length // BLOCK):
        start, end = key_span(number)
        rows = slice(number * BLOCK, end)
        mixed = []
        for head in range(LANES // size):
            chosen = one_head(queries[rows], head, size)
            scores = nt(keys[start:end], chosen) + hide_ref[start:end, rows]
            weights = probabilities(scores).astype(low)
            mixed.append(nn(turned[head * size : (head + 1) * size, start:end], weights))
        context_ref[rows, :] = jnp.concatenate(mixed, axis=0).T.astype(low)


def attend(ids, x, parts, others, hide, size, tail_size):
    length, width = x.shape
    out = pl.BlockSpec((length, LANES), lambda p: (0, p))
    chips, rows, _ = parts[0].shape
    return call(
        functools.partial(attend_kernel, size, tail_size),
        "attend",
        23,
        32,
        grid=(width // LANES,),
        in_specs=[SCALARS, fixed(x.shape), fixed(hide.shape)] + [ANYWHERE] * 8,
        out_specs=[out] * 4 + [fixed((3 * VECTORS, width))],
        out_shape=[jax.ShapeDtypeStruct((length, width), low)] * 4
        + [jax.ShapeDtypeStruct((3 * VECTORS, width), wide)],
        scratch_shapes=[
            pltpu.VMEM((4, chips, 2, rows, width), low),
            pltpu.SemaphoreType.DMA((8,)),
        ],
    )(ids, x, hide, *parts, *others)


def attend_back_kernel(
    size,
    q_ref,
    k_ref,
    v_ref,
    incoming_ref,
    hide_ref,
    dq_ref,
    dk_ref,
    dv_ref,
    key_total,
    value_total,
):
    queries, keys, values, incoming = q_ref[...], k_ref[...], v_ref[...], incoming_ref[...]
    length = queries.shape[0]
    turned = keys.T
    key_total[...] = jnp.zeros_like(key_total)
    value_total[...] = jnp.zeros_like(value_total)
    for number in range(length // BLOCK):
        start, end = key_span(number)
        rows = slice(number * BLOCK, end)
        parts = []
        for head in range(LANES // size):
            chosen = one_head(queries[rows], head, size)
            arriving = one_head(incoming[rows], head, size)
            scores = nt(keys[start:end], chosen) + hide_ref[start:end, rows]
            attention = probabilities(scores)
            weight_grad = nt(values[start:end], arriving)
            balance = jnp.sum(attention * weight_grad, axis=0, keepdims=True)
            score_grad = (attention * (weight_grad - balance)).astype(low)
            key_total[start:end, :] += nn(score_grad, chosen)
            value_total[start:end, :] += nn(attention.astype(low), arriving)
            parts.append(nn(turned[head * size : (head + 1) * size, start:end], score_grad))
        dq_ref[rows, :] = (jnp.concatenate(parts, axis=0).T * (1.0 / math.sqrt(size))).astype(low)
    dk_ref[...] = key_total[...].astype(low)
    dv_ref[...] = value_total[...].astype(low)


def attend_back(queries, keys, values, incoming, hide, size, first, count):
    length = queries.shape[0]
    given = pl.BlockSpec((length, LANES), lambda p: (0, p + first))
    out = pl.BlockSpec((length, LANES), lambda p: (0, p))
    return call(
        functools.partial(attend_back_kernel, size),
        "attend_back",
        7 * count,
        24,
        grid=(count,),
        in_specs=[given] * 4 + [fixed(hide.shape)],
        out_specs=[out] * 3,
        out_shape=[jax.ShapeDtypeStruct((length, count * LANES), low)] * 3,
        scratch_shapes=[pltpu.VMEM((length, LANES), wide)] * 2,
    )(queries, keys, values, incoming, hide)


def middle_kernel(ids_ref, x_ref, y_ref, cotangent_ref, context_ref, table_ref, *refs):
    parts, others = refs[:4], refs[4:8]
    out_ref, grad_y_ref, back_ref, context_grad_ref, kept_ref, away_ref = refs[8:14]
    whole, full, hidden_all, hidden_grad_all, first_all, feed_grad_all = refs[14:20]
    slopes, output_total, sums_total, semaphores = refs[20:]
    step = pl.program_id(0)
    rows, width = x_ref.shape
    inner = hidden_all.shape[1]
    columns = inner // width
    chips = whole.shape[1]
    share = SHARD * columns
    sections = [slice(2 * share, 2 * share + SHARD), slice(share, 2 * share), slice(0, share)]
    copies = [
        fetch(ids_ref, parts, others, whole, semaphores.at[n], section)
        for n, section in enumerate(sections)
    ]

    @pl.when(step == 0)
    def _():
        for group in copies:
            for copy in group:
                copy.start()

    def arrive(n):
        @pl.when(step == 0)
        def _():
            for copy in copies[n]:
                copy.wait()

    def output():
        return whole[:, :, :, sections[0], :].reshape(width, width)

    def up(c):
        start = share + c * SHARD
        return whole[:, :, :, start : start + SHARD, :].reshape(width, width)

    def down(c):
        shards = whole.shape[0] // columns
        return whole[c * shards : (c + 1) * shards, :, :, :share, :].reshape(width, width)

    def line(number):
        return table_ref[number : number + 1, :]

    here = pl.ds(pl.multiple_of(step * rows, rows), rows)
    context = context_ref[...]
    arrive(0)
    branch = nn(context, output()) + line(BIAS_OUTPUT)
    first_normed, first_scale = normalize(x_ref[...].astype(wide) + branch)
    first_out = first_normed * line(GAIN_FIRST) + line(SHIFT_FIRST)
    first_low = first_out.astype(low)
    first_all[here, :] = first_low
    feed = jnp.zeros((rows, width), wide)
    arrive(1)
    arrive(2)
    for c in range(columns):
        units = slice(c * width, (c + 1) * width)
        before = nn(first_low, up(c)) + line(BIAS_UP + c)
        half = 0.5 * (1.0 + lax.erf(before * 0.7071067811865476))
        hidden = (before * half).astype(low)
        slopes[:, units] = half + before * jnp.exp(-0.5 * before * before) * 0.3989422804014327
        hidden_all[here, units] = hidden
        feed = feed + nn(hidden, down(c))
    feed = feed + line(BIAS_DOWN)
    second_normed, second_scale = normalize(first_out + feed)
    final_normed, final_scale = normalize(y_ref[...].astype(wide) + branch + feed)
    out_ref[...] = (
        second_normed * line(GAIN_SECOND)
        + line(SHIFT_SECOND)
        + final_normed * line(GAIN_FINAL)
        + line(SHIFT_FINAL)
    ).astype(low)
    upstream = cotangent_ref[...].astype(wide)
    grad_y = norm_back(upstream * line(GAIN_FINAL), final_normed, final_scale)
    grad_y_ref[...] = grad_y
    second_back = norm_back(upstream * line(GAIN_SECOND), second_normed, second_scale)
    feed_grad = (second_back + grad_y).astype(low)
    feed_grad_all[here, :] = feed_grad
    first_grad = second_back
    up_bias = []
    for c in range(columns):
        units = slice(c * width, (c + 1) * width)
        hidden_grad = (nt(feed_grad, down(c)) * slopes[:, units]).astype(low)
        hidden_grad_all[here, units] = hidden_grad
        up_bias.append(column_sum(hidden_grad))
        first_grad = first_grad + nt(hidden_grad, up(c))
    first_back = norm_back(first_grad * line(GAIN_FIRST), first_normed, first_scale)
    back_ref[...] = first_back
    branch_grad = (first_back + grad_y).astype(low)
    context_grad_ref[...] = nt(branch_grad, output()).astype(low)
    sums = jnp.concatenate(
        [
            column_sum(branch_grad),
            column_sum(first_grad * first_normed),
            column_sum(first_grad),
            column_sum(feed_grad),
            column_sum(upstream * second_normed),
            column_sum(upstream),
            column_sum(upstream * final_normed),
            jnp.zeros((1, width), wide),
        ]
        + up_bias
        + [jnp.zeros((VECTORS - columns, width), wide)],
        axis=0,
    )
    output_part = tn(context, branch_grad)

    @pl.when(step == 0)
    def _():
        sums_total[...] = sums
        output_total[...] = output_part

    @pl.when(step > 0)
    def _():
        sums_total[...] += sums
        output_total[...] += output_part

    @pl.when(step == pl.num_programs(0) - 1)
    def _():
        split = whole.shape[:3]
        shards = width // SHARD
        for c in range(columns):
            units = slice(c * width, (c + 1) * width)
            part = tn(hidden_all[:, units], feed_grad_all[...]).astype(low)
            per = split[0] // columns
            full[c * per : (c + 1) * per, :, :, :share, :] = part.reshape(
                (per,) + split[1:] + (share, width)
            )
            part = tn(first_all[...], hidden_grad_all[:, units]).astype(low)
            start = share + c * SHARD
            full[:, :, :, start : start + SHARD, :] = part.reshape(split + (SHARD, width))
        full[:, :, :, sections[0], :] = (
            output_total[...].astype(low).reshape(split + (SHARD, width))
        )
        lines = slice(2 * share + SHARD, 2 * share + SHARD + VECTORS)
        full[:, :, :, lines, :] = jnp.zeros(split + (VECTORS, width), low)
        tiles = pack_vectors(
            sums_total[:VECTORS], shards, SHARD, sums_total[VECTORS:], share
        )
        for j, tile in enumerate(tiles):
            full[j // (2 * chips), j // 2 % chips, j % 2, lines, :LANES] = tile.astype(low)
        deliver(ids_ref, full, kept_ref, away_ref, semaphores.at[0])


def middle(ids, x, y, cotangent, context, table, parts, others, inner):
    length, width = x.shape
    block = pl.BlockSpec((TILE, width), lambda p: (p, 0))
    chips, rows, _ = parts[0].shape
    packed = jax.ShapeDtypeStruct((4, chips, rows + VECTORS, width), low)
    return call(
        middle_kernel,
        "middle",
        29,
        56,
        grid=(length // TILE,),
        in_specs=[SCALARS] + [block] * 4 + [fixed(table.shape)] + [ANYWHERE] * 8,
        out_specs=[block] * 4 + [ANYWHERE] * 2,
        out_shape=[
            jax.ShapeDtypeStruct((length, width), kind) for kind in (low, wide, wide, low)
        ]
        + [packed] * 2,
        scratch_shapes=[
            pltpu.VMEM((4, chips, 2, rows, width), low),
            pltpu.VMEM((4, chips, 2, rows + VECTORS, width), low),
            pltpu.VMEM((length, inner), low),
            pltpu.VMEM((length, inner), low),
            pltpu.VMEM((length, width), low),
            pltpu.VMEM((length, width), low),
            pltpu.VMEM((TILE, inner), wide),
            pltpu.VMEM((width, width), wide),
            pltpu.VMEM((2 * VECTORS, width), wide),
            pltpu.SemaphoreType.DMA((3, 8)),
        ],
    )(ids, x, y, cotangent, context, table, *parts, *others)


def weights_kernel(calls, ids_ref, x_ref, *refs):
    parts = [refs[3 * n : 3 * n + 3] for n in range(calls)]
    kept_ref, away_ref, full, semaphores = refs[3 * calls :]
    x = x_ref[...]
    width = x.shape[1]
    split = full.shape[:3]
    chips = split[1]
    sums = []
    for n in range(3):
        whole = jnp.concatenate([part[n][...] for part in parts], axis=1)
        grad = tn(x, whole).astype(low)
        full[:, :, :, n * SHARD : (n + 1) * SHARD, :] = grad.reshape(split + (SHARD, width))
        if n != 1:
            sums.append(column_sum(whole))
    sums = jnp.concatenate(sums + [jnp.zeros((VECTORS - 2, width), wide)], axis=0)
    lines = slice(3 * SHARD, 3 * SHARD + VECTORS)
    full[:, :, :, lines, :] = jnp.zeros(split + (VECTORS, width), low)
    for j, tile in enumerate(pack_vectors(sums, width // SHARD, SHARD, None, 0)):
        full[j // (2 * chips), j // 2 % chips, j % 2, lines, :LANES] = tile.astype(low)
    deliver(ids_ref, full, kept_ref, away_ref, semaphores)


def weight_grads(ids, x, parts):
    length, width = x.shape
    flat = [array for part in parts for array in part]
    chips, rows = width // SHARD // 8, 3 * SHARD + VECTORS
    return call(
        functools.partial(weights_kernel, len(parts)),
        "weights",
        5,
        24,
        grid=(1,),
        in_specs=[SCALARS] + [fixed(array.shape) for array in [x] + flat],
        out_specs=[ANYWHERE] * 2,
        out_shape=[jax.ShapeDtypeStruct((4, chips, rows, width), low)] * 2,
        scratch_shapes=[
            pltpu.VMEM((4, chips, 2, rows, width), low),
            pltpu.SemaphoreType.DMA((8,)),
        ],
    )(ids, x, *flat)


def input_kernel(calls, ids_ref, back_ref, *refs):
    sources = [refs[3 * n : 3 * n + 3] for n in range(calls)]
    refs = refs[3 * calls :]
    parts, others = refs[:4], refs[4:8]
    out_ref, whole, semaphores = refs[8:]
    width = back_ref.shape[1]

    @pl.when(pl.program_id(0) == 0)
    def _():
        copies = fetch(ids_ref, parts, others, whole, semaphores, slice(None))
        for copy in copies:
            copy.start()
        for copy in copies:
            copy.wait()

    total = back_ref[...]
    for n in range(3):
        grad = jnp.concatenate([source[n][...] for source in sources], axis=1)
        weight = whole[:, :, :, n * SHARD : (n + 1) * SHARD, :].reshape(width, width)
        total = total + nt(grad, weight)
    out_ref[...] = total


def input_grad(ids, back, sources, parts, others):
    length, width = back.shape

    def block(array):
        return pl.BlockSpec((BLOCK, array.shape[1]), lambda p: (p, 0))

    flat = [array for source in sources for array in source]
    chips, rows, _ = parts[0].shape
    return call(
        functools.partial(input_kernel, len(sources)),
        "input",
        6,
        16,
        grid=(length // BLOCK,),
        in_specs=[SCALARS, block(back)] + [block(array) for array in flat] + [ANYWHERE] * 8,
        out_specs=block(back),
        out_shape=jax.ShapeDtypeStruct(back.shape, wide),
        scratch_shapes=[
            pltpu.VMEM((4, chips, 2, rows, width), low),
            pltpu.SemaphoreType.DMA((8,)),
        ],
    )(ids, back, *flat, *parts, *others)


def radices(extent):
    found = []
    while extent > 1:
        found.append(4 if extent % 4 == 0 else 2)
        extent //= found[-1]
    return found


class Links:
    def __init__(self, mesh):
        self.fsdp = mesh.shape["fsdp"]
        self.count = mesh.shape["dp"] * self.fsdp
        depth = self.fsdp // 2
        self.near = self.digits(1, depth)
        self.far = self.digits(depth.bit_length(), mesh.shape["dp"])

    def digits(self, shift, extent):
        found = []
        for radix in radices(extent):
            found.append((shift, radix))
            shift += radix.bit_length() - 1
        return found

    def flat(self):
        return lax.axis_index("dp") * self.fsdp + lax.axis_index("fsdp")

    def swap(self, values, distance):
        return lax.ppermute(values, AXES, [(i, i ^ distance) for i in range(self.count)])

    def digit(self, shift, radix):
        return (self.flat() >> shift) & (radix - 1)

    def receive(self, parts, shift):
        return [self.swap(part, (k + 1) << shift) for k, part in enumerate(parts)]

    def send(self, block, shift, radix):
        return [self.swap(block, k << shift) for k in range(1, radix)]

    def place(self, block, received, shift, radix):
        digit = self.digit(shift, radix)
        whole = jnp.zeros((radix,) + block.shape, block.dtype)
        for k, part in enumerate([block] + received):
            whole = lax.dynamic_update_index_in_dim(whole, part, digit ^ k, 0)
        return whole.reshape((-1,) + block.shape[1:])

    def spread(self, block, digits):
        for shift, radix in digits:
            block = self.place(block, self.send(block, shift, radix), shift, radix)
        return block

    def pair(self, block):
        other = self.swap(block, 1)
        even = (self.flat() & 1) == 0
        both = jnp.stack([jnp.where(even, block, other), jnp.where(even, other, block)], axis=1)
        return both.reshape((self.count,) + block.shape[1:])

    def halve(self, blocks):
        core = self.flat() & 1
        pairs = blocks.reshape((self.count // 2, 2) + blocks.shape[1:])
        away = lax.dynamic_index_in_dim(pairs, 1 - core, 1, keepdims=False)
        return away.astype(low), lax.dynamic_index_in_dim(pairs, core, 1, keepdims=False)

    def cut(self, total, shift, radix):
        digit = self.digit(shift, radix)
        parts = total.reshape((radix, -1) + total.shape[1:])
        kept, *away = [
            lax.dynamic_index_in_dim(parts, digit ^ k, 0, keepdims=False) for k in range(radix)
        ]
        return kept, [part.astype(low) for part in away]

    def collect(self, total, digits):
        for shift, radix in reversed(digits):
            kept, away = self.cut(total, shift, radix)
            for k, part in enumerate(away):
                kept = kept + self.swap(part, (k + 1) << shift).astype(wide)
            total = kept
        return total


def mask(lengths, length):
    bounds = jnp.cumsum(lengths)
    position = jnp.arange(length, dtype=jnp.int32)
    passed = position[:, None] >= bounds[None, :]
    begin = jnp.sum(jnp.where(passed, lengths[None, :], 0), axis=1)
    key = position[:, None]
    return jnp.where((key >= begin[None, :]) & (key <= position[None, :]), 0.0, neg_large)


def resplit(pieces):
    whole = jnp.concatenate(pieces, axis=1)
    whole = whole.reshape((4, whole.shape[0] // 8, 2) + whole.shape[1:])
    return [whole[k, :, 0] for k in range(4)], [whole[k, :, 1] for k in range(4)]


def body(
    links,
    stream_x,
    stream_y,
    cotangent,
    doc_lengths,
    query_weight,
    query_bias,
    key_weight,
    value_weight,
    value_bias,
    output_weight,
    output_bias,
    first_gain,
    first_shift,
    up_weight,
    up_bias,
    down_weight,
    down_bias,
    second_gain,
    second_shift,
    final_gain,
    final_shift,
):
    length, width = stream_x.shape
    size = width // HEADS
    count = links.count
    rows = query_weight.shape[0]
    inner = count * down_weight.shape[0]
    share = inner // count
    columns = inner // width
    direct = rows == SHARD and len(links.far) == 1
    tail = inner // (width // SHARD)

    vectors = [
        query_bias,
        value_bias,
        output_bias,
        first_gain,
        first_shift,
        down_bias,
        second_gain,
        second_shift,
        final_gain,
        final_shift,
    ]

    def pack_lines(lines, last):
        places = [(n % VECTORS, n // VECTORS * LANES, line) for n, line in enumerate(lines)]
        return sum(
            jnp.pad(
                line[..., None, :],
                [(0, 0)] * (line.ndim - 1)
                + [(row, VECTORS - 1 - row), (lane, width - lane - line.shape[-1])],
            )
            for row, lane, line in places + [(0, 2 * LANES, last)]
        )

    early = jnp.concatenate(
        [query_weight, key_weight, value_weight, pack_lines(vectors, up_bias)], axis=0
    )[None]
    late = jnp.concatenate(
        [down_weight]
        + [up_weight[:, c * width : (c + 1) * width] for c in range(columns)]
        + [output_weight],
        axis=0,
    )[None]
    early = links.spread(early, links.near)
    early, late = lax.optimization_barrier((early, late))
    early = links.spread(early, links.far[:-1])
    late = links.spread(late, links.near[:-1])
    arriving = links.send(early, *links.far[-1]), links.send(late, *links.near[-1])
    hide = mask(doc_lengths[0], length)
    arriving, hide = lax.optimization_barrier((arriving, hide))
    late = links.place(late, arriving[1], *links.near[-1])
    late = links.spread(late, links.far[:-1])
    if direct:
        ids = jnp.stack([links.digit(*links.far[-1]), links.flat() & 1])
        early_parts = [early] + arriving[0]
        early_others = [links.swap(part, 1) for part in early_parts]
    else:
        ids = jnp.zeros((2,), jnp.int32)
        early = links.pair(links.place(early, arriving[0], *links.far[-1]))
        squares = [
            early[:, n * rows : (n + 1) * rows].reshape(-1, SHARD, width) for n in range(3)
        ]
        small = early[:, 3 * rows :]
        lines = [
            small[:, n % VECTORS, n // VECTORS * LANES :][:, :rows].reshape(-1, SHARD)
            for n in range(len(vectors))
        ]
        last = small[:, 0, 2 * LANES :][:, :share].reshape(-1, tail)
        early_parts, early_others = resplit(squares + [pack_lines(lines, last)])
    received = links.send(late, *links.far[-1])
    queries, keys, values, context, table = attend(
        ids, stream_x, early_parts, early_others, hide, size, tail
    )
    received, context = lax.optimization_barrier((received, context))
    if direct:
        late_parts = [late] + received
        late_others = [links.swap(part, 1) for part in late_parts]
    else:
        late = links.pair(links.place(late, received, *links.far[-1]))
        up = late[:, share : 2 * share].reshape(count, columns, rows, width).swapaxes(0, 1)
        up = up.reshape(columns, -1, SHARD, width).swapaxes(0, 1)
        late_parts, late_others = resplit(
            [
                late[:, :share].reshape(-1, tail, width),
                up.reshape(-1, tail, width),
                late[:, 2 * share :].reshape(-1, SHARD, width),
            ]
        )
    block_out, grad_y, back, context_grad, kept, away = middle(
        ids, stream_x, stream_y, cotangent, context, table, late_parts, late_others, inner
    )

    def restore(kept, away):
        both = jnp.stack([kept, away], axis=2)
        return both.reshape((-1,) + both.shape[3:]).astype(wide)

    def real_lines(packed, lines, last):
        found = [packed[:, n, :SHARD].reshape(count, rows) for n in range(lines)]
        return pack_lines(found, packed[:, VECTORS - 1, :tail].reshape(count, share))

    def first_sums(kept, arriving):
        return [kept[k].astype(wide) + arriving[k].astype(wide) for k in range(kept.shape[0])]

    if not direct:
        full = restore(kept, away)
        up = full[:, tail : 2 * tail].reshape(-1, columns, SHARD, width).swapaxes(0, 1)
        up = up.reshape(columns, count, rows, width).swapaxes(0, 1)
        full = jnp.concatenate(
            [
                full[:, :tail].reshape(count, share, width),
                up.reshape(count, share, width),
                full[:, 2 * tail : 2 * tail + SHARD].reshape(count, rows, width),
                real_lines(full[:, 2 * tail + SHARD :], VECTORS - 1, True),
            ],
            axis=1,
        )
        away, kept = links.halve(full)
    arriving = links.swap(away, 1)
    part_a = attend_back(queries, keys, values, context_grad, hide, size, 0, 1)
    arriving, part_a = lax.optimization_barrier((arriving, part_a))
    if direct:
        total, *leaving = first_sums(kept, arriving)
        leaving = [part.astype(low) for part in leaving]
    else:
        total = links.collect(kept.astype(wide) + arriving.astype(wide), links.far[1:])
        total, leaving = links.cut(total, *links.far[0])
    leaving, context_grad = lax.optimization_barrier((leaving, context_grad))
    arriving = links.receive(leaving, links.far[0][0])
    part_b = attend_back(
        queries, keys, values, context_grad, hide, size, 1, width // LANES - 1
    )
    kept, away = weight_grads(ids, stream_x, [part_a, part_b])
    if not direct:
        full = restore(kept, away)
        full = jnp.concatenate(
            [
                full[:, n * SHARD : (n + 1) * SHARD].reshape(count, rows, width)
                for n in range(3)
            ]
            + [real_lines(full[:, 3 * SHARD :], 2, False)],
            axis=1,
        )
        away, kept = links.halve(full)
    crossing = links.swap(away, 1)
    back, away = lax.optimization_barrier((back, away))
    grad_x = input_grad(ids, back, [part_a, part_b], early_parts, early_others)
    for part in arriving:
        total = total + part.astype(wide)
    if direct:
        mine, *leaving = first_sums(kept, crossing)
        for part in links.receive([part.astype(low) for part in leaving], links.far[0][0]):
            mine = mine + part.astype(wide)
    else:
        mine = links.collect(kept.astype(wide) + crossing.astype(wide), links.far)
    total = links.collect(total, links.near)[0]
    mine = links.collect(mine, links.near)[0]

    if direct:
        at = 2 * share + rows
        singles = [total[at + n, :rows] for n in range(VECTORS - 1)]
        up_bias_share = total[at + VECTORS - 1, :share]
        pair = mine[3 * rows, :rows], mine[3 * rows + 1, :rows]
    else:
        at = 2 * share + rows
        singles = [total[at + n, :rows] for n in range(VECTORS - 1)]
        up_bias_share = total[at, 2 * LANES : 2 * LANES + share]
        pair = mine[3 * rows, :rows], mine[3 * rows + 1, :rows]
    up_share = jnp.concatenate(
        [total[share + c * rows : share + (c + 1) * rows] for c in range(columns)], axis=1
    )
    return (
        block_out,
        grad_x,
        grad_y,
        mine[:rows],
        pair[0],
        mine[rows : 2 * rows],
        mine[2 * rows : 3 * rows],
        pair[1],
        total[2 * share : at],
        singles[0],
        singles[1],
        singles[2],
        up_share,
        up_bias_share,
        total[:share],
        singles[3],
        singles[4],
        singles[5],
        singles[6],
        singles[5],
    )


def solution(mesh):
    matrix, vector = P(AXES, None), P(AXES)
    matrices = {0, 1, 2, 3, 4, 6, 7, 9, 13, 15}
    out_matrices = {0, 1, 2, 3, 5, 6, 8, 12, 14}
    return jax.shard_map(
        functools.partial(body, Links(mesh)),
        mesh=mesh,
        in_specs=tuple(matrix if n in matrices else vector for n in range(21)),
        out_specs=tuple(matrix if n in out_matrices else vector for n in range(20)),
        check_vma=False,
    )
```

profile of v0, /device:TPU:0, one launch (start us, length us, event | category | flops | bytes accessed | tf_op | source)
XLA Modules:
  0.0 178.3 jit_solution(14775136631912565736)
XLA Ops:
  2.2 4.0 %collective-permute-start.1 = (bf16[1,56,512]{2,1,0:T(8,128)(2,1)S(1)}, bf16[1,56,512]{2,1,0:T(8,128)(2,1)S(1)}, u32[]{:S(2)}, u32[]{:S(2)}) collective-permute-start(bf16[1,56,512]{2,1,0:T(8,128)(2,1)S(1)} %maximum_bitcast_fusion), channel_id=1, source_target_pairs={{0,4},{1,5},{2,6},{3,7},{4,0},{5,1},{6,2},{7,3},{8,12},{9,13},{10,... | collective-permute-start | bytes 172040 | tf_op jit(solution)/shard_map/ppermute | solution.py:588
  6.3 1.6 collective-permute-start
  13.8 3.2 %collective-permute-start.8 = (bf16[1,144,512]{2,1,0:T(8,128)(2,1)S(1)}, bf16[1,144,512]{2,1,0:T(8,128)(2,1)S(1)}, u32[]{:S(2)}, u32[]{:S(2)}) collective-permute-start(bf16[1,144,512]{2,1,0:T(8,128)(2,1)S(1)} %bitcast.87), channel_id=1, source_target_pairs={{0,6},{1,7},{2,4},{3,5},{4,2},{5,3},{6,0},{7,1},{8,14},{9,15},{10,... | collective-permute-start | bytes 442376 | tf_op jit(solution)/shard_map/ppermute | solution.py:588
  18.7 1.2 collective-permute-start.6
  20.0 2.4 %collective-permute-start.5 = (bf16[4,56,512]{2,1,0:T(8,128)(2,1)S(1)}, bf16[4,56,512]{2,1,0:T(8,128)(2,1)S(1)}, u32[]{:S(2)}, u32[]{:S(2)}) collective-permute-start(bf16[4,56,512]{2,1,0:T(8,128)(2,1)S(1)} %constant_dynamic-update-slice_fusion.6.refs_0_.refs_6_), channel_id=1, source_target_pairs={{0,24},{1,25},{2,26},{3,27},{4,28},{5,29},{6,30},{7,31},{8,16},{9,... | collective-permute-start | bytes 688136 | tf_op jit(solution)/shard_map/ppermute | solution.py:588
  23.9 2.6 %fusion.1.hide_ref = f32[1024,1024]{1,0:T(8,128)} fusion(s32[1024]{0:T(1024)S(1)} %select_reduce_fusion), kind=kLoop, calls=%fused_computation.3 | loop fusion | flops 4194304 | bytes 4198400 | tf_op jit(solution)/shard_map/jit(_where)/select_n | solution.py:646
  26.6 1.4 collective-permute-done.7
  28.7 2.4 %collective-permute-done.4.refs_2_.refs_8_ = bf16[4,56,512]{2,1,0:T(8,128)(2,1)S(1)} collective-permute-done((bf16[4,56,512]{2,1,0:T(8,128)(2,1)S(1)}, bf16[4,56,512]{2,1,0:T(8,128)(2,1)S(1)}, u32[]{:S(2)}, u32[]{:S(2)}) %collective-permute-start.4) | collective-permute-done | bytes 229408 | tf_op jit(solution)/shard_map/ppermute | solution.py:588
  31.8 1.7 collective-permute-start.11
  33.5 1.3 collective-permute-start.10
  35.5 2.2 %copy-done = f32[1024,1024]{1,0:T(8,128)S(1)} copy-done((f32[1024,1024]{1,0:T(8,128)S(1)}, f32[1024,1024]{1,0:T(8,128)}, u32[]{:S(2)}) %copy-start) | copy-done | bytes 4194328
  38.9 22.1 %attend.1 = (bf16[1024,512]{1,0:T(8,128)(2,1)S(1)}, bf16[1024,512]{1,0:T(8,128)(2,1)S(1)}, bf16[1024,512]{1,0:T(8,128)(2,1)S(1)}, bf16[1024,512]{1,0:T(8,128)(2,1)S(1)}, f32[24,512]{1,0:T(8,128)S(1)}) custom-call(s32[2]{0:T(128)S(1)} %pad_add_fusion.1.ids_ref, bf16[1024,512]{1,0:T(8,128)(2,1)S(1)} %copy-done.14, f32[1024,1024]{1,0:T(8,128)S(1)} %copy-done, ...), custom_call_target="tpu_custom_call" | custom-call | flops 5750000128 | bytes 1024 | tf_op jit(solution)/shard_map/attend/pallas_call | solution.py:225
  67.5 29.5 %middle.1 = (bf16[1024,512]{1,0:T(8,128)(2,1)}, f32[1024,512]{1,0:T(8,128)}, f32[1024,512]{1,0:T(8,128)}, bf16[1024,512]{1,0:T(8,128)(2,1)}, bf16[4,4,152,512]{3...) custom-call(s32[2]{0:T(128)} %copy-done.12, bf16[1024,512]{1,0:T(8,128)(2,1)} %x_ref.5, bf16[1024,512]{1,0:T(8,128)(2,1)} %y_ref.1, ...), custom_call_target="tpu_custom_call" | custom-call | flops 7249999872 | bytes 1024 | tf_op jit(solution)/shard_map/middle/pallas_call | solution.py:445
  97.4 1.2 copy-done.3
  98.7 5.6 %attend_back.2 = (bf16[1024,128]{1,0:T(8,128)(2,1)S(1)}, bf16[1024,128]{1,0:T(8,128)(2,1)S(1)}, bf16[1024,128]{1,0:T(8,128)(2,1)S(1)}) custom-call(bf16[1024,512]{1,0:T(8,128)(2,1)S(1)} %get-tuple-element.79.q_ref, bf16[1024,512]{1,0:T(8,128)(2,1)S(1)} %get-tuple-element.80.k_ref, bf16[1024,512]{1,0:T(8,128)(2,1)S(1)} %get-tuple-element.81.v_ref, ...), custom_call_target="tpu_custom_call" | custom-call | flops 1750000000 | bytes 1024 | tf_op jit(solution)/shard_map/attend_back/pallas_call | solution.py:284
  104.9 1.6 collective-permute-start.28
  107.1 1.3 collective-permute-start.30
  108.4 17.8 %attend_back.3 = (bf16[1024,384]{1,0:T(8,128)(2,1)S(1)}, bf16[1024,384]{1,0:T(8,128)(2,1)S(1)}, bf16[1024,384]{1,0:T(8,128)(2,1)S(1)}) custom-call(bf16[1024,512]{1,0:T(8,128)(2,1)S(1)} %get-tuple-element.79.q_ref, bf16[1024,512]{1,0:T(8,128)(2,1)S(1)} %get-tuple-element.80.k_ref, bf16[1024,512]{1,0:T(8,128)(2,1)S(1)} %get-tuple-element.81.v_ref, ...), custom_call_target="tpu_custom_call" | custom-call | flops 5249999872 | bytes 1024 | tf_op jit(solution)/shard_map/attend_back/pallas_call | solution.py:284
  126.3 9.2 %collective-permute-done.29 = bf16[4,152,512]{2,1,0:T(8,128)(2,1)S(1)} collective-permute-done((bf16[4,152,512]{2,1,0:T(8,128)(2,1)S(1)}, bf16[4,152,512]{2,1,0:T(8,128)(2,1)S(1)}, u32[]{:S(2)}, u32[]{:S(2)}) %collective-permute-start.29) | collective-permute-done | bytes 622624 | tf_op jit(solution)/shard_map/ppermute | solution.py:588
  136.0 1.6 collective-permute-start.31
  137.6 2.3 %collective-permute-start.33 = (bf16[1,152,512]{2,1,0:T(8,128)(2,1)S(1)}, bf16[1,152,512]{2,1,0:T(8,128)(2,1)S(1)}, u32[]{:S(2)}, u32[]{:S(2)}) collective-permute-start(bf16[1,152,512]{2,1,0:T(8,128)(2,1)S(1)} %get-tuple-element.109), channel_id=1, source_target_pairs={{0,6},{1,7},{2,4},{3,5},{4,2},{5,3},{6,0},{7,1},{8,14},{9,15},{10,... | collective-permute-start | bytes 466952 | tf_op jit(solution)/shard_map/ppermute | solution.py:588
  140.2 3.1 %weights.1 = (bf16[4,4,56,512]{3,2,1,0:T(8,128)(2,1)S(1)}, bf16[4,4,56,512]{3,2,1,0:T(8,128)(2,1)S(1)}) custom-call(s32[2]{0:T(128)S(1)} %copy-done.13, bf16[1024,512]{1,0:T(8,128)(2,1)S(1)} %copy-done.15, bf16[1024,128]{1,0:T(8,128)(2,1)S(1)} %get-tuple-element.86.refs_0_, bf16[1024,128]{1,0:T(8,128)(2,1)S(1)} %get-tuple-element.87.refs_1_, ...), custom_call_target="tpu_custom_call" | custom-call | flops 1250000000 | bytes 1024 | tf_op jit(solution)/shard_map/weights/pallas_call | solution.py:498
  143.5 4.8 %input.1 = f32[1024,512]{1,0:T(8,128)} custom-call(s32[2]{0:T(128)S(1)} %copy-done.13, f32[1024,512]{1,0:T(8,128)S(1)} %copy-done.2, bf16[1024,128]{1,0:T(8,128)(2,1)S(1)} %get-tuple-element.86.refs_0_, bf16[1024,128]{1,0:T(8,128)(2,1)S(1)} %get-tuple-element.87.refs_1_, bf16[1024,128]{1,0:T(8,128)(2,1)S(1)} %get-tuple-element.88.refs_2_, ...), custom_call_target="tpu_custom_call" | custom-call | flops 1500000000 | bytes 1024 | tf_op jit(solution)/shard_map/input/pallas_call | solution.py:545
  148.3 4.8 %collective-permute-done.32 = bf16[1,152,512]{2,1,0:T(8,128)(2,1)S(1)} collective-permute-done((bf16[1,152,512]{2,1,0:T(8,128)(2,1)S(1)}, bf16[1,152,512]{2,1,0:T(8,128)(2,1)S(1)}, u32[]{:S(2)}, u32[]{:S(2)}) %collective-permute-start.32) | collective-permute-done | bytes 155680 | tf_op jit(solution)/shard_map/ppermute | solution.py:588
  156.1 1.3 collective-permute-start.24
  157.4 1.4 collective-permute-start.23
  159.5 4.4 %collective-permute-done.22 = bf16[4,56,512]{2,1,0:T(8,128)(2,1)S(1)} collective-permute-done((bf16[4,56,512]{2,1,0:T(8,128)(2,1)S(1)}, bf16[4,56,512]{2,1,0:T(8,128)(2,1)S(1)}, u32[]{:S(2)}, u32[]{:S(2)}) %collective-permute-start.22) | collective-permute-done | bytes 229408 | tf_op jit(solution)/shard_map/ppermute | solution.py:588
  163.8 2.6 %collective-permute-done.24 = bf16[4,56,512]{2,1,0:T(8,128)(2,1)S(1)} collective-permute-done((bf16[4,56,512]{2,1,0:T(8,128)(2,1)S(1)}, bf16[4,56,512]{2,1,0:T(8,128)(2,1)S(1)}, u32[]{:S(2)}, u32[]{:S(2)}) %collective-permute-start.24) | collective-permute-done | bytes 229408 | tf_op jit(solution)/shard_map/ppermute | solution.py:588
  166.4 1.4 collective-permute-done.23
  168.0 2.8 %collective-permute-start.27 = (bf16[1,56,512]{2,1,0:T(8,128)(2,1)S(1)}, bf16[1,56,512]{2,1,0:T(8,128)(2,1)S(1)}, u32[]{:S(2)}, u32[]{:S(2)}) collective-permute-start(bf16[1,56,512]{2,1,0:T(8,128)(2,1)S(1)} %get-tuple-element.112), channel_id=1, source_target_pairs={{0,6},{1,7},{2,4},{3,5},{4,2},{5,3},{6,0},{7,1},{8,14},{9,15},{10,... | collective-permute-start | bytes 172040 | tf_op jit(solution)/shard_map/ppermute | solution.py:588
  172.2 2.0 %collective-permute-done.27 = bf16[1,56,512]{2,1,0:T(8,128)(2,1)S(1)} collective-permute-done((bf16[1,56,512]{2,1,0:T(8,128)(2,1)S(1)}, bf16[1,56,512]{2,1,0:T(8,128)(2,1)S(1)}, u32[]{:S(2)}, u32[]{:S(2)}) %collective-permute-start.27) | collective-permute-done | bytes 57376 | tf_op jit(solution)/shard_map/ppermute | solution.py:588
  174.2 2.4 %collective-permute-done.26 = bf16[1,56,512]{2,1,0:T(8,128)(2,1)S(1)} collective-permute-done((bf16[1,56,512]{2,1,0:T(8,128)(2,1)S(1)}, bf16[1,56,512]{2,1,0:T(8,128)(2,1)S(1)}, u32[]{:S(2)}, u32[]{:S(2)}) %collective-permute-start.26) | collective-permute-done | bytes 57376 | tf_op jit(solution)/shard_map/ppermute | solution.py:588
  (138 shorter events, 29.9 us)
Async XLA Ops:
  2.2 10.9 %collective-permute-start.1 = (bf16[1,56,512]{2,1,0:T(8,128)(2,1)S(1)}, bf16[1,56,512]{2,1,0:T(8,128)(2,1)S(1)}, u32[]{:S(2)}, u32[]{:S(2)}) collective-permute-start(bf16[1,56,512]{2,1,0:T(8,128)(2,1)S(1)} %maximum_bitcast_fusion), channel_id=1, source_target_pairs={{0,4},{1,5},{2,6},{3,7},{4,0},{5,1},{6,2},{7,3},{8,12},{9,13},{10,... | collective-permute-start | bytes 172040 | tf_op jit(solution)/shard_map/ppermute | solution.py:588
  6.3 6.8 %collective-permute-start = (bf16[1,56,512]{2,1,0:T(8,128)(2,1)S(1)}, bf16[1,56,512]{2,1,0:T(8,128)(2,1)S(1)}, u32[]{:S(2)}, u32[]{:S(2)}) collective-permute-start(bf16[1,56,512]{2,1,0:T(8,128)(2,1)S(1)} %maximum_bitcast_fusion), channel_id=1, source_target_pairs={{0,2},{1,3},{2,0},{3,1},{4,6},{5,7},{6,4},{7,5},{8,10},{9,11},{10,... | collective-permute-start | bytes 172040 | tf_op jit(solution)/shard_map/ppermute | solution.py:588
  7.8 6.0 %collective-permute-start.2 = (bf16[1,56,512]{2,1,0:T(8,128)(2,1)S(1)}, bf16[1,56,512]{2,1,0:T(8,128)(2,1)S(1)}, u32[]{:S(2)}, u32[]{:S(2)}) collective-permute-start(bf16[1,56,512]{2,1,0:T(8,128)(2,1)S(1)} %maximum_bitcast_fusion), channel_id=1, source_target_pairs={{0,6},{1,7},{2,4},{3,5},{4,2},{5,3},{6,0},{7,1},{8,14},{9,15},{10,... | collective-permute-start | bytes 172040 | tf_op jit(solution)/shard_map/ppermute | solution.py:588
  13.8 9.1 %collective-permute-start.8 = (bf16[1,144,512]{2,1,0:T(8,128)(2,1)S(1)}, bf16[1,144,512]{2,1,0:T(8,128)(2,1)S(1)}, u32[]{:S(2)}, u32[]{:S(2)}) collective-permute-start(bf16[1,144,512]{2,1,0:T(8,128)(2,1)S(1)} %bitcast.87), channel_id=1, source_target_pairs={{0,6},{1,7},{2,4},{3,5},{4,2},{5,3},{6,0},{7,1},{8,14},{9,15},{10,... | collective-permute-start | bytes 442376 | tf_op jit(solution)/shard_map/ppermute | solution.py:588
  18.7 9.3 %collective-permute-start.7 = (bf16[1,144,512]{2,1,0:T(8,128)(2,1)S(1)}, bf16[1,144,512]{2,1,0:T(8,128)(2,1)S(1)}, u32[]{:S(2)}, u32[]{:S(2)}) collective-permute-start(bf16[1,144,512]{2,1,0:T(8,128)(2,1)S(1)} %bitcast.88), channel_id=1, source_target_pairs={{0,4},{1,5},{2,6},{3,7},{4,0},{5,1},{6,2},{7,3},{8,12},{9,13},{10,... | collective-permute-start | bytes 442376 | tf_op jit(solution)/shard_map/ppermute | solution.py:588
  18.7 9.2 %collective-permute-start.6 = (bf16[1,144,512]{2,1,0:T(8,128)(2,1)S(1)}, bf16[1,144,512]{2,1,0:T(8,128)(2,1)S(1)}, u32[]{:S(2)}, u32[]{:S(2)}) collective-permute-start(bf16[1,144,512]{2,1,0:T(8,128)(2,1)S(1)} %bitcast.89), channel_id=1, source_target_pairs={{0,2},{1,3},{2,0},{3,1},{4,6},{5,7},{6,4},{7,5},{8,10},{9,11},{10,... | collective-permute-start | bytes 442376 | tf_op jit(solution)/shard_map/ppermute | solution.py:588
  20.0 8.7 %collective-permute-start.5 = (bf16[4,56,512]{2,1,0:T(8,128)(2,1)S(1)}, bf16[4,56,512]{2,1,0:T(8,128)(2,1)S(1)}, u32[]{:S(2)}, u32[]{:S(2)}) collective-permute-start(bf16[4,56,512]{2,1,0:T(8,128)(2,1)S(1)} %constant_dynamic-update-slice_fusion.6.refs_0_.refs_6_), channel_id=1, source_target_pairs={{0,24},{1,25},{2,26},{3,27},{4,28},{5,29},{6,30},{7,31},{8,16},{9,... | collective-permute-start | bytes 688136 | tf_op jit(solution)/shard_map/ppermute | solution.py:588
  22.4 8.6 %collective-permute-start.4 = (bf16[4,56,512]{2,1,0:T(8,128)(2,1)S(1)}, bf16[4,56,512]{2,1,0:T(8,128)(2,1)S(1)}, u32[]{:S(2)}, u32[]{:S(2)}) collective-permute-start(bf16[4,56,512]{2,1,0:T(8,128)(2,1)S(1)} %constant_dynamic-update-slice_fusion.6.refs_0_.refs_6_), channel_id=1, source_target_pairs={{0,16},{1,17},{2,18},{3,19},{4,20},{5,21},{6,22},{7,23},{8,24},{9,... | collective-permute-start | bytes 688136 | tf_op jit(solution)/shard_map/ppermute | solution.py:588
  22.9 8.2 %collective-permute-start.3 = (bf16[4,56,512]{2,1,0:T(8,128)(2,1)S(1)}, bf16[4,56,512]{2,1,0:T(8,128)(2,1)S(1)}, u32[]{:S(2)}, u32[]{:S(2)}) collective-permute-start(bf16[4,56,512]{2,1,0:T(8,128)(2,1)S(1)} %constant_dynamic-update-slice_fusion.6.refs_0_.refs_6_), channel_id=1, source_target_pairs={{0,8},{1,9},{2,10},{3,11},{4,12},{5,13},{6,14},{7,15},{8,0},{9,1},... | collective-permute-start | bytes 688136 | tf_op jit(solution)/shard_map/ppermute | solution.py:588
  27.9 5.5 %collective-permute-start.12 = (bf16[4,56,512]{2,1,0:T(8,128)(2,1)S(1)}, bf16[4,56,512]{2,1,0:T(8,128)(2,1)S(1)}, u32[]{:S(2)}, u32[]{:S(2)}) collective-permute-start(bf16[4,56,512]{2,1,0:T(8,128)(2,1)S(1)} %constant_dynamic-update-slice_fusion.6.refs_0_.refs_6_), channel_id=1, source_target_pairs={{0,1},{1,0},{2,3},{3,2},{4,5},{5,4},{6,7},{7,6},{8,9},{9,8},{10,11... | collective-permute-start | bytes 688136 | tf_op jit(solution)/shard_map/ppermute | solution.py:588
  31.2 3.6 %collective-permute-start.13 = (bf16[4,56,512]{2,1,0:T(8,128)(2,1)S(1)}, bf16[4,56,512]{2,1,0:T(8,128)(2,1)S(1)}, u32[]{:S(2)}, u32[]{:S(2)}) collective-permute-start(bf16[4,56,512]{2,1,0:T(8,128)(2,1)S(1)} %collective-permute-done.3.refs_1_.refs_7_), channel_id=1, source_target_pairs={{0,1},{1,0},{2,3},{3,2},{4,5},{5,4},{6,7},{7,6},{8,9},{9,8},{10,11... | collective-permute-start | bytes 688136 | tf_op jit(solution)/shard_map/ppermute | solution.py:588
  31.2 4.2 %collective-permute-start.14 = (bf16[4,56,512]{2,1,0:T(8,128)(2,1)S(1)}, bf16[4,56,512]{2,1,0:T(8,128)(2,1)S(1)}, u32[]{:S(2)}, u32[]{:S(2)}) collective-permute-start(bf16[4,56,512]{2,1,0:T(8,128)(2,1)S(1)} %collective-permute-done.4.refs_2_.refs_8_), channel_id=1, source_target_pairs={{0,1},{1,0},{2,3},{3,2},{4,5},{5,4},{6,7},{7,6},{8,9},{9,8},{10,11... | collective-permute-start | bytes 688136 | tf_op jit(solution)/shard_map/ppermute | solution.py:588
  31.7 3.8 %collective-permute-start.15 = (bf16[4,56,512]{2,1,0:T(8,128)(2,1)S(1)}, bf16[4,56,512]{2,1,0:T(8,128)(2,1)S(1)}, u32[]{:S(2)}, u32[]{:S(2)}) collective-permute-start(bf16[4,56,512]{2,1,0:T(8,128)(2,1)S(1)} %collective-permute-done.5.refs_3_.refs_9_), channel_id=1, source_target_pairs={{0,1},{1,0},{2,3},{3,2},{4,5},{5,4},{6,7},{7,6},{8,9},{9,8},{10,11... | collective-permute-start | bytes 688136 | tf_op jit(solution)/shard_map/ppermute | solution.py:588
  31.8 31.0 %collective-permute-start.11 = (bf16[4,144,512]{2,1,0:T(8,128)(2,1)S(1)}, bf16[4,144,512]{2,1,0:T(8,128)(2,1)S(1)}, u32[]{:S(2)}, u32[]{:S(2)}) collective-permute-start(bf16[4,144,512]{2,1,0:T(8,128)(2,1)S(1)} %constant_dynamic-update-slice_fusion.2.refs_0_), channel_id=1, source_target_pairs={{0,24},{1,25},{2,26},{3,27},{4,28},{5,29},{6,30},{7,31},{8,16},{9,... | collective-permute-start | bytes 1769480 | tf_op jit(solution)/shard_map/ppermute | solution.py:588
  33.5 29.2 %collective-permute-start.10 = (bf16[4,144,512]{2,1,0:T(8,128)(2,1)S(1)}, bf16[4,144,512]{2,1,0:T(8,128)(2,1)S(1)}, u32[]{:S(2)}, u32[]{:S(2)}) collective-permute-start(bf16[4,144,512]{2,1,0:T(8,128)(2,1)S(1)} %constant_dynamic-update-slice_fusion.2.refs_0_), channel_id=1, source_target_pairs={{0,16},{1,17},{2,18},{3,19},{4,20},{5,21},{6,22},{7,23},{8,24},{9,... | collective-permute-start | bytes 1769480 | tf_op jit(solution)/shard_map/ppermute | solution.py:588
  34.8 27.9 %collective-permute-start.9 = (bf16[4,144,512]{2,1,0:T(8,128)(2,1)S(1)}, bf16[4,144,512]{2,1,0:T(8,128)(2,1)S(1)}, u32[]{:S(2)}, u32[]{:S(2)}) collective-permute-start(bf16[4,144,512]{2,1,0:T(8,128)(2,1)S(1)} %constant_dynamic-update-slice_fusion.2.refs_0_), channel_id=1, source_target_pairs={{0,8},{1,9},{2,10},{3,11},{4,12},{5,13},{6,14},{7,15},{8,0},{9,1},... | collective-permute-start | bytes 1769480 | tf_op jit(solution)/shard_map/ppermute | solution.py:588
  35.4 28.4 %collective-permute-start.16 = (bf16[4,144,512]{2,1,0:T(8,128)(2,1)S(1)}, bf16[4,144,512]{2,1,0:T(8,128)(2,1)S(1)}, u32[]{:S(2)}, u32[]{:S(2)}) collective-permute-start(bf16[4,144,512]{2,1,0:T(8,128)(2,1)S(1)} %constant_dynamic-update-slice_fusion.2.refs_0_), channel_id=1, source_target_pairs={{0,1},{1,0},{2,3},{3,2},{4,5},{5,4},{6,7},{7,6},{8,9},{9,8},{10,11... | collective-permute-start | bytes 1769480 | tf_op jit(solution)/shard_map/ppermute | solution.py:588
  63.4 3.2 %collective-permute-start.19 = (bf16[4,144,512]{2,1,0:T(8,128)(2,1)S(1)}, bf16[4,144,512]{2,1,0:T(8,128)(2,1)S(1)}, u32[]{:S(2)}, u32[]{:S(2)}) collective-permute-start(bf16[4,144,512]{2,1,0:T(8,128)(2,1)S(1)} %collective-permute-done.11.refs_3_), channel_id=1, source_target_pairs={{0,1},{1,0},{2,3},{3,2},{4,5},{5,4},{6,7},{7,6},{8,9},{9,8},{10,11... | collective-permute-start | bytes 1769480 | tf_op jit(solution)/shard_map/ppermute | solution.py:588
  97.0 7.2 %collective-permute-start.20 = (bf16[4,4,152,512]{3,2,1,0:T(8,128)(2,1)}, bf16[4,4,152,512]{3,2,1,0:T(8,128)(2,1)S(1)}, u32[]{:S(2)}, u32[]{:S(2)}) collective-permute-start(bf16[4,4,152,512]{3,2,1,0:T(8,128)(2,1)} %get-tuple-element.78), channel_id=1, source_target_pairs={{0,1},{1,0},{2,3},{3,2},{4,5},{5,4},{6,7},{7,6},{8,9},{9,8},{10,11... | collective-permute-start | bytes 7471112 | tf_op jit(solution)/shard_map/ppermute | solution.py:588
  104.9 21.4 %collective-permute-start.28 = (bf16[4,152,512]{2,1,0:T(8,128)(2,1)S(1)}, bf16[4,152,512]{2,1,0:T(8,128)(2,1)S(1)}, u32[]{:S(2)}, u32[]{:S(2)}) collective-permute-start(bf16[4,152,512]{2,1,0:T(8,128)(2,1)S(1)} %get-tuple-element.99), channel_id=1, source_target_pairs={{0,8},{1,9},{2,10},{3,11},{4,12},{5,13},{6,14},{7,15},{8,0},{9,1},... | collective-permute-start | bytes 1867784 | tf_op jit(solution)/shard_map/ppermute | solution.py:588
  106.4 29.1 %collective-permute-start.29 = (bf16[4,152,512]{2,1,0:T(8,128)(2,1)S(1)}, bf16[4,152,512]{2,1,0:T(8,128)(2,1)S(1)}, u32[]{:S(2)}, u32[]{:S(2)}) collective-permute-start(bf16[4,152,512]{2,1,0:T(8,128)(2,1)S(1)} %get-tuple-element.100), channel_id=1, source_target_pairs={{0,16},{1,17},{2,18},{3,19},{4,20},{5,21},{6,22},{7,23},{8,24},{9,... | collective-permute-start | bytes 1867784 | tf_op jit(solution)/shard_map/ppermute | solution.py:588
  107.1 28.4 %collective-permute-start.30 = (bf16[4,152,512]{2,1,0:T(8,128)(2,1)S(1)}, bf16[4,152,512]{2,1,0:T(8,128)(2,1)S(1)}, u32[]{:S(2)}, u32[]{:S(2)}) collective-permute-start(bf16[4,152,512]{2,1,0:T(8,128)(2,1)S(1)} %get-tuple-element.101), channel_id=1, source_target_pairs={{0,24},{1,25},{2,26},{3,27},{4,28},{5,29},{6,30},{7,31},{8,16},{9,... | collective-permute-start | bytes 1867784 | tf_op jit(solution)/shard_map/ppermute | solution.py:588
  136.0 12.2 %collective-permute-start.31 = (bf16[1,152,512]{2,1,0:T(8,128)(2,1)S(1)}, bf16[1,152,512]{2,1,0:T(8,128)(2,1)S(1)}, u32[]{:S(2)}, u32[]{:S(2)}) collective-permute-start(bf16[1,152,512]{2,1,0:T(8,128)(2,1)S(1)} %get-tuple-element.108), channel_id=1, source_target_pairs={{0,2},{1,3},{2,0},{3,1},{4,6},{5,7},{6,4},{7,5},{8,10},{9,11},{10,... | collective-permute-start | bytes 466952 | tf_op jit(solution)/shard_map/ppermute | solution.py:588
  137.6 10.6 %collective-permute-start.33 = (bf16[1,152,512]{2,1,0:T(8,128)(2,1)S(1)}, bf16[1,152,512]{2,1,0:T(8,128)(2,1)S(1)}, u32[]{:S(2)}, u32[]{:S(2)}) collective-permute-start(bf16[1,152,512]{2,1,0:T(8,128)(2,1)S(1)} %get-tuple-element.109), channel_id=1, source_target_pairs={{0,6},{1,7},{2,4},{3,5},{4,2},{5,3},{6,0},{7,1},{8,14},{9,15},{10,... | collective-permute-start | bytes 466952 | tf_op jit(solution)/shard_map/ppermute | solution.py:588
  139.9 13.2 %collective-permute-start.32 = (bf16[1,152,512]{2,1,0:T(8,128)(2,1)S(1)}, bf16[1,152,512]{2,1,0:T(8,128)(2,1)S(1)}, u32[]{:S(2)}, u32[]{:S(2)}) collective-permute-start(bf16[1,152,512]{2,1,0:T(8,128)(2,1)S(1)} %get-tuple-element.110), channel_id=1, source_target_pairs={{0,4},{1,5},{2,6},{3,7},{4,0},{5,1},{6,2},{7,3},{8,12},{9,13},{10,... | collective-permute-start | bytes 466952 | tf_op jit(solution)/shard_map/ppermute | solution.py:588
  143.3 11.7 %collective-permute-start.21 = (bf16[4,4,56,512]{3,2,1,0:T(8,128)(2,1)S(1)}, bf16[4,4,56,512]{3,2,1,0:T(8,128)(2,1)S(1)}, u32[]{:S(2)}, u32[]{:S(2)}) collective-permute-start(bf16[4,4,56,512]{3,2,1,0:T(8,128)(2,1)S(1)} %get-tuple-element.95), channel_id=1, source_target_pairs={{0,1},{1,0},{2,3},{3,2},{4,5},{5,4},{6,7},{7,6},{8,9},{9,8},{10,11... | collective-permute-start | bytes 2752520 | tf_op jit(solution)/shard_map/ppermute | solution.py:588
  155.2 8.6 %collective-permute-start.22 = (bf16[4,56,512]{2,1,0:T(8,128)(2,1)S(1)}, bf16[4,56,512]{2,1,0:T(8,128)(2,1)S(1)}, u32[]{:S(2)}, u32[]{:S(2)}) collective-permute-start(bf16[4,56,512]{2,1,0:T(8,128)(2,1)S(1)} %get-tuple-element.105), channel_id=1, source_target_pairs={{0,8},{1,9},{2,10},{3,11},{4,12},{5,13},{6,14},{7,15},{8,0},{9,1},... | collective-permute-start | bytes 688136 | tf_op jit(solution)/shard_map/ppermute | solution.py:588
  156.1 10.3 %collective-permute-start.24 = (bf16[4,56,512]{2,1,0:T(8,128)(2,1)S(1)}, bf16[4,56,512]{2,1,0:T(8,128)(2,1)S(1)}, u32[]{:S(2)}, u32[]{:S(2)}) collective-permute-start(bf16[4,56,512]{2,1,0:T(8,128)(2,1)S(1)} %get-tuple-element.106), channel_id=1, source_target_pairs={{0,24},{1,25},{2,26},{3,27},{4,28},{5,29},{6,30},{7,31},{8,16},{9,... | collective-permute-start | bytes 688136 | tf_op jit(solution)/shard_map/ppermute | solution.py:588
  157.4 10.4 %collective-permute-start.23 = (bf16[4,56,512]{2,1,0:T(8,128)(2,1)S(1)}, bf16[4,56,512]{2,1,0:T(8,128)(2,1)S(1)}, u32[]{:S(2)}, u32[]{:S(2)}) collective-permute-start(bf16[4,56,512]{2,1,0:T(8,128)(2,1)S(1)} %get-tuple-element.107), channel_id=1, source_target_pairs={{0,16},{1,17},{2,18},{3,19},{4,20},{5,21},{6,22},{7,23},{8,24},{9,... | collective-permute-start | bytes 688136 | tf_op jit(solution)/shard_map/ppermute | solution.py:588
  168.0 4.3 %collective-permute-start.25 = (bf16[1,56,512]{2,1,0:T(8,128)(2,1)S(1)}, bf16[1,56,512]{2,1,0:T(8,128)(2,1)S(1)}, u32[]{:S(2)}, u32[]{:S(2)}) collective-permute-start(bf16[1,56,512]{2,1,0:T(8,128)(2,1)S(1)} %get-tuple-element.111), channel_id=1, source_target_pairs={{0,2},{1,3},{2,0},{3,1},{4,6},{5,7},{6,4},{7,5},{8,10},{9,11},{10,... | collective-permute-start | bytes 172040 | tf_op jit(solution)/shard_map/ppermute | solution.py:588
  168.0 6.1 %collective-permute-start.27 = (bf16[1,56,512]{2,1,0:T(8,128)(2,1)S(1)}, bf16[1,56,512]{2,1,0:T(8,128)(2,1)S(1)}, u32[]{:S(2)}, u32[]{:S(2)}) collective-permute-start(bf16[1,56,512]{2,1,0:T(8,128)(2,1)S(1)} %get-tuple-element.112), channel_id=1, source_target_pairs={{0,6},{1,7},{2,4},{3,5},{4,2},{5,3},{6,0},{7,1},{8,14},{9,15},{10,... | collective-permute-start | bytes 172040 | tf_op jit(solution)/shard_map/ppermute | solution.py:588
  170.9 5.7 %collective-permute-start.26 = (bf16[1,56,512]{2,1,0:T(8,128)(2,1)S(1)}, bf16[1,56,512]{2,1,0:T(8,128)(2,1)S(1)}, u32[]{:S(2)}, u32[]{:S(2)}) collective-permute-start(bf16[1,56,512]{2,1,0:T(8,128)(2,1)S(1)} %get-tuple-element.113), channel_id=1, source_target_pairs={{0,4},{1,5},{2,6},{3,7},{4,0},{5,1},{6,2},{7,3},{8,12},{9,13},{10,... | collective-permute-start | bytes 172040 | tf_op jit(solution)/shard_map/ppermute | solution.py:588
  (30 other events, 289.0 us)
where the time goes:
time: 179 us; the launch traced here: 178 us
  Pallas kernels  82.9 us (46%)
  waiting for transfers between devices  35.1 us (20%)
  starting transfers between devices  34.5 us (19%)
  local copies, waits for them, and re-layouts  16.6 us (9%)
  other arithmetic  8.03 us (4%)
    ppermute x34, waiting for transfers between devices, swap(): lax.ppermute(values, AXES, [(i, i ^ distance) for i in range(self.count)])  35.1 us
    ppermute x34, starting transfers between devices, swap(): lax.ppermute(values, AXES, [(i, i ^ distance) for i in range(self.count)])  34.5 us
    pallas_call x1, Pallas kernels, middle(): call(middle_kernel, 'middle', 29, 56, grid=(length // TILE,), in_specs=[S...  29.5 us
    pallas_call x2, Pallas kernels, attend_back(): call(functools.partial(attend_back_kernel, size), 'attend_back', 7 * coun...  23.4 us
    pallas_call x1, Pallas kernels, attend(): call(functools.partial(attend_kernel, size, tail_size), 'attend', 23, 32,...  22.1 us
    unnamed x62, local copies, waits for them, and re-layouts  11.4 us
    pallas_call x1, Pallas kernels, input_grad(): call(functools.partial(input_kernel, len(sources)), 'input', 6, 16, grid=...  4.79 us
  transfers between devices with their start and end apart: 34, of which 16 were waited for; matrix products, arithmetic and copies ran while one was open for 7% of the time, Pallas kernels for 30%

commit v1 on v0

--- a/solution.py
+++ b/solution.py
@@ -100,10 +100,7 @@
                     whole.at[digit ^ k, :, which], target.at[k], semaphores.at[2 * k + n]
                 )
             )
-    for copy in copies:
-        copy.start()
-    for copy in copies:
-        copy.wait()
+    return copies
 
 
 def pack_vectors(sums, shards, size, tail_sums, tail_size):
@@ -136,6 +133,22 @@
     lane = lax.broadcasted_iota(jnp.int32, values.shape, 1)
     mine = (lane >= number * size) & (lane < (number + 1) * size)
     return jnp.where(mine, values, jnp.zeros_like(values))
+
+
+def fill_mask(lengths_ref, hide):
+    length = hide.shape[0]
+    place = lax.broadcasted_iota(jnp.int32, (1, length), 1)
+    begin = jnp.zeros((1, length), jnp.int32)
+    bound = 0
+    for slot in range(lengths_ref.shape[1]):
+        bound = bound + lengths_ref[0, slot]
+        begin = jnp.where(place >= bound, bound, begin)
+    for number in range(length // BLOCK):
+        start, end = key_span(number)
+        queries = slice(number * BLOCK, end)
+        key = lax.broadcasted_iota(jnp.int32, (end - start, BLOCK), 0) + start
+        seen = (key >= begin[:, queries]) & (key <= place[:, queries])
+        hide[start:end, queries] = jnp.where(seen, 0.0, neg_large)
 
 
 def key_span(number):
@@ -172,9 +185,9 @@
     )
 
 
-def attend_kernel(size, tail_size, ids_ref, x_ref, hide_ref, *refs):
+def attend_kernel(size, tail_size, ids_ref, lengths_ref, x_ref, *refs):
     parts, others = refs[:4], refs[4:8]
-    q_ref, k_ref, v_ref, context_ref, table_ref, whole, semaphores = refs[8:]
+    q_ref, k_ref, v_ref, context_ref, table_ref, whole, hide, semaphores = refs[8:]
     pair = pl.program_id(0)
     x = x_ref[...]
     length, width = x.shape
@@ -184,6 +197,7 @@
         copies = fetch(ids_ref, parts, others, whole, semaphores, slice(None))
         for copy in copies:
             copy.start()
+        fill_mask(lengths_ref, hide)
         for copy in copies:
             copy.wait()
         chips = whole.shape[1]
@@ -212,13 +226,13 @@
         mixed = []
         for head in range(LANES // size):
             chosen = one_head(queries[rows], head, size)
-            scores = nt(keys[start:end], chosen) + hide_ref[start:end, rows]
+            scores = nt(keys[start:end], chosen) + hide[start:end, rows]
             weights = probabilities(scores).astype(low)
             mixed.append(nn(turned[head * size : (head + 1) * size, start:end], weights))
         context_ref[rows, :] = jnp.concatenate(mixed, axis=0).T.astype(low)
 
 
-def attend(ids, x, parts, others, hide, size, tail_size):
+def attend(ids, lengths, x, parts, others, size, tail_size):
     length, width = x.shape
     out = pl.BlockSpec((length, LANES), lambda p: (0, p))
     chips, rows, _ = parts[0].shape
@@ -226,33 +240,21 @@
         functools.partial(attend_kernel, size, tail_size),
         "attend",
         23,
-        32,
+        26,
         grid=(width // LANES,),
-        in_specs=[SCALARS, fixed(x.shape), fixed(hide.shape)] + [ANYWHERE] * 8,
+        in_specs=[SCALARS, SCALARS, fixed(x.shape)] + [ANYWHERE] * 8,
         out_specs=[out] * 4 + [fixed((3 * VECTORS, width))],
         out_shape=[jax.ShapeDtypeStruct((length, width), low)] * 4
         + [jax.ShapeDtypeStruct((3 * VECTORS, width), wide)],
         scratch_shapes=[
             pltpu.VMEM((4, chips, 2, rows, width), low),
+            pltpu.VMEM((length, length), wide),
             pltpu.SemaphoreType.DMA((8,)),
         ],
-    )(ids, x, hide, *parts, *others)
-
-
-def attend_back_kernel(
-    size,
-    q_ref,
-    k_ref,
-    v_ref,
-    incoming_ref,
-    hide_ref,
-    dq_ref,
-    dk_ref,
-    dv_ref,
-    key_total,
-    value_total,
-):
-    queries, keys, values, incoming = q_ref[...], k_ref[...], v_ref[...], incoming_ref[...]
+    )(ids, lengths, x, *parts, *others)
+
+
+def pair_back(size, queries, keys, values, incoming, hide, dq_ref, key_total, value_total):
     length = queries.shape[0]
     turned = keys.T
     key_total[...] = jnp.zeros_like(key_total)
@@ -264,7 +266,7 @@
         for head in range(LANES // size):
             chosen = one_head(queries[rows], head, size)
             arriving = one_head(incoming[rows], head, size)
-            scores = nt(keys[start:end], chosen) + hide_ref[start:end, rows]
+            scores = nt(keys[start:end], chosen) + hide[start:end, rows]
             attention = probabilities(scores)
             weight_grad = nt(values[start:end], arriving)
             balance = jnp.sum(attention * weight_grad, axis=0, keepdims=True)
@@ -273,25 +275,114 @@
             value_total[start:end, :] += nn(attention.astype(low), arriving)
             parts.append(nn(turned[head * size : (head + 1) * size, start:end], score_grad))
         dq_ref[rows, :] = (jnp.concatenate(parts, axis=0).T * (1.0 / math.sqrt(size))).astype(low)
+
+
+def first_back_kernel(size, lengths_ref, *refs):
+    given, (dq_ref, dk_ref, dv_ref), (key_total, value_total, hide) = refs[:4], refs[4:7], refs[7:]
+    fill_mask(lengths_ref, hide)
+    pair_back(size, *[ref[...] for ref in given], hide, dq_ref, key_total, value_total)
     dk_ref[...] = key_total[...].astype(low)
     dv_ref[...] = value_total[...].astype(low)
 
 
-def attend_back(queries, keys, values, incoming, hide, size, first, count):
+def first_back(lengths, queries, keys, values, incoming, size):
     length = queries.shape[0]
-    given = pl.BlockSpec((length, LANES), lambda p: (0, p + first))
-    out = pl.BlockSpec((length, LANES), lambda p: (0, p))
+    block = pl.BlockSpec((length, LANES), lambda p: (0, 0))
     return call(
-        functools.partial(attend_back_kernel, size),
-        "attend_back",
-        7 * count,
-        24,
-        grid=(count,),
-        in_specs=[given] * 4 + [fixed(hide.shape)],
-        out_specs=[out] * 3,
-        out_shape=[jax.ShapeDtypeStruct((length, count * LANES), low)] * 3,
-        scratch_shapes=[pltpu.VMEM((length, LANES), wide)] * 2,
-    )(queries, keys, values, incoming, hide)
+        functools.partial(first_back_kernel, size),
+        "first_back",
+        6,
+        16,
+        grid=(1,),
+        in_specs=[SCALARS] + [block] * 4,
+        out_specs=[block] * 3,
+        out_shape=[jax.ShapeDtypeStruct((length, LANES), low)] * 3,
+        scratch_shapes=[pltpu.VMEM((length, LANES), wide)] * 2
+        + [pltpu.VMEM((length, length), wide)],
+    )(lengths, queries, keys, values, incoming)
+
+
+def rest_back_kernel(size, ids_ref, lengths_ref, *refs):
+    given, first, (x_ref, back_ref) = refs[:4], refs[4:7], refs[7:9]
+    parts, others = refs[9:13], refs[13:17]
+    grad_x_ref, kept_ref, away_ref = refs[17:20]
+    dq_part, key_total, value_total, hide, grads, whole, full, semaphores = refs[20:]
+    step = pl.program_id(0)
+    width = x_ref.shape[1]
+    copies = fetch(ids_ref, parts, others, whole, semaphores.at[0], slice(None))
+
+    @pl.when(step == 0)
+    def _():
+        for copy in copies:
+            copy.start()
+        fill_mask(lengths_ref, hide)
+        for n in range(3):
+            grads[n, :, :LANES] = first[n][...]
+
+    pair_back(size, *[ref[...] for ref in given], hide, dq_part, key_total, value_total)
+    here = pl.ds(pl.multiple_of((step + 1) * LANES, LANES), LANES)
+    grads[0, :, here] = dq_part[...]
+    grads[1, :, here] = key_total[...].astype(low)
+    grads[2, :, here] = value_total[...].astype(low)
+
+    @pl.when(step == pl.num_programs(0) - 1)
+    def _():
+        split = full.shape[:3]
+        chips = split[1]
+        sums = []
+        for n in range(3):
+            grad = tn(x_ref[...], grads[n]).astype(low)
+            full[:, :, :, n * SHARD : (n + 1) * SHARD, :] = grad.reshape(split + (SHARD, width))
+            if n != 1:
+                sums.append(column_sum(grads[n]))
+        sums = jnp.concatenate(sums + [jnp.zeros((VECTORS - 2, width), wide)], axis=0)
+        lines = slice(3 * SHARD, 3 * SHARD + VECTORS)
+        full[:, :, :, lines, :] = jnp.zeros(split + (VECTORS, width), low)
+        for j, tile in enumerate(pack_vectors(sums, width // SHARD, SHARD, None, 0)):
+            full[j // (2 * chips), j // 2 % chips, j % 2, lines, :LANES] = tile.astype(low)
+        leaving = deliver(ids_ref, full, kept_ref, away_ref, semaphores.at[1])
+        for copy in leaving:
+            copy.start()
+        for copy in copies:
+            copy.wait()
+        total = back_ref[...]
+        for n in range(3):
+            weight = whole[:, :, :, n * SHARD : (n + 1) * SHARD, :].reshape(width, width)
+            total = total + nt(grads[n], weight)
+        grad_x_ref[...] = total
+        for copy in leaving:
+            copy.wait()
+
+
+def rest_back(ids, lengths, queries, keys, values, incoming, first, x, back, parts, others, size):
+    length, width = x.shape
+    chips, rows, _ = parts[0].shape
+    block = pl.BlockSpec((length, LANES), lambda p: (0, p + 1))
+    packed = jax.ShapeDtypeStruct((4, chips, rows, width), low)
+    return call(
+        functools.partial(rest_back_kernel, size),
+        "rest_back",
+        26,
+        36,
+        grid=(width // LANES - 1,),
+        in_specs=[SCALARS] * 2
+        + [block] * 4
+        + [fixed((length, LANES))] * 3
+        + [fixed(x.shape), fixed(back.shape)]
+        + [ANYWHERE] * 8,
+        out_specs=[fixed(back.shape)] + [ANYWHERE] * 2,
+        out_shape=[jax.ShapeDtypeStruct(back.shape, wide)] + [packed] * 2,
+        scratch_shapes=[
+            pltpu.VMEM((length, LANES), low),
+            pltpu.VMEM((length, LANES), wide),
+            pltpu.VMEM((length, LANES), wide),
+            pltpu.VMEM((length, length), wide),
+            pltpu.VMEM((3, length, width), low),
+            pltpu.VMEM((4, chips, 2, rows, width), low),
+            pltpu.VMEM((4, chips, 2, rows, width), low),
+            pltpu.SemaphoreType.DMA((2, 8)),
+        ],
+    )(ids, lengths, queries, keys, values, incoming, *first, x, back, *parts, *others)
 
 
 def middle_kernel(ids_ref, x_ref, y_ref, cotangent_ref, context_ref, table_ref, *refs):
@@ -434,7 +525,11 @@
         )
         for j, tile in enumerate(tiles):
             full[j // (2 * chips), j // 2 % chips, j % 2, lines, :LANES] = tile.astype(low)
-        deliver(ids_ref, full, kept_ref, away_ref, semaphores.at[0])
+        leaving = deliver(ids_ref, full, kept_ref, away_ref, semaphores.at[0])
+        for copy in leaving:
+            copy.start()
+        for copy in leaving:
+            copy.wait()
 
 
 def middle(ids, x, y, cotangent, context, table, parts, others, inner):
@@ -446,7 +541,7 @@
         middle_kernel,
         "middle",
         29,
-        56,
+        44,
         grid=(length // TILE,),
         in_specs=[SCALARS] + [block] * 4 + [fixed(table.shape)] + [ANYWHERE] * 8,
         out_specs=[block] * 4 + [ANYWHERE] * 2,
@@ -469,95 +564,6 @@
     )(ids, x, y, cotangent, context, table, *parts, *others)
 
 
-def weights_kernel(calls, ids_ref, x_ref, *refs):
-    parts = [refs[3 * n : 3 * n + 3] for n in range(calls)]
-    kept_ref, away_ref, full, semaphores = refs[3 * calls :]
-    x = x_ref[...]
-    width = x.shape[1]
-    split = full.shape[:3]
-    chips = split[1]
-    sums = []
-    for n in range(3):
-        whole = jnp.concatenate([part[n][...] for part in parts], axis=1)
-        grad = tn(x, whole).astype(low)
-        full[:, :, :, n * SHARD : (n + 1) * SHARD, :] = grad.reshape(split + (SHARD, width))
-        if n != 1:
-            sums.append(column_sum(whole))
-    sums = jnp.concatenate(sums + [jnp.zeros((VECTORS - 2, width), wide)], axis=0)
-    lines = slice(3 * SHARD, 3 * SHARD + VECTORS)
-    full[:, :, :, lines, :] = jnp.zeros(split + (VECTORS, width), low)
-    for j, tile in enumerate(pack_vectors(sums, width // SHARD, SHARD, None, 0)):
-        full[j // (2 * chips), j // 2 % chips, j % 2, lines, :LANES] = tile.astype(low)
-    deliver(ids_ref, full, kept_ref, away_ref, semaphores)
-
-
-def weight_grads(ids, x, parts):
-    length, width = x.shape
-    flat = [array for part in parts for array in part]
-    chips, rows = width // SHARD // 8, 3 * SHARD + VECTORS
-    return call(
-        functools.partial(weights_kernel, len(parts)),
-        "weights",
-        5,
-        24,
-        grid=(1,),
-        in_specs=[SCALARS] + [fixed(array.shape) for array in [x] + flat],
-        out_specs=[ANYWHERE] * 2,
-        out_shape=[jax.ShapeDtypeStruct((4, chips, rows, width), low)] * 2,
-        scratch_shapes=[
-            pltpu.VMEM((4, chips, 2, rows, width), low),
-            pltpu.SemaphoreType.DMA((8,)),
-        ],
-    )(ids, x, *flat)
-
-
-def input_kernel(calls, ids_ref, back_ref, *refs):
-    sources = [refs[3 * n : 3 * n + 3] for n in range(calls)]
-    refs = refs[3 * calls :]
-    parts, others = refs[:4], refs[4:8]
-    out_ref, whole, semaphores = refs[8:]
-    width = back_ref.shape[1]
-
-    @pl.when(pl.program_id(0) == 0)
-    def _():
-        copies = fetch(ids_ref, parts, others, whole, semaphores, slice(None))
-        for copy in copies:
-            copy.start()
-        for copy in copies:
-            copy.wait()
-
-    total = back_ref[...]
-    for n in range(3):
-        grad = jnp.concatenate([source[n][...] for source in sources], axis=1)
-        weight = whole[:, :, :, n * SHARD : (n + 1) * SHARD, :].reshape(width, width)
-        total = total + nt(grad, weight)
-    out_ref[...] = total
-
-
-def input_grad(ids, back, sources, parts, others):
-    length, width = back.shape
-
-    def block(array):
-        return pl.BlockSpec((BLOCK, array.shape[1]), lambda p: (p, 0))
-
-    flat = [array for source in sources for array in source]
-    chips, rows, _ = parts[0].shape
-    return call(
-        functools.partial(input_kernel, len(sources)),
-        "input",
-        6,
-        16,
-        grid=(length // BLOCK,),
-        in_specs=[SCALARS, block(back)] + [block(array) for array in flat] + [ANYWHERE] * 8,
-        out_specs=block(back),
-        out_shape=jax.ShapeDtypeStruct(back.shape, wide),
-        scratch_shapes=[
-            pltpu.VMEM((4, chips, 2, rows, width), low),
-            pltpu.SemaphoreType.DMA((8,)),
-        ],
-    )(ids, back, *flat, *parts, *others)
-
-
 def radices(extent):
     found = []
     while extent > 1:
@@ -635,15 +641,6 @@
                 kept = kept + self.swap(part, (k + 1) << shift).astype(wide)
             total = kept
         return total
-
-
-def mask(lengths, length):
-    bounds = jnp.cumsum(lengths)
-    position = jnp.arange(length, dtype=jnp.int32)
-    passed = position[:, None] >= bounds[None, :]
-    begin = jnp.sum(jnp.where(passed, lengths[None, :], 0), axis=1)
-    key = position[:, None]
-    return jnp.where((key >= begin[None, :]) & (key <= position[None, :]), 0.0, neg_large)
 
 
 def resplit(pieces):
@@ -713,28 +710,29 @@
     early = jnp.concatenate(
         [query_weight, key_weight, value_weight, pack_lines(vectors, up_bias)], axis=0
     )[None]
+    early, *local = lax.optimization_barrier((early, down_weight, up_weight, output_weight))
     late = jnp.concatenate(
-        [down_weight]
-        + [up_weight[:, c * width : (c + 1) * width] for c in range(columns)]
-        + [output_weight],
+        [local[0]] + [local[1][:, c * width : (c + 1) * width] for c in range(columns)] + [local[2]],
         axis=0,
     )[None]
+    late = links.spread(late, links.near[:-1])
+    shift, radix = links.near[-1]
+    received = [links.swap(late, k << shift) for k in range(2, radix)]
     early = links.spread(early, links.near)
-    early, late = lax.optimization_barrier((early, late))
+    gated, early = lax.optimization_barrier((late, early))
+    received = [links.swap(gated, 1 << shift)] + received
     early = links.spread(early, links.far[:-1])
-    late = links.spread(late, links.near[:-1])
-    arriving = links.send(early, *links.far[-1]), links.send(late, *links.near[-1])
-    hide = mask(doc_lengths[0], length)
-    arriving, hide = lax.optimization_barrier((arriving, hide))
-    late = links.place(late, arriving[1], *links.near[-1])
+    arriving = links.send(early, *links.far[-1])
+    received, early = lax.optimization_barrier((received, early))
+    late = links.place(late, received, *links.near[-1])
     late = links.spread(late, links.far[:-1])
     if direct:
         ids = jnp.stack([links.digit(*links.far[-1]), links.flat() & 1])
-        early_parts = [early] + arriving[0]
+        early_parts = [early] + arriving
         early_others = [links.swap(part, 1) for part in early_parts]
     else:
         ids = jnp.zeros((2,), jnp.int32)
-        early = links.pair(links.place(early, arriving[0], *links.far[-1]))
+        early = links.pair(links.place(early, arriving, *links.far[-1]))
         squares = [
             early[:, n * rows : (n + 1) * rows].reshape(-1, SHARD, width) for n in range(3)
         ]
@@ -747,7 +745,7 @@
         early_parts, early_others = resplit(squares + [pack_lines(lines, last)])
     received = links.send(late, *links.far[-1])
     queries, keys, values, context, table = attend(
-        ids, stream_x, early_parts, early_others, hide, size, tail
+        ids, doc_lengths, stream_x, early_parts, early_others, size, tail
     )
     received, context = lax.optimization_barrier((received, context))
     if direct:
@@ -794,8 +792,8 @@
         )
         away, kept = links.halve(full)
     arriving = links.swap(away, 1)
-    part_a = attend_back(queries, keys, values, context_grad, hide, size, 0, 1)
-    arriving, part_a = lax.optimization_barrier((arriving, part_a))
+    first = first_back(doc_lengths, queries, keys, values, context_grad, size)
+    arriving, first = lax.optimization_barrier((arriving, first))
     if direct:
         total, *leaving = first_sums(kept, arriving)
         leaving = [part.astype(low) for part in leaving]
@@ -804,10 +802,20 @@
         total, leaving = links.cut(total, *links.far[0])
     leaving, context_grad = lax.optimization_barrier((leaving, context_grad))
     arriving = links.receive(leaving, links.far[0][0])
-    part_b = attend_back(
-        queries, keys, values, context_grad, hide, size, 1, width // LANES - 1
+    grad_x, kept, away = rest_back(
+        ids,
+        doc_lengths,
+        queries,
+        keys,
+        values,
+        context_grad,
+        first,
+        stream_x,
+        back,
+        early_parts,
+        early_others,
+        size,
     )
-    kept, away = weight_grads(ids, stream_x, [part_a, part_b])
     if not direct:
         full = restore(kept, away)
         full = jnp.concatenate(
@@ -819,19 +827,31 @@
             axis=1,
         )
         away, kept = links.halve(full)
+    arriving, kept, away = lax.optimization_barrier((arriving, kept, away))
     crossing = links.swap(away, 1)
-    back, away = lax.optimization_barrier((back, away))
-    grad_x = input_grad(ids, back, [part_a, part_b], early_parts, early_others)
+    if direct:
+        mine, *leaving = first_sums(kept, crossing)
+        leaving = [part.astype(low) for part in leaving]
+    else:
+        mine = links.collect(kept.astype(wide) + crossing.astype(wide), links.far[1:])
+        mine, leaving = links.cut(mine, *links.far[0])
+    arriving, leaving = lax.optimization_barrier((arriving, leaving))
+    crossing = links.receive(leaving, links.far[0][0])
     for part in arriving:
         total = total + part.astype(wide)
-    if direct:
-        mine, *leaving = first_sums(kept, crossing)
-        for part in links.receive([part.astype(low) for part in leaving], links.far[0][0]):
-            mine = mine + part.astype(wide)
-    else:
-        mine = links.collect(kept.astype(wide) + crossing.astype(wide), links.far)
-    total = links.collect(total, links.near)[0]
-    mine = links.collect(mine, links.near)[0]
+    for part in crossing:
+        mine = mine + part.astype(wide)
+    total = links.collect(total, links.near[1:])
+    mine = links.collect(mine, links.near[1:])
+    shift, radix = links.near[0]
+    total, away = links.cut(total, shift, radix)
+    arriving = links.receive(away, shift)
+    mine, leaving = links.cut(mine, shift, radix)
+    early_part, leaving = lax.optimization_barrier((arriving[0], leaving))
+    crossing = links.receive(leaving, shift)
+    arriving, crossing[0] = lax.optimization_barrier((arriving[1:], crossing[0]))
+    total = (total + sum(part.astype(wide) for part in [early_part] + arriving))[0]
+    mine = (mine + sum(part.astype(wide) for part in crossing))[0]
 
     if direct:
         at = 2 * share + rows

time: 179 us -> 159 us (0.89)
  local copies, waits for them, and re-layouts: 16.6 us -> 8.74 us
  other arithmetic: 8.03 us -> 3.67 us
  waiting for transfers between devices: 35.1 us -> 31.1 us
  Pallas kernels: 82.9 us -> 79.8 us
    unnamed x62 -> x20, local copies, waits for them, and re-layouts: 11.4 us -> 4.26 us
    ppermute x34, waiting for transfers between devices: 35.1 us -> 31.1 us  [swap(): lax.ppermute(values, AXES, [(i, i ^ distance) for i in range(self.count)])]
    pallas_call x6 -> x4, Pallas kernels: 82.9 us -> 79.8 us  [the longest x1 27 us: middle(): call(middle_kernel, 'middle', 29, 44, grid=(length // TILE,), in_specs=[S...]
    select_n x1 -> x0, other arithmetic: 2.61 us -> none  [mask(): jnp.where((key >= begin[None, :]) & (key <= position[None, :]), 0.0, neg_...]
  transfers between devices with their start and end apart: 34 -> 34, of which waited for: 16 -> 13; matrix products, arithmetic and copies ran while one was open for 7% -> 5% of each run, Pallas kernels for 30% -> 33%
where the time goes in v1:
time: 159 us
  Pallas kernels  79.8 us (50%)
  starting transfers between devices  34.4 us (22%)
  waiting for transfers between devices  31.1 us (20%)
  local copies, waits for them, and re-layouts  8.74 us (5%)
  other arithmetic  3.67 us (2%)
    ppermute x34, starting transfers between devices, swap(): lax.ppermute(values, AXES, [(i, i ^ distance) for i in range(self.count)])  34.4 us
    ppermute x34, waiting for transfers between devices, swap(): lax.ppermute(values, AXES, [(i, i ^ distance) for i in range(self.count)])  31.1 us
    pallas_call x1, Pallas kernels, middle(): call(middle_kernel, 'middle', 29, 44, grid=(length // TILE,), in_specs=[S...  27 us
    pallas_call x1, Pallas kernels, rest_back(): call(functools.partial(rest_back_kernel, size), 'rest_back', 26, 36, grid...  24.7 us
    pallas_call x1, Pallas kernels, attend(): call(functools.partial(attend_kernel, size, tail_size), 'attend', 23, 26,...  22.1 us
    pallas_call x1, Pallas kernels, first_back(): call(functools.partial(first_back_kernel, size), 'first_back', 6, 16, gri...  6.04 us
    unnamed x20, local copies, waits for them, and re-layouts  4.26 us
  transfers between devices with their start and end apart: 34, of which 13 were waited for; matrix products, arithmetic and copies ran while one was open for 5% of the time, Pallas kernels for 33%

profile of v1, /device:TPU:0, one launch (start us, length us, event | category | flops | bytes accessed | tf_op | source)
XLA Modules:
  0.0 158.6 jit_solution(5284484169467947043)
XLA Ops:
  0.7 0.8 pad_add_fusion
  1.5 0.8 maximum_bitcast_fusion
  2.2 5.0 %collective-permute-start.2 = (bf16[1,56,512]{2,1,0:T(8,128)(2,1)S(1)}, bf16[1,56,512]{2,1,0:T(8,128)(2,1)S(1)}, u32[]{:S(2)}, u32[]{:S(2)}) collective-permute-start(bf16[1,56,512]{2,1,0:T(8,128)(2,1)S(1)} %maximum_bitcast_fusion), channel_id=1, source_target_pairs={{0,6},{1,7},{2,4},{3,5},{4,2},{5,3},{6,0},{7,1},{8,14},{9,15},{10,... | collective-permute-start | bytes 172040 | tf_op jit(solution)/shard_map/ppermute | solution.py:594
  7.9 0.8 constant_dynamic-update-slice_fusion.1
  12.3 2.3 %collective-permute-start.4 = (bf16[1,144,512]{2,1,0:T(8,128)(2,1)S(1)}, bf16[1,144,512]{2,1,0:T(8,128)(2,1)S(1)}, u32[]{:S(2)}, u32[]{:S(2)}) collective-permute-start(bf16[1,144,512]{2,1,0:T(8,128)(2,1)S(1)} %bitcast.84), channel_id=1, source_target_pairs={{0,4},{1,5},{2,6},{3,7},{4,0},{5,1},{6,2},{7,3},{8,12},{9,13},{10,... | collective-permute-start | bytes 442376 | tf_op jit(solution)/shard_map/ppermute | solution.py:594
  14.7 1.5 collective-permute-start.5
  16.2 2.5 %collective-permute-start.11 = (bf16[4,56,512]{2,1,0:T(8,128)(2,1)S(1)}, bf16[4,56,512]{2,1,0:T(8,128)(2,1)S(1)}, u32[]{:S(2)}, u32[]{:S(2)}) collective-permute-start(bf16[4,56,512]{2,1,0:T(8,128)(2,1)S(1)} %constant_dynamic-update-slice_fusion.5.refs_0_.refs_9_), channel_id=1, source_target_pairs={{0,24},{1,25},{2,26},{3,27},{4,28},{5,29},{6,30},{7,31},{8,16},{9,... | collective-permute-start | bytes 688136 | tf_op jit(solution)/shard_map/ppermute | solution.py:594
  19.8 5.8 %collective-permute-done.4 = bf16[1,144,512]{2,1,0:T(8,128)(2,1)S(1)} collective-permute-done((bf16[1,144,512]{2,1,0:T(8,128)(2,1)S(1)}, bf16[1,144,512]{2,1,0:T(8,128)(2,1)S(1)}, u32[]{:S(2)}, u32[]{:S(2)}) %collective-permute-start.4) | collective-permute-done | bytes 147488 | tf_op jit(solution)/shard_map/ppermute | solution.py:594
  25.7 5.0 %collective-permute-done.3 = bf16[1,144,512]{2,1,0:T(8,128)(2,1)S(1)} collective-permute-done((bf16[1,144,512]{2,1,0:T(8,128)(2,1)S(1)}, bf16[1,144,512]{2,1,0:T(8,128)(2,1)S(1)}, u32[]{:S(2)}, u32[]{:S(2)}) %collective-permute-start.3) | collective-permute-done | bytes 147488 | tf_op jit(solution)/shard_map/ppermute | solution.py:594
  31.9 2.5 %collective-permute-start.8 = (bf16[4,144,512]{2,1,0:T(8,128)(2,1)S(1)}, bf16[4,144,512]{2,1,0:T(8,128)(2,1)S(1)}, u32[]{:S(2)}, u32[]{:S(2)}) collective-permute-start(bf16[4,144,512]{2,1,0:T(8,128)(2,1)S(1)} %constant_dynamic-update-slice_fusion.2.refs_0_), channel_id=1, source_target_pairs={{0,24},{1,25},{2,26},{3,27},{4,28},{5,29},{6,30},{7,31},{8,16},{9,... | collective-permute-start | bytes 1769480 | tf_op jit(solution)/shard_map/ppermute | solution.py:594
  35.6 22.1 %attend.1 = (bf16[1024,512]{1,0:T(8,128)(2,1)S(1)}, bf16[1024,512]{1,0:T(8,128)(2,1)S(1)}, bf16[1024,512]{1,0:T(8,128)(2,1)S(1)}, bf16[1024,512]{1,0:T(8,128)(2,1)S(1)}, f32[24,512]{1,0:T(8,128)S(1)}) custom-call(s32[2]{0:T(128)S(1)} %pad_add_fusion.1.ids_ref, s32[1,16]{1,0:T(1,128)S(1)} %copy-done.3, bf16[1024,512]{1,0:T(8,128)(2,1)S(1)} %copy-done.2, ...), custom_call_target="tpu_custom_call" | custom-call | flops 5750000128 | bytes 1024 | tf_op jit(solution)/shard_map/attend/pallas_call | solution.py:239
  57.8 3.1 %collective-permute-done.7.refs_2_ = bf16[4,144,512]{2,1,0:T(8,128)(2,1)S(1)} collective-permute-done((bf16[4,144,512]{2,1,0:T(8,128)(2,1)S(1)}, bf16[4,144,512]{2,1,0:T(8,128)(2,1)S(1)}, u32[]{:S(2)}, u32[]{:S(2)}) %collective-permute-start.7) | collective-permute-done | bytes 589856 | tf_op jit(solution)/shard_map/ppermute | solution.py:594
  61.4 1.5 collective-permute-done.17.refs_5_
  62.9 0.8 collective-permute-done.18.refs_6_
  63.8 0.8 collective-permute-done.19.refs_7_
  64.6 27.0 %middle.1 = (bf16[1024,512]{1,0:T(8,128)(2,1)}, f32[1024,512]{1,0:T(8,128)}, f32[1024,512]{1,0:T(8,128)}, bf16[1024,512]{1,0:T(8,128)(2,1)S(1)}, bf16[4,4,152,51...) custom-call(s32[2]{0:T(128)S(1)} %pad_add_fusion.1.ids_ref, bf16[1024,512]{1,0:T(8,128)(2,1)S(1)} %copy-done.2, ...), custom_call_target="tpu_custom_call" | custom-call | flops 7249999872 | bytes 1024 | tf_op jit(solution)/shard_map/middle/pallas_call | solution.py:540
  91.8 6.0 %first_back.1 = (bf16[1024,128]{1,0:T(8,128)(2,1)S(1)}, bf16[1024,128]{1,0:T(8,128)(2,1)S(1)}, bf16[1024,128]{1,0:T(8,128)(2,1)S(1)}) custom-call(s32[1,16]{1,0:T(1,128)S(1)} %copy-done.3, bf16[1024,512]{1,0:T(8,128)(2,1)S(1)} %get-tuple-element.94.refs_0_, bf16[1024,512]{1,0:T(8,128)(2,1)S(1)} %get-tuple-element.95.refs_1_, ...), custom_call_target="tpu_custom_call" | custom-call | flops 1500000000 | bytes 1024 | tf_op jit(solution)/shard_map/first_back/pallas_call | solution.py:291
  98.4 1.6 collective-permute-start.21
  99.9 0.8 collective-permute-start.22
  100.8 1.2 collective-permute-start.23
  101.9 24.7 %rest_back.1 = (f32[1024,512]{1,0:T(8,128)}, bf16[4,4,56,512]{3,2,1,0:T(8,128)(2,1)S(1)}, bf16[4,4,56,512]{3,2,1,0:T(8,128)(2,1)S(1)}) custom-call(s32[2]{0:T(128)S(1)} %pad_add_fusion.1.ids_ref, s32[1,16]{1,0:T(1,128)S(1)} %copy-done.3, bf16[1024,512]{1,0:T(8,128)(2,1)S(1)} %get-tuple-element.94.refs_0_, bf16[1024,512]{1,0:T(8,128)(2,1)S(1)} %get-tuple-element.95.refs_1_, ...), custom_call_target="tpu_custom_call" | custom-call | flops 6499999744 | bytes 1024 | tf_op jit(solution)/shard_map/rest_back/pallas_call | solution.py:362
  126.6 2.8 %collective-permute-done.22 = bf16[4,152,512]{2,1,0:T(8,128)(2,1)S(1)} collective-permute-done((bf16[4,152,512]{2,1,0:T(8,128)(2,1)S(1)}, bf16[4,152,512]{2,1,0:T(8,128)(2,1)S(1)}, u32[]{:S(2)}, u32[]{:S(2)}) %collective-permute-start.22) | collective-permute-done | bytes 622624 | tf_op jit(solution)/shard_map/ppermute | solution.py:594
  129.4 2.5 %collective-permute-done.24 = bf16[4,4,56,512]{3,2,1,0:T(8,128)(2,1)S(1)} collective-permute-done((bf16[4,4,56,512]{3,2,1,0:T(8,128)(2,1)S(1)}, bf16[4,4,56,512]{3,2,1,0:T(8,128)(2,1)S(1)}, u32[]{:S(2)}, u32[]{:S(2)}) %collective-permute-start.24) | collective-permute-done | bytes 917536 | tf_op jit(solution)/shard_map/ppermute | solution.py:594
  132.6 1.4 collective-permute-start.26
  134.1 1.5 collective-permute-start.27
  136.1 2.9 %collective-permute-start.29 = (bf16[1,152,512]{2,1,0:T(8,128)(2,1)S(1)}, bf16[1,152,512]{2,1,0:T(8,128)(2,1)S(1)}, u32[]{:S(2)}, u32[]{:S(2)}) collective-permute-start(bf16[1,152,512]{2,1,0:T(8,128)(2,1)S(1)} %get-tuple-element.140), channel_id=1, source_target_pairs={{0,6},{1,7},{2,4},{3,5},{4,2},{5,3},{6,0},{7,1},{8,14},{9,15},{10,... | collective-permute-start | bytes 466952 | tf_op jit(solution)/shard_map/ppermute | solution.py:594
  139.0 1.6 collective-permute-done.25
  140.5 1.6 %collective-permute-start.28 = (bf16[1,152,512]{2,1,0:T(8,128)(2,1)S(1)}, bf16[1,152,512]{2,1,0:T(8,128)(2,1)S(1)}, u32[]{:S(2)}, u32[]{:S(2)}) collective-permute-start(bf16[1,152,512]{2,1,0:T(8,128)(2,1)S(1)} %get-tuple-element.142), channel_id=1, source_target_pairs={{0,4},{1,5},{2,6},{3,7},{4,0},{5,1},{6,2},{7,3},{8,12},{9,13},{10,... | collective-permute-start | bytes 466952 | tf_op jit(solution)/shard_map/ppermute | solution.py:594
  142.2 2.7 %collective-permute-done.27 = bf16[4,56,512]{2,1,0:T(8,128)(2,1)S(1)} collective-permute-done((bf16[4,56,512]{2,1,0:T(8,128)(2,1)S(1)}, bf16[4,56,512]{2,1,0:T(8,128)(2,1)S(1)}, u32[]{:S(2)}, u32[]{:S(2)}) %collective-permute-start.27) | collective-permute-done | bytes 229408 | tf_op jit(solution)/shard_map/ppermute | solution.py:594
  145.1 3.7 %collective-permute-done.30 = bf16[1,152,512]{2,1,0:T(8,128)(2,1)S(1)} collective-permute-done((bf16[1,152,512]{2,1,0:T(8,128)(2,1)S(1)}, bf16[1,152,512]{2,1,0:T(8,128)(2,1)S(1)}, u32[]{:S(2)}, u32[]{:S(2)}) %collective-permute-start.30) | collective-permute-done | bytes 155680 | tf_op jit(solution)/shard_map/ppermute | solution.py:594
  149.2 1.0 collective-permute-start.32
  150.2 3.0 %collective-permute-start.33 = (bf16[1,56,512]{2,1,0:T(8,128)(2,1)S(1)}, bf16[1,56,512]{2,1,0:T(8,128)(2,1)S(1)}, u32[]{:S(2)}, u32[]{:S(2)}) collective-permute-start(bf16[1,56,512]{2,1,0:T(8,128)(2,1)S(1)} %get-tuple-element.130), channel_id=1, source_target_pairs={{0,6},{1,7},{2,4},{3,5},{4,2},{5,3},{6,0},{7,1},{8,14},{9,15},{10,... | collective-permute-start | bytes 172040 | tf_op jit(solution)/shard_map/ppermute | solution.py:594
  (89 shorter events, 16.3 us)
Async XLA Ops:
  2.2 14.0 %collective-permute-start.2 = (bf16[1,56,512]{2,1,0:T(8,128)(2,1)S(1)}, bf16[1,56,512]{2,1,0:T(8,128)(2,1)S(1)}, u32[]{:S(2)}, u32[]{:S(2)}) collective-permute-start(bf16[1,56,512]{2,1,0:T(8,128)(2,1)S(1)} %maximum_bitcast_fusion), channel_id=1, source_target_pairs={{0,6},{1,7},{2,4},{3,5},{4,2},{5,3},{6,0},{7,1},{8,14},{9,15},{10,... | collective-permute-start | bytes 172040 | tf_op jit(solution)/shard_map/ppermute | solution.py:594
  7.3 8.9 %collective-permute-start.1 = (bf16[1,56,512]{2,1,0:T(8,128)(2,1)S(1)}, bf16[1,56,512]{2,1,0:T(8,128)(2,1)S(1)}, u32[]{:S(2)}, u32[]{:S(2)}) collective-permute-start(bf16[1,56,512]{2,1,0:T(8,128)(2,1)S(1)} %maximum_bitcast_fusion), channel_id=1, source_target_pairs={{0,4},{1,5},{2,6},{3,7},{4,0},{5,1},{6,2},{7,3},{8,12},{9,13},{10,... | collective-permute-start | bytes 172040 | tf_op jit(solution)/shard_map/ppermute | solution.py:594
  7.3 8.9 %collective-permute-start = (bf16[1,56,512]{2,1,0:T(8,128)(2,1)S(1)}, bf16[1,56,512]{2,1,0:T(8,128)(2,1)S(1)}, u32[]{:S(2)}, u32[]{:S(2)}) collective-permute-start(bf16[1,56,512]{2,1,0:T(8,128)(2,1)S(1)} %maximum_bitcast_fusion), channel_id=1, source_target_pairs={{0,2},{1,3},{2,0},{3,1},{4,6},{5,7},{6,4},{7,5},{8,10},{9,11},{10,... | collective-permute-start | bytes 172040 | tf_op jit(solution)/shard_map/ppermute | solution.py:594
  12.3 13.3 %collective-permute-start.4 = (bf16[1,144,512]{2,1,0:T(8,128)(2,1)S(1)}, bf16[1,144,512]{2,1,0:T(8,128)(2,1)S(1)}, u32[]{:S(2)}, u32[]{:S(2)}) collective-permute-start(bf16[1,144,512]{2,1,0:T(8,128)(2,1)S(1)} %bitcast.84), channel_id=1, source_target_pairs={{0,4},{1,5},{2,6},{3,7},{4,0},{5,1},{6,2},{7,3},{8,12},{9,13},{10,... | collective-permute-start | bytes 442376 | tf_op jit(solution)/shard_map/ppermute | solution.py:594
  14.7 11.0 %collective-permute-start.5 = (bf16[1,144,512]{2,1,0:T(8,128)(2,1)S(1)}, bf16[1,144,512]{2,1,0:T(8,128)(2,1)S(1)}, u32[]{:S(2)}, u32[]{:S(2)}) collective-permute-start(bf16[1,144,512]{2,1,0:T(8,128)(2,1)S(1)} %bitcast.85), channel_id=1, source_target_pairs={{0,6},{1,7},{2,4},{3,5},{4,2},{5,3},{6,0},{7,1},{8,14},{9,15},{10,... | collective-permute-start | bytes 442376 | tf_op jit(solution)/shard_map/ppermute | solution.py:594
  16.2 14.5 %collective-permute-start.11 = (bf16[4,56,512]{2,1,0:T(8,128)(2,1)S(1)}, bf16[4,56,512]{2,1,0:T(8,128)(2,1)S(1)}, u32[]{:S(2)}, u32[]{:S(2)}) collective-permute-start(bf16[4,56,512]{2,1,0:T(8,128)(2,1)S(1)} %constant_dynamic-update-slice_fusion.5.refs_0_.refs_9_), channel_id=1, source_target_pairs={{0,24},{1,25},{2,26},{3,27},{4,28},{5,29},{6,30},{7,31},{8,16},{9,... | collective-permute-start | bytes 688136 | tf_op jit(solution)/shard_map/ppermute | solution.py:594
  18.8 12.6 %collective-permute-start.10 = (bf16[4,56,512]{2,1,0:T(8,128)(2,1)S(1)}, bf16[4,56,512]{2,1,0:T(8,128)(2,1)S(1)}, u32[]{:S(2)}, u32[]{:S(2)}) collective-permute-start(bf16[4,56,512]{2,1,0:T(8,128)(2,1)S(1)} %constant_dynamic-update-slice_fusion.5.refs_0_.refs_9_), channel_id=1, source_target_pairs={{0,16},{1,17},{2,18},{3,19},{4,20},{5,21},{6,22},{7,23},{8,24},{9,... | collective-permute-start | bytes 688136 | tf_op jit(solution)/shard_map/ppermute | solution.py:594
  19.3 12.2 %collective-permute-start.9 = (bf16[4,56,512]{2,1,0:T(8,128)(2,1)S(1)}, bf16[4,56,512]{2,1,0:T(8,128)(2,1)S(1)}, u32[]{:S(2)}, u32[]{:S(2)}) collective-permute-start(bf16[4,56,512]{2,1,0:T(8,128)(2,1)S(1)} %constant_dynamic-update-slice_fusion.5.refs_0_.refs_9_), channel_id=1, source_target_pairs={{0,8},{1,9},{2,10},{3,11},{4,12},{5,13},{6,14},{7,15},{8,0},{9,1},... | collective-permute-start | bytes 688136 | tf_op jit(solution)/shard_map/ppermute | solution.py:594
  25.6 5.1 %collective-permute-start.3 = (bf16[1,144,512]{2,1,0:T(8,128)(2,1)S(1)}, bf16[1,144,512]{2,1,0:T(8,128)(2,1)S(1)}, u32[]{:S(2)}, u32[]{:S(2)}) collective-permute-start(bf16[1,144,512]{2,1,0:T(8,128)(2,1)S(1)} %bitcast.86), channel_id=1, source_target_pairs={{0,2},{1,3},{2,0},{3,1},{4,6},{5,7},{6,4},{7,5},{8,10},{9,11},{10,... | collective-permute-start | bytes 442376 | tf_op jit(solution)/shard_map/ppermute | solution.py:594
  30.7 3.7 %collective-permute-start.12 = (bf16[4,56,512]{2,1,0:T(8,128)(2,1)S(1)}, bf16[4,56,512]{2,1,0:T(8,128)(2,1)S(1)}, u32[]{:S(2)}, u32[]{:S(2)}) collective-permute-start(bf16[4,56,512]{2,1,0:T(8,128)(2,1)S(1)} %constant_dynamic-update-slice_fusion.5.refs_0_.refs_9_), channel_id=1, source_target_pairs={{0,1},{1,0},{2,3},{3,2},{4,5},{5,4},{6,7},{7,6},{8,9},{9,8},{10,11... | collective-permute-start | bytes 688136 | tf_op jit(solution)/shard_map/ppermute | solution.py:594
  30.8 4.2 %collective-permute-start.15 = (bf16[4,56,512]{2,1,0:T(8,128)(2,1)S(1)}, bf16[4,56,512]{2,1,0:T(8,128)(2,1)S(1)}, u32[]{:S(2)}, u32[]{:S(2)}) collective-permute-start(bf16[4,56,512]{2,1,0:T(8,128)(2,1)S(1)} %collective-permute-done.11.refs_3_.refs_12_), channel_id=1, source_target_pairs={{0,1},{1,0},{2,3},{3,2},{4,5},{5,4},{6,7},{7,6},{8,9},{9,8},{10,11... | collective-permute-start | bytes 688136 | tf_op jit(solution)/shard_map/ppermute | solution.py:594
  31.4 4.2 %collective-permute-start.14 = (bf16[4,56,512]{2,1,0:T(8,128)(2,1)S(1)}, bf16[4,56,512]{2,1,0:T(8,128)(2,1)S(1)}, u32[]{:S(2)}, u32[]{:S(2)}) collective-permute-start(bf16[4,56,512]{2,1,0:T(8,128)(2,1)S(1)} %collective-permute-done.10.refs_2_.refs_11_), channel_id=1, source_target_pairs={{0,1},{1,0},{2,3},{3,2},{4,5},{5,4},{6,7},{7,6},{8,9},{9,8},{10,11... | collective-permute-start | bytes 688136 | tf_op jit(solution)/shard_map/ppermute | solution.py:594
  31.4 4.2 %collective-permute-start.13 = (bf16[4,56,512]{2,1,0:T(8,128)(2,1)S(1)}, bf16[4,56,512]{2,1,0:T(8,128)(2,1)S(1)}, u32[]{:S(2)}, u32[]{:S(2)}) collective-permute-start(bf16[4,56,512]{2,1,0:T(8,128)(2,1)S(1)} %collective-permute-done.9.refs_1_.refs_10_), channel_id=1, source_target_pairs={{0,1},{1,0},{2,3},{3,2},{4,5},{5,4},{6,7},{7,6},{8,9},{9,8},{10,11... | collective-permute-start | bytes 688136 | tf_op jit(solution)/shard_map/ppermute | solution.py:594
  31.9 25.9 %collective-permute-start.8 = (bf16[4,144,512]{2,1,0:T(8,128)(2,1)S(1)}, bf16[4,144,512]{2,1,0:T(8,128)(2,1)S(1)}, u32[]{:S(2)}, u32[]{:S(2)}) collective-permute-start(bf16[4,144,512]{2,1,0:T(8,128)(2,1)S(1)} %constant_dynamic-update-slice_fusion.2.refs_0_), channel_id=1, source_target_pairs={{0,24},{1,25},{2,26},{3,27},{4,28},{5,29},{6,30},{7,31},{8,16},{9,... | collective-permute-start | bytes 1769480 | tf_op jit(solution)/shard_map/ppermute | solution.py:594
  34.4 26.4 %collective-permute-start.7 = (bf16[4,144,512]{2,1,0:T(8,128)(2,1)S(1)}, bf16[4,144,512]{2,1,0:T(8,128)(2,1)S(1)}, u32[]{:S(2)}, u32[]{:S(2)}) collective-permute-start(bf16[4,144,512]{2,1,0:T(8,128)(2,1)S(1)} %constant_dynamic-update-slice_fusion.2.refs_0_), channel_id=1, source_target_pairs={{0,16},{1,17},{2,18},{3,19},{4,20},{5,21},{6,22},{7,23},{8,24},{9,... | collective-permute-start | bytes 1769480 | tf_op jit(solution)/shard_map/ppermute | solution.py:594
  34.9 26.0 %collective-permute-start.6 = (bf16[4,144,512]{2,1,0:T(8,128)(2,1)S(1)}, bf16[4,144,512]{2,1,0:T(8,128)(2,1)S(1)}, u32[]{:S(2)}, u32[]{:S(2)}) collective-permute-start(bf16[4,144,512]{2,1,0:T(8,128)(2,1)S(1)} %constant_dynamic-update-slice_fusion.2.refs_0_), channel_id=1, source_target_pairs={{0,8},{1,9},{2,10},{3,11},{4,12},{5,13},{6,14},{7,15},{8,0},{9,1},... | collective-permute-start | bytes 1769480 | tf_op jit(solution)/shard_map/ppermute | solution.py:594
  35.6 25.9 %collective-permute-start.16 = (bf16[4,144,512]{2,1,0:T(8,128)(2,1)S(1)}, bf16[4,144,512]{2,1,0:T(8,128)(2,1)S(1)}, u32[]{:S(2)}, u32[]{:S(2)}) collective-permute-start(bf16[4,144,512]{2,1,0:T(8,128)(2,1)S(1)} %constant_dynamic-update-slice_fusion.2.refs_0_), channel_id=1, source_target_pairs={{0,1},{1,0},{2,3},{3,2},{4,5},{5,4},{6,7},{7,6},{8,9},{9,8},{10,11... | collective-permute-start | bytes 1769480 | tf_op jit(solution)/shard_map/ppermute | solution.py:594
  60.9 2.8 %collective-permute-start.18 = (bf16[4,144,512]{2,1,0:T(8,128)(2,1)S(1)}, bf16[4,144,512]{2,1,0:T(8,128)(2,1)S(1)}, u32[]{:S(2)}, u32[]{:S(2)}) collective-permute-start(bf16[4,144,512]{2,1,0:T(8,128)(2,1)S(1)} %collective-permute-done.7.refs_2_), channel_id=1, source_target_pairs={{0,1},{1,0},{2,3},{3,2},{4,5},{5,4},{6,7},{7,6},{8,9},{9,8},{10,11... | collective-permute-start | bytes 1769480 | tf_op jit(solution)/shard_map/ppermute | solution.py:594
  61.4 3.2 %collective-permute-start.19 = (bf16[4,144,512]{2,1,0:T(8,128)(2,1)S(1)}, bf16[4,144,512]{2,1,0:T(8,128)(2,1)S(1)}, u32[]{:S(2)}, u32[]{:S(2)}) collective-permute-start(bf16[4,144,512]{2,1,0:T(8,128)(2,1)S(1)} %collective-permute-done.8.refs_3_), channel_id=1, source_target_pairs={{0,1},{1,0},{2,3},{3,2},{4,5},{5,4},{6,7},{7,6},{8,9},{9,8},{10,11... | collective-permute-start | bytes 1769480 | tf_op jit(solution)/shard_map/ppermute | solution.py:594
  91.6 6.2 %collective-permute-start.20 = (bf16[4,4,152,512]{3,2,1,0:T(8,128)(2,1)}, bf16[4,4,152,512]{3,2,1,0:T(8,128)(2,1)S(1)}, u32[]{:S(2)}, u32[]{:S(2)}) collective-permute-start(bf16[4,4,152,512]{3,2,1,0:T(8,128)(2,1)} %get-tuple-element.98), channel_id=1, source_target_pairs={{0,1},{1,0},{2,3},{3,2},{4,5},{5,4},{6,7},{7,6},{8,9},{9,8},{10,11... | collective-permute-start | bytes 7471112 | tf_op jit(solution)/shard_map/ppermute | solution.py:594
  98.4 28.2 %collective-permute-start.21 = (bf16[4,152,512]{2,1,0:T(8,128)(2,1)S(1)}, bf16[4,152,512]{2,1,0:T(8,128)(2,1)S(1)}, u32[]{:S(2)}, u32[]{:S(2)}) collective-permute-start(bf16[4,152,512]{2,1,0:T(8,128)(2,1)S(1)} %get-tuple-element.111), channel_id=1, source_target_pairs={{0,8},{1,9},{2,10},{3,11},{4,12},{5,13},{6,14},{7,15},{8,0},{9,1},... | collective-permute-start | bytes 1867784 | tf_op jit(solution)/shard_map/ppermute | solution.py:594
  99.9 29.4 %collective-permute-start.22 = (bf16[4,152,512]{2,1,0:T(8,128)(2,1)S(1)}, bf16[4,152,512]{2,1,0:T(8,128)(2,1)S(1)}, u32[]{:S(2)}, u32[]{:S(2)}) collective-permute-start(bf16[4,152,512]{2,1,0:T(8,128)(2,1)S(1)} %get-tuple-element.112), channel_id=1, source_target_pairs={{0,16},{1,17},{2,18},{3,19},{4,20},{5,21},{6,22},{7,23},{8,24},{9,... | collective-permute-start | bytes 1867784 | tf_op jit(solution)/shard_map/ppermute | solution.py:594
  100.8 28.6 %collective-permute-start.23 = (bf16[4,152,512]{2,1,0:T(8,128)(2,1)S(1)}, bf16[4,152,512]{2,1,0:T(8,128)(2,1)S(1)}, u32[]{:S(2)}, u32[]{:S(2)}) collective-permute-start(bf16[4,152,512]{2,1,0:T(8,128)(2,1)S(1)} %get-tuple-element.113), channel_id=1, source_target_pairs={{0,24},{1,25},{2,26},{3,27},{4,28},{5,29},{6,30},{7,31},{8,16},{9,... | collective-permute-start | bytes 1867784 | tf_op jit(solution)/shard_map/ppermute | solution.py:594
  132.0 8.5 %collective-permute-start.25 = (bf16[4,56,512]{2,1,0:T(8,128)(2,1)S(1)}, bf16[4,56,512]{2,1,0:T(8,128)(2,1)S(1)}, u32[]{:S(2)}, u32[]{:S(2)}) collective-permute-start(bf16[4,56,512]{2,1,0:T(8,128)(2,1)S(1)} %get-tuple-element.121), channel_id=1, source_target_pairs={{0,8},{1,9},{2,10},{3,11},{4,12},{5,13},{6,14},{7,15},{8,0},{9,1},... | collective-permute-start | bytes 688136 | tf_op jit(solution)/shard_map/ppermute | solution.py:594
  132.6 9.5 %collective-permute-start.26 = (bf16[4,56,512]{2,1,0:T(8,128)(2,1)S(1)}, bf16[4,56,512]{2,1,0:T(8,128)(2,1)S(1)}, u32[]{:S(2)}, u32[]{:S(2)}) collective-permute-start(bf16[4,56,512]{2,1,0:T(8,128)(2,1)S(1)} %get-tuple-element.122), channel_id=1, source_target_pairs={{0,16},{1,17},{2,18},{3,19},{4,20},{5,21},{6,22},{7,23},{8,24},{9,... | collective-permute-start | bytes 688136 | tf_op jit(solution)/shard_map/ppermute | solution.py:594
  134.1 10.9 %collective-permute-start.27 = (bf16[4,56,512]{2,1,0:T(8,128)(2,1)S(1)}, bf16[4,56,512]{2,1,0:T(8,128)(2,1)S(1)}, u32[]{:S(2)}, u32[]{:S(2)}) collective-permute-start(bf16[4,56,512]{2,1,0:T(8,128)(2,1)S(1)} %get-tuple-element.123), channel_id=1, source_target_pairs={{0,24},{1,25},{2,26},{3,27},{4,28},{5,29},{6,30},{7,31},{8,16},{9,... | collective-permute-start | bytes 688136 | tf_op jit(solution)/shard_map/ppermute | solution.py:594
  136.1 17.1 %collective-permute-start.29 = (bf16[1,152,512]{2,1,0:T(8,128)(2,1)S(1)}, bf16[1,152,512]{2,1,0:T(8,128)(2,1)S(1)}, u32[]{:S(2)}, u32[]{:S(2)}) collective-permute-start(bf16[1,152,512]{2,1,0:T(8,128)(2,1)S(1)} %get-tuple-element.140), channel_id=1, source_target_pairs={{0,6},{1,7},{2,4},{3,5},{4,2},{5,3},{6,0},{7,1},{8,14},{9,15},{10,... | collective-permute-start | bytes 466952 | tf_op jit(solution)/shard_map/ppermute | solution.py:594
  139.0 9.8 %collective-permute-start.30 = (bf16[1,152,512]{2,1,0:T(8,128)(2,1)S(1)}, bf16[1,152,512]{2,1,0:T(8,128)(2,1)S(1)}, u32[]{:S(2)}, u32[]{:S(2)}) collective-permute-start(bf16[1,152,512]{2,1,0:T(8,128)(2,1)S(1)} %get-tuple-element.141), channel_id=1, source_target_pairs={{0,2},{1,3},{2,0},{3,1},{4,6},{5,7},{6,4},{7,5},{8,10},{9,11},{10,... | collective-permute-start | bytes 466952 | tf_op jit(solution)/shard_map/ppermute | solution.py:594
  140.5 12.6 %collective-permute-start.28 = (bf16[1,152,512]{2,1,0:T(8,128)(2,1)S(1)}, bf16[1,152,512]{2,1,0:T(8,128)(2,1)S(1)}, u32[]{:S(2)}, u32[]{:S(2)}) collective-permute-start(bf16[1,152,512]{2,1,0:T(8,128)(2,1)S(1)} %get-tuple-element.142), channel_id=1, source_target_pairs={{0,4},{1,5},{2,6},{3,7},{4,0},{5,1},{6,2},{7,3},{8,12},{9,13},{10,... | collective-permute-start | bytes 466952 | tf_op jit(solution)/shard_map/ppermute | solution.py:594
  148.8 4.4 %collective-permute-start.31 = (bf16[1,56,512]{2,1,0:T(8,128)(2,1)S(1)}, bf16[1,56,512]{2,1,0:T(8,128)(2,1)S(1)}, u32[]{:S(2)}, u32[]{:S(2)}) collective-permute-start(bf16[1,56,512]{2,1,0:T(8,128)(2,1)S(1)} %get-tuple-element.127), channel_id=1, source_target_pairs={{0,2},{1,3},{2,0},{3,1},{4,6},{5,7},{6,4},{7,5},{8,10},{9,11},{10,... | collective-permute-start | bytes 172040 | tf_op jit(solution)/shard_map/ppermute | solution.py:594
  149.2 6.4 %collective-permute-start.32 = (bf16[1,56,512]{2,1,0:T(8,128)(2,1)S(1)}, bf16[1,56,512]{2,1,0:T(8,128)(2,1)S(1)}, u32[]{:S(2)}, u32[]{:S(2)}) collective-permute-start(bf16[1,56,512]{2,1,0:T(8,128)(2,1)S(1)} %get-tuple-element.129), channel_id=1, source_target_pairs={{0,4},{1,5},{2,6},{3,7},{4,0},{5,1},{6,2},{7,3},{8,12},{9,13},{10,... | collective-permute-start | bytes 172040 | tf_op jit(solution)/shard_map/ppermute | solution.py:594
  150.2 6.0 %collective-permute-start.33 = (bf16[1,56,512]{2,1,0:T(8,128)(2,1)S(1)}, bf16[1,56,512]{2,1,0:T(8,128)(2,1)S(1)}, u32[]{:S(2)}, u32[]{:S(2)}) collective-permute-start(bf16[1,56,512]{2,1,0:T(8,128)(2,1)S(1)} %get-tuple-element.130), channel_id=1, source_target_pairs={{0,6},{1,7},{2,4},{3,5},{4,2},{5,3},{6,0},{7,1},{8,14},{9,15},{10,... | collective-permute-start | bytes 172040 | tf_op jit(solution)/shard_map/ppermute | solution.py:594
  (9 other events, 115.3 us)

commit v2 on v1

--- a/solution.py
+++ b/solution.py
@@ -75,32 +75,35 @@
 ANYWHERE = pl.BlockSpec(memory_space=pl.ANY)
 
 
-def fetch(ids_ref, parts, others, whole, semaphores, rows):
+WHOLES = [(k, slice(None)) for k in range(4)]
+HALVES = [(0, slice(None))] + [(k, half) for k in (1, 2, 3) for half in (slice(0, 2), slice(2, 4))]
+
+
+def fetch(ids_ref, pieces, parts, others, whole, semaphores, rows):
     digit, core = ids_ref[0], ids_ref[1]
     copies = []
-    for k, (part, other) in enumerate(zip(parts, others)):
+    for m, ((k, depth), part, other) in enumerate(zip(pieces, parts, others)):
         for n, (source, which) in enumerate(((part, core), (other, 1 - core))):
             copies.append(
                 pltpu.make_async_copy(
                     source.at[:, rows],
-                    whole.at[digit ^ k, :, which, rows],
-                    semaphores.at[2 * k + n],
+                    whole.at[digit ^ k, depth, which, rows],
+                    semaphores.at[2 * m + n],
                 )
             )
     return copies
 
 
-def deliver(ids_ref, whole, kept, away, semaphores):
+def deliver(ids_ref, whole, kept, away, semaphores, group, rows):
     digit, core = ids_ref[0], ids_ref[1]
-    copies = []
-    for k in range(whole.shape[0]):
-        for n, (target, which) in enumerate(((kept, core), (away, 1 - core))):
-            copies.append(
-                pltpu.make_async_copy(
-                    whole.at[digit ^ k, :, which], target.at[k], semaphores.at[2 * k + n]
-                )
-            )
-    return copies
+    return [
+        pltpu.make_async_copy(
+            whole.at[group, :, which, rows],
+            target.at[digit ^ group, :, rows],
+            semaphores.at[2 * group + n],
+        )
+        for n, (target, which) in enumerate(((kept, core), (away, 1 - core)))
+    ]
 
 
 def pack_vectors(sums, shards, size, tail_sums, tail_size):
@@ -185,16 +188,16 @@
     )
 
 
-def attend_kernel(size, tail_size, ids_ref, lengths_ref, x_ref, *refs):
+def attend_kernel(size, tail_size, first, ids_ref, lengths_ref, x_ref, *refs):
     parts, others = refs[:4], refs[4:8]
-    q_ref, k_ref, v_ref, context_ref, table_ref, whole, hide, semaphores = refs[8:]
-    pair = pl.program_id(0)
+    q_ref, k_ref, v_ref, context_ref, table_ref, whole, hide, semaphores = refs[-8:]
+    pair = pl.program_id(0) + first
     x = x_ref[...]
     length, width = x.shape
 
-    @pl.when(pair == 0)
+    @pl.when(pair == first)
     def _():
-        copies = fetch(ids_ref, parts, others, whole, semaphores, slice(None))
+        copies = fetch(ids_ref, WHOLES, parts, others, whole, semaphores, slice(None))
         for copy in copies:
             copy.start()
         fill_mask(lengths_ref, hide)
@@ -220,38 +223,56 @@
     k_ref[...] = keys
     v_ref[...] = values
     turned = values.T
-    for number in range(length // BLOCK):
+    units = [(n, head) for n in range(length // BLOCK) for head in range(LANES // size)]
+
+    def scored(unit):
+        number, head = unit
         start, end = key_span(number)
         rows = slice(number * BLOCK, end)
-        mixed = []
-        for head in range(LANES // size):
-            chosen = one_head(queries[rows], head, size)
-            scores = nt(keys[start:end], chosen) + hide[start:end, rows]
-            weights = probabilities(scores).astype(low)
-            mixed.append(nn(turned[head * size : (head + 1) * size, start:end], weights))
-        context_ref[rows, :] = jnp.concatenate(mixed, axis=0).T.astype(low)
-
-
-def attend(ids, lengths, x, parts, others, size, tail_size):
+        return nt(keys[start:end], one_head(queries[rows], head, size)) + hide[start:end, rows]
+
+    def finish(unit, weights):
+        number, head = unit
+        start, end = key_span(number)
+        done.append(nn(turned[head * size : (head + 1) * size, start:end], weights))
+        if head == LANES // size - 1:
+            rows = slice(number * BLOCK, end)
+            context_ref[rows, :] = jnp.concatenate(done, axis=0).T.astype(low)
+            done.clear()
+
+    ahead = [scored(unit) for unit in units[:2]]
+    done, behind = [], []
+    for at, unit in enumerate(units):
+        scores = ahead.pop(0)
+        if at + 2 < len(units):
+            ahead.append(scored(units[at + 2]))
+        behind.append((unit, probabilities(scores).astype(low)))
+        if at > 0:
+            finish(*behind.pop(0))
+    finish(*behind.pop())
+
+
+def attend(ids, lengths, x, parts, others, size, tail_size, first, count, given=()):
     length, width = x.shape
-    out = pl.BlockSpec((length, LANES), lambda p: (0, p))
+    out = pl.BlockSpec((length, LANES), lambda p: (0, p + first))
     chips, rows, _ = parts[0].shape
     return call(
-        functools.partial(attend_kernel, size, tail_size),
+        functools.partial(attend_kernel, size, tail_size, first),
         "attend",
-        23,
+        4 * count,
         26,
-        grid=(width // LANES,),
-        in_specs=[SCALARS, SCALARS, fixed(x.shape)] + [ANYWHERE] * 8,
+        grid=(count,),
+        in_specs=[SCALARS, SCALARS, fixed(x.shape)] + [ANYWHERE] * (8 + len(given)),
         out_specs=[out] * 4 + [fixed((3 * VECTORS, width))],
         out_shape=[jax.ShapeDtypeStruct((length, width), low)] * 4
         + [jax.ShapeDtypeStruct((3 * VECTORS, width), wide)],
+        input_output_aliases={11 + n: n for n in range(len(given))},
         scratch_shapes=[
             pltpu.VMEM((4, chips, 2, rows, width), low),
             pltpu.VMEM((length, length), wide),
             pltpu.SemaphoreType.DMA((8,)),
         ],
-    )(ids, lengths, x, *parts, *others)
+    )(ids, lengths, x, *parts, *others, *given)
 
 
 def pair_back(size, queries, keys, values, incoming, hide, dq_ref, key_total, value_total):
@@ -259,22 +280,43 @@
     turned = keys.T
     key_total[...] = jnp.zeros_like(key_total)
     value_total[...] = jnp.zeros_like(value_total)
-    for number in range(length // BLOCK):
+    units = [(n, head) for n in range(length // BLOCK) for head in range(LANES // size)]
+
+    def prepared(unit):
+        number, head = unit
         start, end = key_span(number)
         rows = slice(number * BLOCK, end)
-        parts = []
-        for head in range(LANES // size):
-            chosen = one_head(queries[rows], head, size)
-            arriving = one_head(incoming[rows], head, size)
-            scores = nt(keys[start:end], chosen) + hide[start:end, rows]
-            attention = probabilities(scores)
-            weight_grad = nt(values[start:end], arriving)
-            balance = jnp.sum(attention * weight_grad, axis=0, keepdims=True)
-            score_grad = (attention * (weight_grad - balance)).astype(low)
-            key_total[start:end, :] += nn(score_grad, chosen)
-            value_total[start:end, :] += nn(attention.astype(low), arriving)
-            parts.append(nn(turned[head * size : (head + 1) * size, start:end], score_grad))
-        dq_ref[rows, :] = (jnp.concatenate(parts, axis=0).T * (1.0 / math.sqrt(size))).astype(low)
+        chosen = one_head(queries[rows], head, size)
+        arriving = one_head(incoming[rows], head, size)
+        scores = nt(keys[start:end], chosen) + hide[start:end, rows]
+        return chosen, arriving, scores, nt(values[start:end], arriving)
+
+    def finish(unit, chosen, arriving, attention, score_grad):
+        number, head = unit
+        start, end = key_span(number)
+        value_total[start:end, :] += nn(attention, arriving)
+        key_total[start:end, :] += nn(score_grad, chosen)
+        parts.append(nn(turned[head * size : (head + 1) * size, start:end], score_grad))
+        if head == LANES // size - 1:
+            rows = slice(number * BLOCK, end)
+            dq_ref[rows, :] = (
+                jnp.concatenate(parts, axis=0).T * (1.0 / math.sqrt(size))
+            ).astype(low)
+            parts.clear()
+
+    ahead = [prepared(units[0])]
+    parts, behind = [], []
+    for at, unit in enumerate(units):
+        chosen, arriving, scores, weight_grad = ahead.pop(0)
+        if at + 1 < len(units):
+            ahead.append(prepared(units[at + 1]))
+        attention = probabilities(scores)
+        balance = jnp.sum(attention * weight_grad, axis=0, keepdims=True)
+        score_grad = (attention * (weight_grad - balance)).astype(low)
+        behind.append((unit, chosen, arriving, attention.astype(low), score_grad))
+        if at > 0:
+            finish(*behind.pop(0))
+    finish(*behind.pop())
 
 
 def first_back_kernel(size, lengths_ref, *refs):
@@ -302,103 +344,139 @@
     )(lengths, queries, keys, values, incoming)
 
 
-def rest_back_kernel(size, ids_ref, lengths_ref, *refs):
-    given, first, (x_ref, back_ref) = refs[:4], refs[4:7], refs[7:9]
-    parts, others = refs[9:13], refs[13:17]
-    grad_x_ref, kept_ref, away_ref = refs[17:20]
-    dq_part, key_total, value_total, hide, grads, whole, full, semaphores = refs[20:]
+def rest_back_kernel(size, lengths_ref, *refs):
+    given, first, grads_ref = refs[:4], refs[4:7], refs[7]
+    dq_part, key_total, value_total, hide = refs[8:]
     step = pl.program_id(0)
-    width = x_ref.shape[1]
-    copies = fetch(ids_ref, parts, others, whole, semaphores.at[0], slice(None))
 
     @pl.when(step == 0)
     def _():
-        for copy in copies:
-            copy.start()
         fill_mask(lengths_ref, hide)
         for n in range(3):
-            grads[n, :, :LANES] = first[n][...]
+            grads_ref[n, :, :LANES] = first[n][...]
 
     pair_back(size, *[ref[...] for ref in given], hide, dq_part, key_total, value_total)
     here = pl.ds(pl.multiple_of((step + 1) * LANES, LANES), LANES)
-    grads[0, :, here] = dq_part[...]
-    grads[1, :, here] = key_total[...].astype(low)
-    grads[2, :, here] = value_total[...].astype(low)
-
-    @pl.when(step == pl.num_programs(0) - 1)
-    def _():
-        split = full.shape[:3]
-        chips = split[1]
-        sums = []
-        for n in range(3):
-            grad = tn(x_ref[...], grads[n]).astype(low)
-            full[:, :, :, n * SHARD : (n + 1) * SHARD, :] = grad.reshape(split + (SHARD, width))
-            if n != 1:
-                sums.append(column_sum(grads[n]))
-        sums = jnp.concatenate(sums + [jnp.zeros((VECTORS - 2, width), wide)], axis=0)
-        lines = slice(3 * SHARD, 3 * SHARD + VECTORS)
-        full[:, :, :, lines, :] = jnp.zeros(split + (VECTORS, width), low)
-        for j, tile in enumerate(pack_vectors(sums, width // SHARD, SHARD, None, 0)):
-            full[j // (2 * chips), j // 2 % chips, j % 2, lines, :LANES] = tile.astype(low)
-        leaving = deliver(ids_ref, full, kept_ref, away_ref, semaphores.at[1])
-        for copy in leaving:
-            copy.start()
-        for copy in copies:
-            copy.wait()
-        total = back_ref[...]
-        for n in range(3):
-            weight = whole[:, :, :, n * SHARD : (n + 1) * SHARD, :].reshape(width, width)
-            total = total + nt(grads[n], weight)
-        grad_x_ref[...] = total
-        for copy in leaving:
-            copy.wait()
-
-
-def rest_back(ids, lengths, queries, keys, values, incoming, first, x, back, parts, others, size):
-    length, width = x.shape
-    chips, rows, _ = parts[0].shape
+    grads_ref[0, :, here] = dq_part[...]
+    grads_ref[1, :, here] = key_total[...].astype(low)
+    grads_ref[2, :, here] = value_total[...].astype(low)
+
+
+def rest_back(lengths, queries, keys, values, incoming, first, size):
+    length, width = queries.shape
     block = pl.BlockSpec((length, LANES), lambda p: (0, p + 1))
-    packed = jax.ShapeDtypeStruct((4, chips, rows, width), low)
     return call(
         functools.partial(rest_back_kernel, size),
         "rest_back",
-        26,
-        36,
+        14,
+        28,
         grid=(width // LANES - 1,),
-        in_specs=[SCALARS] * 2
-        + [block] * 4
-        + [fixed((length, LANES))] * 3
-        + [fixed(x.shape), fixed(back.shape)]
-        + [ANYWHERE] * 8,
-        out_specs=[fixed(back.shape)] + [ANYWHERE] * 2,
-        out_shape=[jax.ShapeDtypeStruct(back.shape, wide)] + [packed] * 2,
+        in_specs=[SCALARS] + [block] * 4 + [fixed((length, LANES))] * 3,
+        out_specs=fixed((3, length, width)),
+        out_shape=jax.ShapeDtypeStruct((3, length, width), low),
         scratch_shapes=[
             pltpu.VMEM((length, LANES), low),
             pltpu.VMEM((length, LANES), wide),
             pltpu.VMEM((length, LANES), wide),
             pltpu.VMEM((length, length), wide),
-            pltpu.VMEM((3, length, width), low),
+        ],
+    )(lengths, queries, keys, values, incoming, *first)
+
+
+def project_back_kernel(tail_size, ids_ref, grads_ref, x_ref, back_ref, sums_ref, *refs):
+    parts, others, refs = refs[:4], refs[4:8], refs[8:]
+    grad_x_ref, kept_ref, away_ref, bias_sums, whole, full, semaphores = refs
+    step = pl.program_id(0)
+    width = x_ref.shape[1]
+    split = full.shape[:3]
+    chips = split[1]
+    copies = fetch(ids_ref, WHOLES, parts, others, whole, semaphores.at[0], slice(None))
+
+    @pl.when(step == 0)
+    def _():
+        for copy in copies:
+            copy.start()
+        grad_x_ref[...] = back_ref[...]
+        bias_sums[...] = jnp.zeros_like(bias_sums)
+
+    grads = grads_ref[0]
+    here = pl.ds(pl.multiple_of(step * SHARD, SHARD), SHARD)
+    full[:, :, :, here, :] = tn(x_ref[...], grads).astype(low).reshape(split + (SHARD, width))
+    bias_sums[pl.ds(step, 1), :] = jnp.where(step == 1, sums_ref[5:6], column_sum(grads))
+
+    @pl.when(step == 0)
+    def _():
+        for copy in copies:
+            copy.wait()
+
+    leaving = []
+    for group in range(split[0]):
+        leaving += deliver(
+            ids_ref, full, kept_ref, away_ref, semaphores.at[1], group, slice(None)
+        )
+
+    @pl.when(step == pl.num_programs(0) - 1)
+    def _():
+        lines = slice(3 * SHARD, 3 * SHARD + VECTORS)
+        full[:, :, :, lines, :] = jnp.zeros(split + (VECTORS, width), low)
+        shards = width // SHARD
+        places = pack_vectors(
+            sums_ref[:VECTORS], shards, SHARD, sums_ref[VECTORS:], tail_size
+        ), pack_vectors(bias_sums[...], shards, SHARD, None, 0)
+        for n, tiles in enumerate(places):
+            for j, tile in enumerate(tiles):
+                full[
+                    j // (2 * chips), j // 2 % chips, j % 2, lines, n * LANES : (n + 1) * LANES
+                ] = tile.astype(low)
+        for copy in leaving:
+            copy.start()
+
+    weight = whole[:, :, :, here, :].reshape(width, width)
+    grad_x_ref[...] += nt(grads, weight)
+
+    @pl.when(step == pl.num_programs(0) - 1)
+    def _():
+        for copy in leaving:
+            copy.wait()
+
+
+def project_back(ids, grads, x, back, sums, parts, others, tail):
+    length, width = x.shape
+    chips, rows, _ = parts[0].shape
+    packed = jax.ShapeDtypeStruct((4, chips, rows, width), low)
+    return call(
+        functools.partial(project_back_kernel, tail),
+        "project_back",
+        7,
+        24,
+        grid=(3,),
+        in_specs=[SCALARS, pl.BlockSpec((1, length, width), lambda p: (p, 0, 0))]
+        + [fixed(x.shape), fixed(back.shape), fixed(sums.shape)]
+        + [ANYWHERE] * 8,
+        out_specs=[fixed(back.shape)] + [ANYWHERE] * 2,
+        out_shape=[jax.ShapeDtypeStruct(back.shape, wide)] + [packed] * 2,
+        scratch_shapes=[
+            pltpu.VMEM((VECTORS, width), wide),
             pltpu.VMEM((4, chips, 2, rows, width), low),
             pltpu.VMEM((4, chips, 2, rows, width), low),
             pltpu.SemaphoreType.DMA((2, 8)),
         ],
-    )(ids, lengths, queries, keys, values, incoming, *first, x, back, *parts, *others)
+    )(ids, grads, x, back, sums, *parts, *others)
 
 
 def middle_kernel(ids_ref, x_ref, y_ref, cotangent_ref, context_ref, table_ref, *refs):
-    parts, others = refs[:4], refs[4:8]
-    out_ref, grad_y_ref, back_ref, context_grad_ref, kept_ref, away_ref = refs[8:14]
-    whole, full, hidden_all, hidden_grad_all, first_all, feed_grad_all = refs[14:20]
-    slopes, output_total, sums_total, semaphores = refs[20:]
+    parts, others, refs = refs[:7], refs[7:14], refs[14:]
+    out_ref, grad_y_ref, back_ref, context_grad_ref, sums_ref, kept_ref, away_ref = refs[:7]
+    whole, full, hidden_all, hidden_grad_all, first_all, feed_grad_all = refs[7:13]
+    slopes, output_total, sums_total, semaphores, send_semaphores = refs[13:]
     step = pl.program_id(0)
     rows, width = x_ref.shape
     inner = hidden_all.shape[1]
     columns = inner // width
-    chips = whole.shape[1]
     share = SHARD * columns
-    sections = [slice(2 * share, 2 * share + SHARD), slice(share, 2 * share), slice(0, share)]
+    sections = [slice(2 * share, 2 * share + SHARD), slice(0, 2 * share)]
     copies = [
-        fetch(ids_ref, parts, others, whole, semaphores.at[n], section)
+        fetch(ids_ref, HALVES, parts, others, whole, semaphores.at[n], section)
         for n, section in enumerate(sections)
     ]
 
@@ -422,8 +500,7 @@
         return whole[:, :, :, start : start + SHARD, :].reshape(width, width)
 
     def down(c):
-        shards = whole.shape[0] // columns
-        return whole[c * shards : (c + 1) * shards, :, :, :share, :].reshape(width, width)
+        return whole[c, :, :, :share, :].reshape(width, width)
 
     def line(number):
         return table_ref[number : number + 1, :]
@@ -438,10 +515,14 @@
     first_all[here, :] = first_low
     feed = jnp.zeros((rows, width), wide)
     arrive(1)
-    arrive(2)
+
+    def before_of(c):
+        return nn(first_low, up(c)) + line(BIAS_UP + c)
+
+    ahead = before_of(0)
     for c in range(columns):
         units = slice(c * width, (c + 1) * width)
-        before = nn(first_low, up(c)) + line(BIAS_UP + c)
+        before, ahead = ahead, before_of(c + 1) if c + 1 < columns else None
         half = 0.5 * (1.0 + lax.erf(before * 0.7071067811865476))
         hidden = (before * half).astype(low)
         slopes[:, units] = half + before * jnp.exp(-0.5 * before * before) * 0.3989422804014327
@@ -464,9 +545,11 @@
     feed_grad_all[here, :] = feed_grad
     first_grad = second_back
     up_bias = []
+    ahead = nt(feed_grad, down(0))
     for c in range(columns):
         units = slice(c * width, (c + 1) * width)
-        hidden_grad = (nt(feed_grad, down(c)) * slopes[:, units]).astype(low)
+        product, ahead = ahead, nt(feed_grad, down(c + 1)) if c + 1 < columns else None
+        hidden_grad = (product * slopes[:, units]).astype(low)
         hidden_grad_all[here, units] = hidden_grad
         up_bias.append(column_sum(hidden_grad))
         first_grad = first_grad + nt(hidden_grad, up(c))
@@ -504,30 +587,34 @@
     @pl.when(step == pl.num_programs(0) - 1)
     def _():
         split = whole.shape[:3]
-        shards = width // SHARD
+        groups = split[0]
+        leaving = []
+
+        def send(n, group, rows):
+            for copy in deliver(
+                ids_ref, full, kept_ref, away_ref, send_semaphores.at[n], group, rows
+            ):
+                copy.start()
+                leaving.append(copy)
+
+        sums_ref[...] = sums_total[...]
+        full[:, :, :, sections[0], :] = (
+            output_total[...].astype(low).reshape(split + (SHARD, width))
+        )
+        for group in range(groups):
+            send(0, group, sections[0])
+        for c in range(columns):
+            units = slice(c * width, (c + 1) * width)
+            part = tn(first_all[...], hidden_grad_all[:, units]).astype(low)
+            rows = slice(share + c * SHARD, share + (c + 1) * SHARD)
+            full[:, :, :, rows, :] = part.reshape(split + (SHARD, width))
+            for group in range(groups):
+                send(1 + c, group, rows)
         for c in range(columns):
             units = slice(c * width, (c + 1) * width)
             part = tn(hidden_all[:, units], feed_grad_all[...]).astype(low)
-            per = split[0] // columns
-            full[c * per : (c + 1) * per, :, :, :share, :] = part.reshape(
-                (per,) + split[1:] + (share, width)
-            )
-            part = tn(first_all[...], hidden_grad_all[:, units]).astype(low)
-            start = share + c * SHARD
-            full[:, :, :, start : start + SHARD, :] = part.reshape(split + (SHARD, width))
-        full[:, :, :, sections[0], :] = (
-            output_total[...].astype(low).reshape(split + (SHARD, width))
-        )
-        lines = slice(2 * share + SHARD, 2 * share + SHARD + VECTORS)
-        full[:, :, :, lines, :] = jnp.zeros(split + (VECTORS, width), low)
-        tiles = pack_vectors(
-            sums_total[:VECTORS], shards, SHARD, sums_total[VECTORS:], share
-        )
-        for j, tile in enumerate(tiles):
-            full[j // (2 * chips), j // 2 % chips, j % 2, lines, :LANES] = tile.astype(low)
-        leaving = deliver(ids_ref, full, kept_ref, away_ref, semaphores.at[0])
-        for copy in leaving:
-            copy.start()
+            full[c, :, :, :share, :] = part.reshape(split[1:] + (share, width))
+            send(1 + columns, c, slice(0, share))
         for copy in leaving:
             copy.wait()
 
@@ -536,22 +623,24 @@
     length, width = x.shape
     block = pl.BlockSpec((TILE, width), lambda p: (p, 0))
     chips, rows, _ = parts[0].shape
-    packed = jax.ShapeDtypeStruct((4, chips, rows + VECTORS, width), low)
+    packed = jax.ShapeDtypeStruct((4, chips, rows, width), low)
+    columns = inner // width
     return call(
         middle_kernel,
         "middle",
         29,
         44,
         grid=(length // TILE,),
-        in_specs=[SCALARS] + [block] * 4 + [fixed(table.shape)] + [ANYWHERE] * 8,
-        out_specs=[block] * 4 + [ANYWHERE] * 2,
+        in_specs=[SCALARS] + [block] * 4 + [fixed(table.shape)] + [ANYWHERE] * 14,
+        out_specs=[block] * 4 + [fixed((2 * VECTORS, width))] + [ANYWHERE] * 2,
         out_shape=[
             jax.ShapeDtypeStruct((length, width), kind) for kind in (low, wide, wide, low)
         ]
+        + [jax.ShapeDtypeStruct((2 * VECTORS, width), wide)]
         + [packed] * 2,
         scratch_shapes=[
             pltpu.VMEM((4, chips, 2, rows, width), low),
-            pltpu.VMEM((4, chips, 2, rows + VECTORS, width), low),
+            pltpu.VMEM((4, chips, 2, rows, width), low),
             pltpu.VMEM((length, inner), low),
             pltpu.VMEM((length, inner), low),
             pltpu.VMEM((length, width), low),
@@ -559,7 +648,8 @@
             pltpu.VMEM((TILE, inner), wide),
             pltpu.VMEM((width, width), wide),
             pltpu.VMEM((2 * VECTORS, width), wide),
-            pltpu.SemaphoreType.DMA((3, 8)),
+            pltpu.SemaphoreType.DMA((2, 14)),
+            pltpu.SemaphoreType.DMA((columns + 2, 8)),
         ],
     )(ids, x, y, cotangent, context, table, *parts, *others)
 
@@ -602,11 +692,12 @@
     def send(self, block, shift, radix):
         return [self.swap(block, k << shift) for k in range(1, radix)]
 
-    def place(self, block, received, shift, radix):
+    def place(self, block, received, shift, radix, axis=0):
         digit = self.digit(shift, radix)
-        whole = jnp.zeros((radix,) + block.shape, block.dtype)
+        shape = block.shape[:axis] + (radix,) + block.shape[axis:]
+        whole = jnp.zeros(shape, block.dtype)
         for k, part in enumerate([block] + received):
-            whole = lax.dynamic_update_index_in_dim(whole, part, digit ^ k, 0)
+            whole = lax.dynamic_update_index_in_dim(whole, part, digit ^ k, axis)
         return whole.reshape((-1,) + block.shape[1:])
 
     def spread(self, block, digits):
@@ -647,6 +738,31 @@
     whole = jnp.concatenate(pieces, axis=1)
     whole = whole.reshape((4, whole.shape[0] // 8, 2) + whole.shape[1:])
     return [whole[k, :, 0] for k in range(4)], [whole[k, :, 1] for k in range(4)]
+
+
+def pack_kernel(query, key, value, vectors, output, up, down, early_ref, late_ref):
+    rows, width = query.shape
+    share = down.shape[0]
+    for n, array in enumerate((query, key, value)):
+        early_ref[n * rows : (n + 1) * rows] = array[...]
+    early_ref[3 * rows :] = vectors[...]
+    late_ref[:share] = down[...]
+    late_ref[2 * share :] = output[...]
+    for c in range(share // rows):
+        start = share + c * rows
+        late_ref[start : start + rows] = up[:, c * width : (c + 1) * width]
+
+
+def pack(query, key, value, vectors, output, up, down):
+    rows, width = query.shape
+    shapes = [(3 * rows + VECTORS, width), (2 * down.shape[0] + rows, width)]
+    return call(
+        pack_kernel,
+        "pack",
+        1,
+        60,
+        out_shape=[jax.ShapeDtypeStruct(shape, low) for shape in shapes],
+    )(query, key, value, vectors, output, up, down)
 
 
 def body(
@@ -680,7 +796,7 @@
     inner = count * down_weight.shape[0]
     share = inner // count
     columns = inner // width
-    direct = rows == SHARD and len(links.far) == 1
+    direct = rows == SHARD and (links.near, links.far) == ([(1, 4)], [(3, 4)])
     tail = inner // (width // SHARD)
 
     vectors = [
@@ -707,24 +823,33 @@
             for row, lane, line in places + [(0, 2 * LANES, last)]
         )
 
-    early = jnp.concatenate(
-        [query_weight, key_weight, value_weight, pack_lines(vectors, up_bias)], axis=0
-    )[None]
-    early, *local = lax.optimization_barrier((early, down_weight, up_weight, output_weight))
-    late = jnp.concatenate(
-        [local[0]] + [local[1][:, c * width : (c + 1) * width] for c in range(columns)] + [local[2]],
-        axis=0,
-    )[None]
-    late = links.spread(late, links.near[:-1])
-    shift, radix = links.near[-1]
-    received = [links.swap(late, k << shift) for k in range(2, radix)]
-    early = links.spread(early, links.near)
-    gated, early = lax.optimization_barrier((late, early))
-    received = [links.swap(gated, 1 << shift)] + received
+    packed = pack_lines(vectors, up_bias)
+    if direct:
+        early, late = pack(
+            query_weight, key_weight, value_weight, packed, output_weight, up_weight, down_weight
+        )
+    else:
+        early = jnp.concatenate([query_weight, key_weight, value_weight, packed], axis=0)
+        ups = [up_weight[:, c * width : (c + 1) * width] for c in range(columns)]
+        late = jnp.concatenate([down_weight] + ups + [output_weight], axis=0)
+    early, late = early[None], late[None]
+    if direct:
+        shift = links.near[0][0]
+        late = links.spread(late, [(shift + 1, 2)])
+        early = links.spread(early, links.near)
+    else:
+        late = links.spread(late, links.near[:-1])
+        received = links.send(late, *links.near[-1])
+        early = links.spread(early, links.near)
     early = links.spread(early, links.far[:-1])
     arriving = links.send(early, *links.far[-1])
-    received, early = lax.optimization_barrier((received, early))
-    late = links.place(late, received, *links.near[-1])
+    if direct:
+        late, arriving[0] = lax.optimization_barrier((late, arriving[0]))
+        received = links.send(late, shift, 2)
+        late = links.place(late, received, shift, 2, axis=1)
+    else:
+        received, early = lax.optimization_barrier((received, early))
+        late = links.place(late, received, *links.near[-1])
     late = links.spread(late, links.far[:-1])
     if direct:
         ids = jnp.stack([links.digit(*links.far[-1]), links.flat() & 1])
@@ -743,26 +868,46 @@
         ]
         last = small[:, 0, 2 * LANES :][:, :share].reshape(-1, tail)
         early_parts, early_others = resplit(squares + [pack_lines(lines, last)])
-    received = links.send(late, *links.far[-1])
-    queries, keys, values, context, table = attend(
-        ids, doc_lengths, stream_x, early_parts, early_others, size, tail
+    attending = functools.partial(
+        attend, ids, doc_lengths, stream_x, early_parts, early_others, size, tail
     )
-    received, context = lax.optimization_barrier((received, context))
+    pairs = width // LANES
     if direct:
-        late_parts = [late] + received
+        across, along = 1 << links.far[0][0], 2 << links.far[0][0]
+        halves = late[:2], late[2:]
+        received = {
+            (1, 0): links.swap(halves[0], across),
+            (2, 1): links.swap(halves[1], along),
+            (2, 0): links.swap(halves[0], along),
+            (1, 1): links.swap(halves[1], across),
+        }
+        *attended, table = attending(0, pairs - 1)
+        received, attended = lax.optimization_barrier((received, attended))
+        received[3, 0] = links.swap(received[1, 0], along)
+        received[3, 1] = links.swap(received[2, 1], across)
+        *attended, _ = attending(pairs - 1, 1, attended)
+        received, attended = lax.optimization_barrier((received, attended))
+        late_parts = [late] + [received[k, half] for k in (1, 2, 3) for half in (0, 1)]
         late_others = [links.swap(part, 1) for part in late_parts]
     else:
+        received = links.send(late, *links.far[-1])
+        *attended, table = attending(0, pairs)
+        received, attended = lax.optimization_barrier((received, attended))
         late = links.pair(links.place(late, received, *links.far[-1]))
         up = late[:, share : 2 * share].reshape(count, columns, rows, width).swapaxes(0, 1)
         up = up.reshape(columns, -1, SHARD, width).swapaxes(0, 1)
-        late_parts, late_others = resplit(
-            [
-                late[:, :share].reshape(-1, tail, width),
-                up.reshape(-1, tail, width),
-                late[:, 2 * share :].reshape(-1, SHARD, width),
-            ]
-        )
-    block_out, grad_y, back, context_grad, kept, away = middle(
+        late_parts, late_others = [
+            [side[0]] + [part[n : n + 2] for part in side[1:] for n in (0, 2)]
+            for side in resplit(
+                [
+                    late[:, :share].reshape(-1, tail, width),
+                    up.reshape(-1, tail, width),
+                    late[:, 2 * share :].reshape(-1, SHARD, width),
+                ]
+            )
+        ]
+    queries, keys, values, context = attended
+    block_out, grad_y, back, context_grad, sums, kept, away = middle(
         ids, stream_x, stream_y, cotangent, context, table, late_parts, late_others, inner
     )
 
@@ -770,8 +915,11 @@
         both = jnp.stack([kept, away], axis=2)
         return both.reshape((-1,) + both.shape[3:]).astype(wide)
 
-    def real_lines(packed, lines, last):
-        found = [packed[:, n, :SHARD].reshape(count, rows) for n in range(lines)]
+    def real_lines(packed):
+        found = [
+            packed[:, n % VECTORS, n // VECTORS * LANES :][:, :SHARD].reshape(count, rows)
+            for n in range(VECTORS + 3)
+        ]
         return pack_lines(found, packed[:, VECTORS - 1, :tail].reshape(count, share))
 
     def first_sums(kept, arriving):
@@ -786,7 +934,6 @@
                 full[:, :tail].reshape(count, share, width),
                 up.reshape(count, share, width),
                 full[:, 2 * tail : 2 * tail + SHARD].reshape(count, rows, width),
-                real_lines(full[:, 2 * tail + SHARD :], VECTORS - 1, True),
             ],
             axis=1,
         )
@@ -794,27 +941,35 @@
     arriving = links.swap(away, 1)
     first = first_back(doc_lengths, queries, keys, values, context_grad, size)
     arriving, first = lax.optimization_barrier((arriving, first))
+    going = functools.partial(
+        rest_back, doc_lengths, queries, keys, values, first=first, size=size
+    )
     if direct:
-        total, *leaving = first_sums(kept, arriving)
-        leaving = [part.astype(low) for part in leaving]
+        part = first_sums(kept, arriving)
+        leaving = [
+            jnp.stack([part[1][:2], part[3][:2]]).astype(low),
+            jnp.stack([part[2][2:], part[3][2:]]).astype(low),
+        ]
+        staying = part[0], part[2][:2], part[1][2:]
+        leaving, staying, context_grad = lax.optimization_barrier((leaving, staying, context_grad))
+        arriving = [links.swap(leaving[0], across), links.swap(leaving[1], along)]
+        grads = going(incoming=context_grad)
+        arriving, grads = lax.optimization_barrier((arriving, grads))
+        leaving = [
+            (staying[n + 1] + arriving[n][1].astype(wide)).astype(low) for n in (0, 1)
+        ]
+        total = [staying[0][:2], staying[0][2:]]
+        total = [total[n] + arriving[n][0].astype(wide) for n in (0, 1)]
+        leaving, total, grads = lax.optimization_barrier((leaving, total, grads))
+        arriving = [links.swap(leaving[0], along), links.swap(leaving[1], across)]
     else:
         total = links.collect(kept.astype(wide) + arriving.astype(wide), links.far[1:])
         total, leaving = links.cut(total, *links.far[0])
-    leaving, context_grad = lax.optimization_barrier((leaving, context_grad))
-    arriving = links.receive(leaving, links.far[0][0])
-    grad_x, kept, away = rest_back(
-        ids,
-        doc_lengths,
-        queries,
-        keys,
-        values,
-        context_grad,
-        first,
-        stream_x,
-        back,
-        early_parts,
-        early_others,
-        size,
+        leaving, context_grad = lax.optimization_barrier((leaving, context_grad))
+        arriving = links.receive(leaving, links.far[0][0])
+        grads = going(incoming=context_grad)
+    grad_x, kept, away = project_back(
+        ids, grads, stream_x, back, sums, early_parts, early_others, tail
     )
     if not direct:
         full = restore(kept, away)
@@ -823,7 +978,7 @@
                 full[:, n * SHARD : (n + 1) * SHARD].reshape(count, rows, width)
                 for n in range(3)
             ]
-            + [real_lines(full[:, 3 * SHARD :], 2, False)],
+            + [real_lines(full[:, 3 * SHARD :])],
             axis=1,
         )
         away, kept = links.halve(full)
@@ -837,8 +992,11 @@
         mine, leaving = links.cut(mine, *links.far[0])
     arriving, leaving = lax.optimization_barrier((arriving, leaving))
     crossing = links.receive(leaving, links.far[0][0])
-    for part in arriving:
-        total = total + part.astype(wide)
+    if direct:
+        total = jnp.concatenate([total[n] + arriving[n].astype(wide) for n in (0, 1)])
+    else:
+        for part in arriving:
+            total = total + part.astype(wide)
     for part in crossing:
         mine = mine + part.astype(wide)
     total = links.collect(total, links.near[1:])
@@ -851,21 +1009,21 @@
     crossing = links.receive(leaving, shift)
     arriving, crossing[0] = lax.optimization_barrier((arriving[1:], crossing[0]))
     total = (total + sum(part.astype(wide) for part in [early_part] + arriving))[0]
-    mine = (mine + sum(part.astype(wide) for part in crossing))[0]
-
-    if direct:
-        at = 2 * share + rows
-        singles = [total[at + n, :rows] for n in range(VECTORS - 1)]
-        up_bias_share = total[at + VECTORS - 1, :share]
-        pair = mine[3 * rows, :rows], mine[3 * rows + 1, :rows]
-    else:
-        at = 2 * share + rows
-        singles = [total[at + n, :rows] for n in range(VECTORS - 1)]
-        up_bias_share = total[at, 2 * LANES : 2 * LANES + share]
-        pair = mine[3 * rows, :rows], mine[3 * rows + 1, :rows]
+    at = 2 * share + rows
     up_share = jnp.concatenate(
         [total[share + c * rows : share + (c + 1) * rows] for c in range(columns)], axis=1
     )
+    settled = [total[:share], up_share, total[2 * share : at]]
+    settled, crossing[1:] = lax.optimization_barrier((settled, crossing[1:]))
+    mine = (mine + sum(part.astype(wide) for part in crossing))[0]
+
+    lines = mine[3 * rows :]
+    singles = [lines[n, :rows] for n in range(VECTORS - 1)]
+    pair = lines[0, LANES : LANES + rows], lines[2, LANES : LANES + rows]
+    if direct:
+        up_bias_share = lines[VECTORS - 1, :share]
+    else:
+        up_bias_share = lines[0, 2 * LANES : 2 * LANES + share]
     return (
         block_out,
         grad_x,
@@ -875,18 +1033,18 @@
         mine[rows : 2 * rows],
         mine[2 * rows : 3 * rows],
         pair[1],
-        total[2 * share : at],
+        settled[2],
         singles[0],
         singles[1],
         singles[2],
-        up_share,
+        settled[1],
         up_bias_share,
-        total[:share],
+        settled[0],
         singles[3],
         singles[4],
         singles[5],
         singles[6],
-        singles[5],
+        lines[1, LANES : LANES + rows],
     )
 
 

time: 159 us -> 150 us (0.943)
  starting transfers between devices: 34.4 us -> 46.8 us
  Pallas kernels: 79.8 us -> 68.6 us
  waiting for transfers between devices: 31.1 us -> 23.7 us
  local copies, waits for them, and re-layouts: 8.74 us -> 5.23 us
    ppermute x34 -> x40, starting transfers between devices: 34.4 us -> 46.8 us  [swap(): lax.ppermute(values, AXES, [(i, i ^ distance) for i in range(self.count)])]
    pallas_call x2 -> x5, Pallas kernels: 46.8 us -> 38.5 us  [the longest x2 15.6 us: attend(): call(functools.partial(attend_kernel, size, tail_size, first), 'attend',...]
    ppermute x34 -> x40, waiting for transfers between devices: 31.1 us -> 23.7 us  [swap(): lax.ppermute(values, AXES, [(i, i ^ distance) for i in range(self.count)])]
    unnamed x20 -> x12, local copies, waits for them, and re-layouts: 4.26 us -> 0.03 us
    dynamic_update_slice x8, local copies, waits for them, and re-layouts: 0.11 us -> 1.85 us  [place(): whole = lax.dynamic_update_index_in_dim(whole, part, digit ^ k, axis)]
  transfers between devices with their start and end apart: 34 -> 40, of which waited for: 13 -> 13; matrix products, arithmetic and copies ran while one was open for 5% -> 3% of each run, Pallas kernels for 33% -> 28%
where the time goes in v2:
time: 150 us
  Pallas kernels  68.6 us (46%)
  starting transfers between devices  46.8 us (31%)
  waiting for transfers between devices  23.7 us (16%)
  local copies, waits for them, and re-layouts  5.23 us (3%)
  other arithmetic  4.13 us (3%)
    ppermute x40, starting transfers between devices, swap(): lax.ppermute(values, AXES, [(i, i ^ distance) for i in range(self.count)])  46.8 us
    pallas_call x1, Pallas kernels, middle(): call(middle_kernel, 'middle', 29, 44, grid=(length // TILE,), in_specs=[S...  25.5 us
    ppermute x40, waiting for transfers between devices, swap(): lax.ppermute(values, AXES, [(i, i ^ distance) for i in range(self.count)])  23.7 us
    pallas_call x2, Pallas kernels, attend(): call(functools.partial(attend_kernel, size, tail_size, first), 'attend',...  15.6 us
    pallas_call x1, Pallas kernels, rest_back(): call(functools.partial(rest_back_kernel, size), 'rest_back', 14, 28, grid...  13.2 us
    pallas_call x1, Pallas kernels, project_back(): call(functools.partial(project_back_kernel, tail), 'project_back', 7, 24,...  8.02 us
    pallas_call x1, Pallas kernels, first_back(): call(functools.partial(first_back_kernel, size), 'first_back', 6, 16, gri...  4.53 us
  transfers between devices with their start and end apart: 40, of which 13 were waited for; matrix products, arithmetic and copies ran while one was open for 3% of the time, Pallas kernels for 28%

profile of v2, /device:TPU:0, one launch (start us, length us, event | category | flops | bytes accessed | tf_op | source)
XLA Modules:
  0.0 149.5 jit_solution(6198944076690726761)
XLA Ops:
  0.7 1.4 pad_add_fusion.vectors
  2.1 1.6 %pack.1 = (bf16[56,512]{1,0:T(8,128)(2,1)}, bf16[144,512]{1,0:T(8,128)(2,1)}) custom-call(bf16[16,512]{1,0:T(8,128)(2,1)} %query.1, bf16[16,512]{1,0:T(8,128)(2,1)} %key.1, bf16[16,512]{1,0:T(8,128)(2,1)} %value.1, bf16[8,512]{1,0:T(8,128)(2,1)} %pad_add_fusion.vectors, bf16[16,512]{1,0:T(8,128)(2,1)} %output.1, bf16[16,2048]{1,0:T(8,128)(2,1)} %up.1, ...), custom_call_target="tpu_custom_call" | custom-call | flops 250000000 | bytes 1024 | tf_op jit(solution)/shard_map/pack/pallas_call | solution.py:759
  3.7 4.0 %collective-permute-start.2 = (bf16[1,56,512]{2,1,0:T(8,128)(2,1)}, bf16[1,56,512]{2,1,0:T(8,128)(2,1)S(1)}, u32[]{:S(2)}, u32[]{:S(2)}) collective-permute-start(bf16[1,56,512]{2,1,0:T(8,128)(2,1)} %bitcast.103), channel_id=1, source_target_pairs={{0,4},{1,5},{2,6},{3,7},{4,0},{5,1},{6,2},{7,3},{8,12},{9,13},{10,... | collective-permute-start | bytes 172040 | tf_op jit(solution)/shard_map/ppermute | solution.py:684
  7.7 1.6 %collective-permute-start.1 = (bf16[1,56,512]{2,1,0:T(8,128)(2,1)}, bf16[1,56,512]{2,1,0:T(8,128)(2,1)S(1)}, u32[]{:S(2)}, u32[]{:S(2)}) collective-permute-start(bf16[1,56,512]{2,1,0:T(8,128)(2,1)} %bitcast.104), channel_id=1, source_target_pairs={{0,2},{1,3},{2,0},{3,1},{4,6},{5,7},{6,4},{7,5},{8,10},{9,11},{10,... | collective-permute-start | bytes 172040 | tf_op jit(solution)/shard_map/ppermute | solution.py:684
  9.3 1.9 %collective-permute-start = (bf16[1,144,512]{2,1,0:T(8,128)(2,1)}, bf16[1,144,512]{2,1,0:T(8,128)(2,1)S(1)}, u32[]{:S(2)}, u32[]{:S(2)}) collective-permute-start(bf16[1,144,512]{2,1,0:T(8,128)(2,1)} %bitcast.102), channel_id=1, source_target_pairs={{0,4},{1,5},{2,6},{3,7},{4,0},{5,1},{6,2},{7,3},{8,12},{9,13},{10,... | collective-permute-start | bytes 442376 | tf_op jit(solution)/shard_map/ppermute | solution.py:684
  12.2 3.9 %collective-permute-done.3 = bf16[1,56,512]{2,1,0:T(8,128)(2,1)S(1)} collective-permute-done((bf16[1,56,512]{2,1,0:T(8,128)(2,1)}, bf16[1,56,512]{2,1,0:T(8,128)(2,1)S(1)}, u32[]{:S(2)}, u32[]{:S(2)}) %collective-permute-start.3) | collective-permute-done | bytes 57376 | tf_op jit(solution)/shard_map/ppermute | solution.py:684
  16.1 2.5 %collective-permute-start.11 = (bf16[4,56,512]{2,1,0:T(8,128)(2,1)S(1)}, bf16[4,56,512]{2,1,0:T(8,128)(2,1)S(1)}, u32[]{:S(2)}, u32[]{:S(2)}) collective-permute-start(bf16[4,56,512]{2,1,0:T(8,128)(2,1)S(1)} %constant_dynamic-update-slice_fusion.refs_0_), channel_id=1, source_target_pairs={{0,24},{1,25},{2,26},{3,27},{4,28},{5,29},{6,30},{7,31},{8,16},{9,... | collective-permute-start | bytes 688136 | tf_op jit(solution)/shard_map/ppermute | solution.py:684
  20.7 6.6 %collective-permute-done.4.refs_1_ = bf16[4,56,512]{2,1,0:T(8,128)(2,1)S(1)} collective-permute-done((bf16[4,56,512]{2,1,0:T(8,128)(2,1)S(1)}, bf16[4,56,512]{2,1,0:T(8,128)(2,1)S(1)}, u32[]{:S(2)}, u32[]{:S(2)}) %collective-permute-start.4) | collective-permute-done | bytes 229408 | tf_op jit(solution)/shard_map/ppermute | solution.py:684
  27.2 1.4 collective-permute-start.5
  29.8 4.2 %collective-permute-done.5 = bf16[2,144,512]{2,1,0:T(8,128)(2,1)S(1)} collective-permute-done((bf16[2,144,512]{2,1,0:T(8,128)(2,1)S(1)}, bf16[2,144,512]{2,1,0:T(8,128)(2,1)S(1)}, u32[]{:S(2)}, u32[]{:S(2)}) %collective-permute-start.5) | collective-permute-done | bytes 294944 | tf_op jit(solution)/shard_map/ppermute | solution.py:684
  34.6 1.5 %collective-permute-start.7 = (bf16[2,144,512]{2,1,0:T(8,128)(2,1)S(1)}, bf16[2,144,512]{2,1,0:T(8,128)(2,1)S(1)}, u32[]{:S(2)}, u32[]{:S(2)}) collective-permute-start(bf16[2,144,512]{2,1,0:T(8,128)(2,1)S(1)} %get-tuple-element.202), channel_id=1, source_target_pairs={{0,8},{1,9},{2,10},{3,11},{4,12},{5,13},{6,14},{7,15},{8,0},{9,1},... | collective-permute-start | bytes 884744 | tf_op jit(solution)/shard_map/ppermute | solution.py:684
  36.1 1.5 %collective-permute-start.8 = (bf16[2,144,512]{2,1,0:T(8,128)(2,1)S(1)}, bf16[2,144,512]{2,1,0:T(8,128)(2,1)S(1)}, u32[]{:S(2)}, u32[]{:S(2)}) collective-permute-start(bf16[2,144,512]{2,1,0:T(8,128)(2,1)S(1)} %get-tuple-element.203), channel_id=1, source_target_pairs={{0,16},{1,17},{2,18},{3,19},{4,20},{5,21},{6,22},{7,23},{8,24},{9,... | collective-permute-start | bytes 884744 | tf_op jit(solution)/shard_map/ppermute | solution.py:684
  38.2 10.5 %attend.2 = (bf16[1024,512]{1,0:T(8,128)(2,1)S(1)}, bf16[1024,512]{1,0:T(8,128)(2,1)S(1)}, bf16[1024,512]{1,0:T(8,128)(2,1)S(1)}, bf16[1024,512]{1,0:T(8,128)(2,1)S(1)}, f32[24,512]{1,0:T(8,128)S(1)}) custom-call(s32[2]{0:T(128)S(1)} %pad_add_fusion.1.ids_ref, s32[1,16]{1,0:T(1,128)S(1)} %copy-done.2, bf16[1024,512]{1,0:T(8,128)(2,1)S(1)} %copy-done, ...), custom_call_target="tpu_custom_call" | custom-call | flops 3000000000 | bytes 1024 | tf_op jit(solution)/shard_map/attend/pallas_call | solution.py:259
  49.3 1.5 %collective-permute-start.17 = (bf16[2,144,512]{2,1,0:T(8,128)(2,1)S(1)}, bf16[2,144,512]{2,1,0:T(8,128)(2,1)S(1)}, u32[]{:S(2)}, u32[]{:S(2)}) collective-permute-start(bf16[2,144,512]{2,1,0:T(8,128)(2,1)S(1)} %collective-permute-done.9.refs_4_), channel_id=1, source_target_pairs={{0,8},{1,9},{2,10},{3,11},{4,12},{5,13},{6,14},{7,15},{8,0},{9,1},... | collective-permute-start | bytes 884744 | tf_op jit(solution)/shard_map/ppermute | solution.py:684
  50.9 5.1 %attend.3 = (bf16[1024,512]{1,0:T(8,128)(2,1)S(1)}, bf16[1024,512]{1,0:T(8,128)(2,1)S(1)}, bf16[1024,512]{1,0:T(8,128)(2,1)S(1)}, bf16[1024,512]{1,0:T(8,128)(2,1)S(1)}, f32[24,512]{1,0:T(8,128)}) custom-call(s32[2]{0:T(128)S(1)} %pad_add_fusion.1.ids_ref, ...), custom_call_target="tpu_custom_call", output_to_operand_aliasing={{0}: (11, {}), {1}: (12, {}), {2}: (13, {}), {3}: (14, {})} | custom-call | flops 1000000000 | bytes 1024 | tf_op jit(solution)/shard_map/attend/pallas_call | solution.py:259
  59.9 25.5 %middle.1 = (bf16[1024,512]{1,0:T(8,128)(2,1)}, f32[1024,512]{1,0:T(8,128)}, f32[1024,512]{1,0:T(8,128)}, bf16[1024,512]{1,0:T(8,128)(2,1)S(1)}, f32[16,512]{1,0...) custom-call(s32[2]{0:T(128)S(1)} %pad_add_fusion.1.ids_ref, ...), custom_call_target="tpu_custom_call" | custom-call | flops 7249999872 | bytes 1024 | tf_op jit(solution)/shard_map/middle/pallas_call | solution.py:628
  85.9 4.5 %first_back.1 = (bf16[1024,128]{1,0:T(8,128)(2,1)S(1)}, bf16[1024,128]{1,0:T(8,128)(2,1)S(1)}, bf16[1024,128]{1,0:T(8,128)(2,1)S(1)}) custom-call(s32[1,16]{1,0:T(1,128)S(1)} %copy-done.2, bf16[1024,512]{1,0:T(8,128)(2,1)S(1)} %get-tuple-element.134.refs_0_, bf16[1024,512]{1,0:T(8,128)(2,1)S(1)} %get-tuple-element.135.refs_1_, ...), custom_call_target="tpu_custom_call" | custom-call | flops 1500000000 | bytes 1024 | tf_op jit(solution)/shard_map/first_back/pallas_call | solution.py:333
  91.5 1.3 collective-permute-start.26
  92.8 1.5 %collective-permute-start.27 = (bf16[2,2,144,512]{3,2,1,0:T(8,128)(2,1)S(1)}, bf16[2,2,144,512]{3,2,1,0:T(8,128)(2,1)S(1)}, u32[]{:S(2)}, u32[]{:S(2)}) collective-permute-start(bf16[2,2,144,512]{3,2,1,0:T(8,128)(2,1)S(1)} %get-tuple-element.144), channel_id=1, source_target_pairs={{0,16},{1,17},{2,18},{3,19},{4,20},{5,21},{6,22},{7,23},{8,24},{9,... | collective-permute-start | bytes 1769480 | tf_op jit(solution)/shard_map/ppermute | solution.py:684
  94.3 13.2 %rest_back.1.grads_ref = bf16[3,1024,512]{2,1,0:T(8,128)(2,1)S(1)} custom-call(s32[1,16]{1,0:T(1,128)S(1)} %copy-done.2, bf16[1024,512]{1,0:T(8,128)(2,1)S(1)} %get-tuple-element.134.refs_0_, bf16[1024,512]{1,0:T(8,128)(2,1)S(1)} %get-tuple-element.135.refs_1_, bf16[1024,512]{1,0:T(8,128)(2,1)S(1)} %get-tuple-element.136.refs_2_, ...), custom_call_target="tpu_custom_call" | custom-call | flops 3500000000 | bytes 1024 | tf_op jit(solution)/shard_map/rest_back/pallas_call | solution.py:368
  108.5 1.6 %collective-permute-start.28 = (bf16[2,144,512]{2,1,0:T(8,128)(2,1)S(1)}, bf16[2,144,512]{2,1,0:T(8,128)(2,1)S(1)}, u32[]{:S(2)}, u32[]{:S(2)}) collective-permute-start(bf16[2,144,512]{2,1,0:T(8,128)(2,1)S(1)} %get-tuple-element.159), channel_id=1, source_target_pairs={{0,16},{1,17},{2,18},{3,19},{4,20},{5,21},{6,22},{7,23},{8,24},{9,... | collective-permute-start | bytes 884744 | tf_op jit(solution)/shard_map/ppermute | solution.py:684
  110.7 8.0 %project_back.1 = (f32[1024,512]{1,0:T(8,128)}, bf16[4,4,56,512]{3,2,1,0:T(8,128)(2,1)S(1)}, bf16[4,4,56,512]{3,2,1,0:T(8,128)(2,1)S(1)}) custom-call(s32[2]{0:T(128)S(1)} %pad_add_fusion.1.ids_ref, bf16[3,1024,512]{2,1,0:T(8,128)(2,1)S(1)} %rest_back.1.grads_ref, bf16[1024,512]{1,0:T(8,128)(2,1)S(1)} %copy-done, f32[1024,512]{1,0:T(8,128)S(1)} %copy-done.1, ...), custom_call_target="tpu_custom_call" | custom-call | flops 1750000000 | bytes 1024 | tf_op jit(solution)/shard_map/project_back/pallas_call | solution.py:447
  118.9 2.5 %collective-permute-done.30 = bf16[4,4,56,512]{3,2,1,0:T(8,128)(2,1)S(1)} collective-permute-done((bf16[4,4,56,512]{3,2,1,0:T(8,128)(2,1)S(1)}, bf16[4,4,56,512]{3,2,1,0:T(8,128)(2,1)S(1)}, u32[]{:S(2)}, u32[]{:S(2)}) %collective-permute-start.30) | collective-permute-done | bytes 917536 | tf_op jit(solution)/shard_map/ppermute | solution.py:684
  121.5 1.4 collective-permute-start.31
  123.5 1.6 %collective-permute-start.33 = (bf16[4,56,512]{2,1,0:T(8,128)(2,1)S(1)}, bf16[4,56,512]{2,1,0:T(8,128)(2,1)S(1)}, u32[]{:S(2)}, u32[]{:S(2)}) collective-permute-start(bf16[4,56,512]{2,1,0:T(8,128)(2,1)S(1)} %get-tuple-element.169), channel_id=1, source_target_pairs={{0,24},{1,25},{2,26},{3,27},{4,28},{5,29},{6,30},{7,31},{8,16},{9,... | collective-permute-start | bytes 688136 | tf_op jit(solution)/shard_map/ppermute | solution.py:684
  125.4 1.5 collective-permute-start.36
  126.9 4.0 %collective-permute-start.34 = (bf16[1,144,512]{2,1,0:T(8,128)(2,1)S(1)}, bf16[1,144,512]{2,1,0:T(8,128)(2,1)S(1)}, u32[]{:S(2)}, u32[]{:S(2)}) collective-permute-start(bf16[1,144,512]{2,1,0:T(8,128)(2,1)S(1)} %get-tuple-element.194), channel_id=1, source_target_pairs={{0,4},{1,5},{2,6},{3,7},{4,0},{5,1},{6,2},{7,3},{8,12},{9,13},{10,... | collective-permute-start | bytes 442376 | tf_op jit(solution)/shard_map/ppermute | solution.py:684
  130.9 4.0 %collective-permute-start.35 = (bf16[1,144,512]{2,1,0:T(8,128)(2,1)S(1)}, bf16[1,144,512]{2,1,0:T(8,128)(2,1)S(1)}, u32[]{:S(2)}, u32[]{:S(2)}) collective-permute-start(bf16[1,144,512]{2,1,0:T(8,128)(2,1)S(1)} %get-tuple-element.195), channel_id=1, source_target_pairs={{0,6},{1,7},{2,4},{3,5},{4,2},{5,3},{6,0},{7,1},{8,14},{9,15},{10,... | collective-permute-start | bytes 442376 | tf_op jit(solution)/shard_map/ppermute | solution.py:684
  135.4 1.5 collective-permute-start.37
  136.9 4.0 %collective-permute-start.38 = (bf16[1,56,512]{2,1,0:T(8,128)(2,1)S(1)}, bf16[1,56,512]{2,1,0:T(8,128)(2,1)S(1)}, u32[]{:S(2)}, u32[]{:S(2)}) collective-permute-start(bf16[1,56,512]{2,1,0:T(8,128)(2,1)S(1)} %get-tuple-element.179), channel_id=1, source_target_pairs={{0,4},{1,5},{2,6},{3,7},{4,0},{5,1},{6,2},{7,3},{8,12},{9,13},{10,... | collective-permute-start | bytes 172040 | tf_op jit(solution)/shard_map/ppermute | solution.py:684
  140.9 1.2 collective-permute-start.39
  144.2 3.6 %collective-permute-done.38 = bf16[1,56,512]{2,1,0:T(8,128)(2,1)S(1)} collective-permute-done((bf16[1,56,512]{2,1,0:T(8,128)(2,1)S(1)}, bf16[1,56,512]{2,1,0:T(8,128)(2,1)S(1)}, u32[]{:S(2)}, u32[]{:S(2)}) %collective-permute-start.38) | collective-permute-done | bytes 57376 | tf_op jit(solution)/shard_map/ppermute | solution.py:684
  (103 shorter events, 18.2 us)
Async XLA Ops:
  3.7 8.4 %collective-permute-start.2 = (bf16[1,56,512]{2,1,0:T(8,128)(2,1)}, bf16[1,56,512]{2,1,0:T(8,128)(2,1)S(1)}, u32[]{:S(2)}, u32[]{:S(2)}) collective-permute-start(bf16[1,56,512]{2,1,0:T(8,128)(2,1)} %bitcast.103), channel_id=1, source_target_pairs={{0,4},{1,5},{2,6},{3,7},{4,0},{5,1},{6,2},{7,3},{8,12},{9,13},{10,... | collective-permute-start | bytes 172040 | tf_op jit(solution)/shard_map/ppermute | solution.py:684
  9.3 6.8 %collective-permute-start.3 = (bf16[1,56,512]{2,1,0:T(8,128)(2,1)}, bf16[1,56,512]{2,1,0:T(8,128)(2,1)S(1)}, u32[]{:S(2)}, u32[]{:S(2)}) collective-permute-start(bf16[1,56,512]{2,1,0:T(8,128)(2,1)} %bitcast.105), channel_id=1, source_target_pairs={{0,6},{1,7},{2,4},{3,5},{4,2},{5,3},{6,0},{7,1},{8,14},{9,15},{10,... | collective-permute-start | bytes 172040 | tf_op jit(solution)/shard_map/ppermute | solution.py:684
  9.3 11.3 %collective-permute-start = (bf16[1,144,512]{2,1,0:T(8,128)(2,1)}, bf16[1,144,512]{2,1,0:T(8,128)(2,1)S(1)}, u32[]{:S(2)}, u32[]{:S(2)}) collective-permute-start(bf16[1,144,512]{2,1,0:T(8,128)(2,1)} %bitcast.102), channel_id=1, source_target_pairs={{0,4},{1,5},{2,6},{3,7},{4,0},{5,1},{6,2},{7,3},{8,12},{9,13},{10,... | collective-permute-start | bytes 442376 | tf_op jit(solution)/shard_map/ppermute | solution.py:684
  16.1 13.1 %collective-permute-start.11 = (bf16[4,56,512]{2,1,0:T(8,128)(2,1)S(1)}, bf16[4,56,512]{2,1,0:T(8,128)(2,1)S(1)}, u32[]{:S(2)}, u32[]{:S(2)}) collective-permute-start(bf16[4,56,512]{2,1,0:T(8,128)(2,1)S(1)} %constant_dynamic-update-slice_fusion.refs_0_), channel_id=1, source_target_pairs={{0,24},{1,25},{2,26},{3,27},{4,28},{5,29},{6,30},{7,31},{8,16},{9,... | collective-permute-start | bytes 688136 | tf_op jit(solution)/shard_map/ppermute | solution.py:684
  18.6 10.6 %collective-permute-start.10 = (bf16[4,56,512]{2,1,0:T(8,128)(2,1)S(1)}, bf16[4,56,512]{2,1,0:T(8,128)(2,1)S(1)}, u32[]{:S(2)}, u32[]{:S(2)}) collective-permute-start(bf16[4,56,512]{2,1,0:T(8,128)(2,1)S(1)} %constant_dynamic-update-slice_fusion.refs_0_), channel_id=1, source_target_pairs={{0,16},{1,17},{2,18},{3,19},{4,20},{5,21},{6,22},{7,23},{8,24},{9,... | collective-permute-start | bytes 688136 | tf_op jit(solution)/shard_map/ppermute | solution.py:684
  19.1 8.1 %collective-permute-start.4 = (bf16[4,56,512]{2,1,0:T(8,128)(2,1)S(1)}, bf16[4,56,512]{2,1,0:T(8,128)(2,1)S(1)}, u32[]{:S(2)}, u32[]{:S(2)}) collective-permute-start(bf16[4,56,512]{2,1,0:T(8,128)(2,1)S(1)} %constant_dynamic-update-slice_fusion.refs_0_), channel_id=1, source_target_pairs={{0,8},{1,9},{2,10},{3,11},{4,12},{5,13},{6,14},{7,15},{8,0},{9,1},... | collective-permute-start | bytes 688136 | tf_op jit(solution)/shard_map/ppermute | solution.py:684
  27.2 6.7 %collective-permute-start.5 = (bf16[2,144,512]{2,1,0:T(8,128)(2,1)S(1)}, bf16[2,144,512]{2,1,0:T(8,128)(2,1)S(1)}, u32[]{:S(2)}, u32[]{:S(2)}) collective-permute-start(bf16[2,144,512]{2,1,0:T(8,128)(2,1)S(1)} %constant_dynamic-update-slice_fusion.4), channel_id=1, source_target_pairs={{0,2},{1,3},{2,0},{3,1},{4,6},{5,7},{6,4},{7,5},{8,10},{9,11},{10,... | collective-permute-start | bytes 884744 | tf_op jit(solution)/shard_map/ppermute | solution.py:684
  28.7 5.9 %collective-permute-start.12 = (bf16[4,56,512]{2,1,0:T(8,128)(2,1)S(1)}, bf16[4,56,512]{2,1,0:T(8,128)(2,1)S(1)}, u32[]{:S(2)}, u32[]{:S(2)}) collective-permute-start(bf16[4,56,512]{2,1,0:T(8,128)(2,1)S(1)} %constant_dynamic-update-slice_fusion.refs_0_), channel_id=1, source_target_pairs={{0,1},{1,0},{2,3},{3,2},{4,5},{5,4},{6,7},{7,6},{8,9},{9,8},{10,11... | collective-permute-start | bytes 688136 | tf_op jit(solution)/shard_map/ppermute | solution.py:684
  28.7 9.6 %collective-permute-start.13 = (bf16[4,56,512]{2,1,0:T(8,128)(2,1)S(1)}, bf16[4,56,512]{2,1,0:T(8,128)(2,1)S(1)}, u32[]{:S(2)}, u32[]{:S(2)}) collective-permute-start(bf16[4,56,512]{2,1,0:T(8,128)(2,1)S(1)} %collective-permute-done.4.refs_1_), channel_id=1, source_target_pairs={{0,1},{1,0},{2,3},{3,2},{4,5},{5,4},{6,7},{7,6},{8,9},{9,8},{10,11... | collective-permute-start | bytes 688136 | tf_op jit(solution)/shard_map/ppermute | solution.py:684
  29.2 6.9 %collective-permute-start.15 = (bf16[4,56,512]{2,1,0:T(8,128)(2,1)S(1)}, bf16[4,56,512]{2,1,0:T(8,128)(2,1)S(1)}, u32[]{:S(2)}, u32[]{:S(2)}) collective-permute-start(bf16[4,56,512]{2,1,0:T(8,128)(2,1)S(1)} %collective-permute-done.11.refs_3_), channel_id=1, source_target_pairs={{0,1},{1,0},{2,3},{3,2},{4,5},{5,4},{6,7},{7,6},{8,9},{9,8},{10,11... | collective-permute-start | bytes 688136 | tf_op jit(solution)/shard_map/ppermute | solution.py:684
  29.2 8.4 %collective-permute-start.14 = (bf16[4,56,512]{2,1,0:T(8,128)(2,1)S(1)}, bf16[4,56,512]{2,1,0:T(8,128)(2,1)S(1)}, u32[]{:S(2)}, u32[]{:S(2)}) collective-permute-start(bf16[4,56,512]{2,1,0:T(8,128)(2,1)S(1)} %collective-permute-done.10.refs_2_), channel_id=1, source_target_pairs={{0,1},{1,0},{2,3},{3,2},{4,5},{5,4},{6,7},{7,6},{8,9},{9,8},{10,11... | collective-permute-start | bytes 688136 | tf_op jit(solution)/shard_map/ppermute | solution.py:684
  34.0 14.7 %collective-permute-start.9 = (bf16[2,144,512]{2,1,0:T(8,128)(2,1)S(1)}, bf16[2,144,512]{2,1,0:T(8,128)(2,1)S(1)}, u32[]{:S(2)}, u32[]{:S(2)}) collective-permute-start(bf16[2,144,512]{2,1,0:T(8,128)(2,1)S(1)} %get-tuple-element.202), channel_id=1, source_target_pairs={{0,16},{1,17},{2,18},{3,19},{4,20},{5,21},{6,22},{7,23},{8,24},{9,... | collective-permute-start | bytes 884744 | tf_op jit(solution)/shard_map/ppermute | solution.py:684
  34.6 14.2 %collective-permute-start.7 = (bf16[2,144,512]{2,1,0:T(8,128)(2,1)S(1)}, bf16[2,144,512]{2,1,0:T(8,128)(2,1)S(1)}, u32[]{:S(2)}, u32[]{:S(2)}) collective-permute-start(bf16[2,144,512]{2,1,0:T(8,128)(2,1)S(1)} %get-tuple-element.202), channel_id=1, source_target_pairs={{0,8},{1,9},{2,10},{3,11},{4,12},{5,13},{6,14},{7,15},{8,0},{9,1},... | collective-permute-start | bytes 884744 | tf_op jit(solution)/shard_map/ppermute | solution.py:684
  36.1 12.7 %collective-permute-start.8 = (bf16[2,144,512]{2,1,0:T(8,128)(2,1)S(1)}, bf16[2,144,512]{2,1,0:T(8,128)(2,1)S(1)}, u32[]{:S(2)}, u32[]{:S(2)}) collective-permute-start(bf16[2,144,512]{2,1,0:T(8,128)(2,1)S(1)} %get-tuple-element.203), channel_id=1, source_target_pairs={{0,16},{1,17},{2,18},{3,19},{4,20},{5,21},{6,22},{7,23},{8,24},{9,... | collective-permute-start | bytes 884744 | tf_op jit(solution)/shard_map/ppermute | solution.py:684
  37.6 11.2 %collective-permute-start.6 = (bf16[2,144,512]{2,1,0:T(8,128)(2,1)S(1)}, bf16[2,144,512]{2,1,0:T(8,128)(2,1)S(1)}, u32[]{:S(2)}, u32[]{:S(2)}) collective-permute-start(bf16[2,144,512]{2,1,0:T(8,128)(2,1)S(1)} %get-tuple-element.203), channel_id=1, source_target_pairs={{0,8},{1,9},{2,10},{3,11},{4,12},{5,13},{6,14},{7,15},{8,0},{9,1},... | collective-permute-start | bytes 884744 | tf_op jit(solution)/shard_map/ppermute | solution.py:684
  48.8 7.2 %collective-permute-start.16 = (bf16[2,144,512]{2,1,0:T(8,128)(2,1)S(1)}, bf16[2,144,512]{2,1,0:T(8,128)(2,1)S(1)}, u32[]{:S(2)}, u32[]{:S(2)}) collective-permute-start(bf16[2,144,512]{2,1,0:T(8,128)(2,1)S(1)} %collective-permute-done.6.refs_1_), channel_id=1, source_target_pairs={{0,16},{1,17},{2,18},{3,19},{4,20},{5,21},{6,22},{7,23},{8,24},{9,... | collective-permute-start | bytes 884744 | tf_op jit(solution)/shard_map/ppermute | solution.py:684
  49.3 6.7 %collective-permute-start.17 = (bf16[2,144,512]{2,1,0:T(8,128)(2,1)S(1)}, bf16[2,144,512]{2,1,0:T(8,128)(2,1)S(1)}, u32[]{:S(2)}, u32[]{:S(2)}) collective-permute-start(bf16[2,144,512]{2,1,0:T(8,128)(2,1)S(1)} %collective-permute-done.9.refs_4_), channel_id=1, source_target_pairs={{0,8},{1,9},{2,10},{3,11},{4,12},{5,13},{6,14},{7,15},{8,0},{9,1},... | collective-permute-start | bytes 884744 | tf_op jit(solution)/shard_map/ppermute | solution.py:684
  50.9 6.3 %collective-permute-start.18 = (bf16[4,144,512]{2,1,0:T(8,128)(2,1)S(1)}, bf16[4,144,512]{2,1,0:T(8,128)(2,1)S(1)}, u32[]{:S(2)}, u32[]{:S(2)}) collective-permute-start(bf16[4,144,512]{2,1,0:T(8,128)(2,1)S(1)} %bitcast.100), channel_id=1, source_target_pairs={{0,1},{1,0},{2,3},{3,2},{4,5},{5,4},{6,7},{7,6},{8,9},{9,8},{10,11... | collective-permute-start | bytes 1769480 | tf_op jit(solution)/shard_map/ppermute | solution.py:684
  85.4 5.0 %collective-permute-start.25 = (bf16[4,4,144,512]{3,2,1,0:T(8,128)(2,1)}, bf16[4,4,144,512]{3,2,1,0:T(8,128)(2,1)S(1)}, u32[]{:S(2)}, u32[]{:S(2)}) collective-permute-start(bf16[4,4,144,512]{3,2,1,0:T(8,128)(2,1)} %get-tuple-element.133), channel_id=1, source_target_pairs={{0,1},{1,0},{2,3},{3,2},{4,5},{5,4},{6,7},{7,6},{8,9},{9,8},{10,11... | collective-permute-start | bytes 7077896 | tf_op jit(solution)/shard_map/ppermute | solution.py:684
  91.5 16.1 %collective-permute-start.26 = (bf16[2,2,144,512]{3,2,1,0:T(8,128)(2,1)S(1)}, bf16[2,2,144,512]{3,2,1,0:T(8,128)(2,1)S(1)}, u32[]{:S(2)}, u32[]{:S(2)}) collective-permute-start(bf16[2,2,144,512]{3,2,1,0:T(8,128)(2,1)S(1)} %get-tuple-element.143), channel_id=1, source_target_pairs={{0,8},{1,9},{2,10},{3,11},{4,12},{5,13},{6,14},{7,15},{8,0},{9,1},... | collective-permute-start | bytes 1769480 | tf_op jit(solution)/shard_map/ppermute | solution.py:684
  92.8 15.3 %collective-permute-start.27 = (bf16[2,2,144,512]{3,2,1,0:T(8,128)(2,1)S(1)}, bf16[2,2,144,512]{3,2,1,0:T(8,128)(2,1)S(1)}, u32[]{:S(2)}, u32[]{:S(2)}) collective-permute-start(bf16[2,2,144,512]{3,2,1,0:T(8,128)(2,1)S(1)} %get-tuple-element.144), channel_id=1, source_target_pairs={{0,16},{1,17},{2,18},{3,19},{4,20},{5,21},{6,22},{7,23},{8,24},{9,... | collective-permute-start | bytes 1769480 | tf_op jit(solution)/shard_map/ppermute | solution.py:684
  108.5 10.3 %collective-permute-start.28 = (bf16[2,144,512]{2,1,0:T(8,128)(2,1)S(1)}, bf16[2,144,512]{2,1,0:T(8,128)(2,1)S(1)}, u32[]{:S(2)}, u32[]{:S(2)}) collective-permute-start(bf16[2,144,512]{2,1,0:T(8,128)(2,1)S(1)} %get-tuple-element.159), channel_id=1, source_target_pairs={{0,16},{1,17},{2,18},{3,19},{4,20},{5,21},{6,22},{7,23},{8,24},{9,... | collective-permute-start | bytes 884744 | tf_op jit(solution)/shard_map/ppermute | solution.py:684
  110.1 8.7 %collective-permute-start.29 = (bf16[2,144,512]{2,1,0:T(8,128)(2,1)S(1)}, bf16[2,144,512]{2,1,0:T(8,128)(2,1)S(1)}, u32[]{:S(2)}, u32[]{:S(2)}) collective-permute-start(bf16[2,144,512]{2,1,0:T(8,128)(2,1)S(1)} %get-tuple-element.160), channel_id=1, source_target_pairs={{0,8},{1,9},{2,10},{3,11},{4,12},{5,13},{6,14},{7,15},{8,0},{9,1},... | collective-permute-start | bytes 884744 | tf_op jit(solution)/shard_map/ppermute | solution.py:684
  121.5 9.4 %collective-permute-start.31 = (bf16[4,56,512]{2,1,0:T(8,128)(2,1)S(1)}, bf16[4,56,512]{2,1,0:T(8,128)(2,1)S(1)}, u32[]{:S(2)}, u32[]{:S(2)}) collective-permute-start(bf16[4,56,512]{2,1,0:T(8,128)(2,1)S(1)} %get-tuple-element.167), channel_id=1, source_target_pairs={{0,8},{1,9},{2,10},{3,11},{4,12},{5,13},{6,14},{7,15},{8,0},{9,1},... | collective-permute-start | bytes 688136 | tf_op jit(solution)/shard_map/ppermute | solution.py:684
  123.0 12.3 %collective-permute-start.32 = (bf16[4,56,512]{2,1,0:T(8,128)(2,1)S(1)}, bf16[4,56,512]{2,1,0:T(8,128)(2,1)S(1)}, u32[]{:S(2)}, u32[]{:S(2)}) collective-permute-start(bf16[4,56,512]{2,1,0:T(8,128)(2,1)S(1)} %get-tuple-element.168), channel_id=1, source_target_pairs={{0,16},{1,17},{2,18},{3,19},{4,20},{5,21},{6,22},{7,23},{8,24},{9,... | collective-permute-start | bytes 688136 | tf_op jit(solution)/shard_map/ppermute | solution.py:684
  123.5 11.8 %collective-permute-start.33 = (bf16[4,56,512]{2,1,0:T(8,128)(2,1)S(1)}, bf16[4,56,512]{2,1,0:T(8,128)(2,1)S(1)}, u32[]{:S(2)}, u32[]{:S(2)}) collective-permute-start(bf16[4,56,512]{2,1,0:T(8,128)(2,1)S(1)} %get-tuple-element.169), channel_id=1, source_target_pairs={{0,24},{1,25},{2,26},{3,27},{4,28},{5,29},{6,30},{7,31},{8,16},{9,... | collective-permute-start | bytes 688136 | tf_op jit(solution)/shard_map/ppermute | solution.py:684
  125.4 10.0 %collective-permute-start.36 = (bf16[1,144,512]{2,1,0:T(8,128)(2,1)S(1)}, bf16[1,144,512]{2,1,0:T(8,128)(2,1)S(1)}, u32[]{:S(2)}, u32[]{:S(2)}) collective-permute-start(bf16[1,144,512]{2,1,0:T(8,128)(2,1)S(1)} %get-tuple-element.193), channel_id=1, source_target_pairs={{0,2},{1,3},{2,0},{3,1},{4,6},{5,7},{6,4},{7,5},{8,10},{9,11},{10,... | collective-permute-start | bytes 442376 | tf_op jit(solution)/shard_map/ppermute | solution.py:684
  126.9 15.2 %collective-permute-start.34 = (bf16[1,144,512]{2,1,0:T(8,128)(2,1)S(1)}, bf16[1,144,512]{2,1,0:T(8,128)(2,1)S(1)}, u32[]{:S(2)}, u32[]{:S(2)}) collective-permute-start(bf16[1,144,512]{2,1,0:T(8,128)(2,1)S(1)} %get-tuple-element.194), channel_id=1, source_target_pairs={{0,4},{1,5},{2,6},{3,7},{4,0},{5,1},{6,2},{7,3},{8,12},{9,13},{10,... | collective-permute-start | bytes 442376 | tf_op jit(solution)/shard_map/ppermute | solution.py:684
  130.9 11.2 %collective-permute-start.35 = (bf16[1,144,512]{2,1,0:T(8,128)(2,1)S(1)}, bf16[1,144,512]{2,1,0:T(8,128)(2,1)S(1)}, u32[]{:S(2)}, u32[]{:S(2)}) collective-permute-start(bf16[1,144,512]{2,1,0:T(8,128)(2,1)S(1)} %get-tuple-element.195), channel_id=1, source_target_pairs={{0,6},{1,7},{2,4},{3,5},{4,2},{5,3},{6,0},{7,1},{8,14},{9,15},{10,... | collective-permute-start | bytes 442376 | tf_op jit(solution)/shard_map/ppermute | solution.py:684
  135.4 6.7 %collective-permute-start.37 = (bf16[1,56,512]{2,1,0:T(8,128)(2,1)S(1)}, bf16[1,56,512]{2,1,0:T(8,128)(2,1)S(1)}, u32[]{:S(2)}, u32[]{:S(2)}) collective-permute-start(bf16[1,56,512]{2,1,0:T(8,128)(2,1)S(1)} %get-tuple-element.174), channel_id=1, source_target_pairs={{0,2},{1,3},{2,0},{3,1},{4,6},{5,7},{6,4},{7,5},{8,10},{9,11},{10,... | collective-permute-start | bytes 172040 | tf_op jit(solution)/shard_map/ppermute | solution.py:684
  136.9 10.9 %collective-permute-start.38 = (bf16[1,56,512]{2,1,0:T(8,128)(2,1)S(1)}, bf16[1,56,512]{2,1,0:T(8,128)(2,1)S(1)}, u32[]{:S(2)}, u32[]{:S(2)}) collective-permute-start(bf16[1,56,512]{2,1,0:T(8,128)(2,1)S(1)} %get-tuple-element.179), channel_id=1, source_target_pairs={{0,4},{1,5},{2,6},{3,7},{4,0},{5,1},{6,2},{7,3},{8,12},{9,13},{10,... | collective-permute-start | bytes 172040 | tf_op jit(solution)/shard_map/ppermute | solution.py:684
  140.9 6.9 %collective-permute-start.39 = (bf16[1,56,512]{2,1,0:T(8,128)(2,1)S(1)}, bf16[1,56,512]{2,1,0:T(8,128)(2,1)S(1)}, u32[]{:S(2)}, u32[]{:S(2)}) collective-permute-start(bf16[1,56,512]{2,1,0:T(8,128)(2,1)S(1)} %get-tuple-element.180), channel_id=1, source_target_pairs={{0,6},{1,7},{2,4},{3,5},{4,2},{5,3},{6,0},{7,1},{8,14},{9,15},{10,... | collective-permute-start | bytes 172040 | tf_op jit(solution)/shard_map/ppermute | solution.py:684
  (14 other events, 60.9 us)

commit v3 on v2

--- a/solution.py
+++ b/solution.py
@@ -383,37 +383,21 @@
     )(lengths, queries, keys, values, incoming, *first)
 
 
-def project_back_kernel(tail_size, ids_ref, grads_ref, x_ref, back_ref, sums_ref, *refs):
-    parts, others, refs = refs[:4], refs[4:8], refs[8:]
-    grad_x_ref, kept_ref, away_ref, bias_sums, whole, full, semaphores = refs
+def weights_kernel(tail_size, ids_ref, grads_ref, x_ref, sums_ref, *refs):
+    kept_ref, away_ref, bias_sums, full, semaphores = refs
     step = pl.program_id(0)
     width = x_ref.shape[1]
     split = full.shape[:3]
     chips = split[1]
-    copies = fetch(ids_ref, WHOLES, parts, others, whole, semaphores.at[0], slice(None))
 
     @pl.when(step == 0)
     def _():
-        for copy in copies:
-            copy.start()
-        grad_x_ref[...] = back_ref[...]
         bias_sums[...] = jnp.zeros_like(bias_sums)
 
     grads = grads_ref[0]
     here = pl.ds(pl.multiple_of(step * SHARD, SHARD), SHARD)
     full[:, :, :, here, :] = tn(x_ref[...], grads).astype(low).reshape(split + (SHARD, width))
     bias_sums[pl.ds(step, 1), :] = jnp.where(step == 1, sums_ref[5:6], column_sum(grads))
-
-    @pl.when(step == 0)
-    def _():
-        for copy in copies:
-            copy.wait()
-
-    leaving = []
-    for group in range(split[0]):
-        leaving += deliver(
-            ids_ref, full, kept_ref, away_ref, semaphores.at[1], group, slice(None)
-        )
 
     @pl.when(step == pl.num_programs(0) - 1)
     def _():
@@ -428,40 +412,78 @@
                 full[
                     j // (2 * chips), j // 2 % chips, j % 2, lines, n * LANES : (n + 1) * LANES
                 ] = tile.astype(low)
+        leaving = []
+        for group in range(split[0]):
+            leaving += deliver(
+                ids_ref, full, kept_ref, away_ref, semaphores, group, slice(None)
+            )
         for copy in leaving:
             copy.start()
-
-    weight = whole[:, :, :, here, :].reshape(width, width)
-    grad_x_ref[...] += nt(grads, weight)
-
-    @pl.when(step == pl.num_programs(0) - 1)
-    def _():
         for copy in leaving:
             copy.wait()
 
 
-def project_back(ids, grads, x, back, sums, parts, others, tail):
+def weight_grads(ids, grads, x, sums, tail):
     length, width = x.shape
-    chips, rows, _ = parts[0].shape
+    chips, rows = width // SHARD // 8, 3 * SHARD + VECTORS
     packed = jax.ShapeDtypeStruct((4, chips, rows, width), low)
     return call(
-        functools.partial(project_back_kernel, tail),
-        "project_back",
-        7,
-        24,
+        functools.partial(weights_kernel, tail),
+        "weights",
+        4,
+        16,
         grid=(3,),
         in_specs=[SCALARS, pl.BlockSpec((1, length, width), lambda p: (p, 0, 0))]
-        + [fixed(x.shape), fixed(back.shape), fixed(sums.shape)]
-        + [ANYWHERE] * 8,
-        out_specs=[fixed(back.shape)] + [ANYWHERE] * 2,
-        out_shape=[jax.ShapeDtypeStruct(back.shape, wide)] + [packed] * 2,
+        + [fixed(x.shape), fixed(sums.shape)],
+        out_specs=[ANYWHERE] * 2,
+        out_shape=[packed] * 2,
         scratch_shapes=[
             pltpu.VMEM((VECTORS, width), wide),
             pltpu.VMEM((4, chips, 2, rows, width), low),
+            pltpu.SemaphoreType.DMA((8,)),
+        ],
+    )(ids, grads, x, sums)
+
+
+def input_kernel(ids_ref, back_ref, grads_ref, *refs):
+    parts, others = refs[:4], refs[4:8]
+    out_ref, whole, semaphores = refs[8:]
+    width = back_ref.shape[1]
+
+    @pl.when(pl.program_id(0) == 0)
+    def _():
+        copies = fetch(ids_ref, WHOLES, parts, others, whole, semaphores, slice(None))
+        for copy in copies:
+            copy.start()
+        for copy in copies:
+            copy.wait()
+
+    total = back_ref[...]
+    for n in range(3):
+        weight = whole[:, :, :, n * SHARD : (n + 1) * SHARD, :].reshape(width, width)
+        total = total + nt(grads_ref[n], weight)
+    out_ref[...] = total
+
+
+def input_grad(ids, back, grads, parts, others):
+    length, width = back.shape
+    block = pl.BlockSpec((BLOCK, width), lambda p: (p, 0))
+    chips, rows, _ = parts[0].shape
+    return call(
+        input_kernel,
+        "input",
+        5,
+        14,
+        grid=(length // BLOCK,),
+        in_specs=[SCALARS, block, pl.BlockSpec((3, BLOCK, width), lambda p: (0, p, 0))]
+        + [ANYWHERE] * 8,
+        out_specs=block,
+        out_shape=jax.ShapeDtypeStruct(back.shape, wide),
+        scratch_shapes=[
             pltpu.VMEM((4, chips, 2, rows, width), low),
-            pltpu.SemaphoreType.DMA((2, 8)),
+            pltpu.SemaphoreType.DMA((8,)),
         ],
-    )(ids, grads, x, back, sums, *parts, *others)
+    )(ids, back, grads, *parts, *others)
 
 
 def middle_kernel(ids_ref, x_ref, y_ref, cotangent_ref, context_ref, table_ref, *refs):
@@ -844,7 +866,8 @@
     early = links.spread(early, links.far[:-1])
     arriving = links.send(early, *links.far[-1])
     if direct:
-        late, arriving[0] = lax.optimization_barrier((late, arriving[0]))
+        near_own = links.swap(early, 1)
+        late, near_own = lax.optimization_barrier((late, near_own))
         received = links.send(late, shift, 2)
         late = links.place(late, received, shift, 2, axis=1)
     else:
@@ -854,7 +877,7 @@
     if direct:
         ids = jnp.stack([links.digit(*links.far[-1]), links.flat() & 1])
         early_parts = [early] + arriving
-        early_others = [links.swap(part, 1) for part in early_parts]
+        early_others = [near_own] + [links.swap(part, 1) for part in early_parts[1:]]
     else:
         ids = jnp.zeros((2,), jnp.int32)
         early = links.pair(links.place(early, arriving, *links.far[-1]))
@@ -968,9 +991,7 @@
         leaving, context_grad = lax.optimization_barrier((leaving, context_grad))
         arriving = links.receive(leaving, links.far[0][0])
         grads = going(incoming=context_grad)
-    grad_x, kept, away = project_back(
-        ids, grads, stream_x, back, sums, early_parts, early_others, tail
-    )
+    kept, away = weight_grads(ids, grads, stream_x, sums, tail)
     if not direct:
         full = restore(kept, away)
         full = jnp.concatenate(
@@ -990,24 +1011,27 @@
     else:
         mine = links.collect(kept.astype(wide) + crossing.astype(wide), links.far[1:])
         mine, leaving = links.cut(mine, *links.far[0])
-    arriving, leaving = lax.optimization_barrier((arriving, leaving))
+    leaving, grads = lax.optimization_barrier((leaving, grads))
     crossing = links.receive(leaving, links.far[0][0])
+    grad_x = input_grad(ids, back, grads, early_parts, early_others)
     if direct:
         total = jnp.concatenate([total[n] + arriving[n].astype(wide) for n in (0, 1)])
     else:
         for part in arriving:
             total = total + part.astype(wide)
+    total = links.collect(total, links.near[1:])
+    shift, radix = links.near[0]
+    total, away = links.cut(total, shift, radix)
+    away[0], grad_x = lax.optimization_barrier((away[0], grad_x))
+    arriving = links.receive(away, shift)
+    crossing, grad_x = lax.optimization_barrier((crossing, grad_x))
     for part in crossing:
         mine = mine + part.astype(wide)
-    total = links.collect(total, links.near[1:])
     mine = links.collect(mine, links.near[1:])
-    shift, radix = links.near[0]
-    total, away = links.cut(total, shift, radix)
-    arriving = links.receive(away, shift)
     mine, leaving = links.cut(mine, shift, radix)
-    early_part, leaving = lax.optimization_barrier((arriving[0], leaving))
+    early_part, leaving = lax.optimization_barrier((arriving[-1], leaving))
     crossing = links.receive(leaving, shift)
-    arriving, crossing[0] = lax.optimization_barrier((arriving[1:], crossing[0]))
+    arriving, crossing[0] = lax.optimization_barrier((arriving[:-1], crossing[0]))
     total = (total + sum(part.astype(wide) for part in [early_part] + arriving))[0]
     at = 2 * share + rows
     up_share = jnp.concatenate(

time: 150 us -> 146 us (0.973)
  starting transfers between devices: 46.8 us -> 41.9 us
    ppermute x40, starting transfers between devices: 46.8 us -> 41.9 us  [swap(): lax.ppermute(values, AXES, [(i, i ^ distance) for i in range(self.count)])]
    pallas_call x1 -> x2, Pallas kernels: 8.02 us -> 8.39 us  [the longest x1 4.82 us: input_grad(): call(input_kernel, 'input', 5, 14, grid=(length // BLOCK,), in_specs=[SCA...]
  transfers between devices with their start and end apart: 40 -> 40, of which waited for: 13 -> 25; matrix products, arithmetic and copies ran while one was open for 3% -> 3% of each run, Pallas kernels for 28% -> 29%
where the time goes in v3:
time: 146 us
  Pallas kernels  68.9 us (47%)
  starting transfers between devices  41.9 us (29%)
  waiting for transfers between devices  24.3 us (17%)
  local copies, waits for them, and re-layouts  5.25 us (4%)
  other arithmetic  4.13 us (3%)
    ppermute x40, starting transfers between devices, swap(): lax.ppermute(values, AXES, [(i, i ^ distance) for i in range(self.count)])  41.9 us
    pallas_call x1, Pallas kernels, middle(): call(middle_kernel, 'middle', 29, 44, grid=(length // TILE,), in_specs=[S...  25.5 us
    ppermute x40, waiting for transfers between devices, swap(): lax.ppermute(values, AXES, [(i, i ^ distance) for i in range(self.count)])  24.3 us
    pallas_call x2, Pallas kernels, attend(): call(functools.partial(attend_kernel, size, tail_size, first), 'attend',...  15.6 us
    pallas_call x1, Pallas kernels, rest_back(): call(functools.partial(rest_back_kernel, size), 'rest_back', 14, 28, grid...  13.2 us
    pallas_call x1, Pallas kernels, input_grad(): call(input_kernel, 'input', 5, 14, grid=(length // BLOCK,), in_specs=[SCA...  4.82 us
    pallas_call x1, Pallas kernels, first_back(): call(functools.partial(first_back_kernel, size), 'first_back', 6, 16, gri...  4.53 us
    pallas_call x1, Pallas kernels, weight_grads(): call(functools.partial(weights_kernel, tail), 'weights', 4, 16, grid=(3,)...  3.57 us
  transfers between devices with their start and end apart: 40, of which 25 were waited for; matrix products, arithmetic and copies ran while one was open for 3% of the time, Pallas kernels for 29%

profile of v3, /device:TPU:0, one launch (start us, length us, event | category | flops | bytes accessed | tf_op | source)
XLA Modules:
  0.0 145.5 jit_solution(12329869275473285297)
XLA Ops:
  0.7 1.4 pad_add_fusion.vectors
  2.1 1.6 %pack.1 = (bf16[56,512]{1,0:T(8,128)(2,1)}, bf16[144,512]{1,0:T(8,128)(2,1)}) custom-call(bf16[16,512]{1,0:T(8,128)(2,1)} %query.1, bf16[16,512]{1,0:T(8,128)(2,1)} %key.1, bf16[16,512]{1,0:T(8,128)(2,1)} %value.1, bf16[8,512]{1,0:T(8,128)(2,1)} %pad_add_fusion.vectors, bf16[16,512]{1,0:T(8,128)(2,1)} %output.1, bf16[16,2048]{1,0:T(8,128)(2,1)} %up.1, ...), custom_call_target="tpu_custom_call" | custom-call | flops 250000000 | bytes 1024 | tf_op jit(solution)/shard_map/pack/pallas_call | solution.py:781
  3.7 4.0 %collective-permute-start.2 = (bf16[1,56,512]{2,1,0:T(8,128)(2,1)}, bf16[1,56,512]{2,1,0:T(8,128)(2,1)S(1)}, u32[]{:S(2)}, u32[]{:S(2)}) collective-permute-start(bf16[1,56,512]{2,1,0:T(8,128)(2,1)} %bitcast.103), channel_id=1, source_target_pairs={{0,4},{1,5},{2,6},{3,7},{4,0},{5,1},{6,2},{7,3},{8,12},{9,13},{10,... | collective-permute-start | bytes 172040 | tf_op jit(solution)/shard_map/ppermute | solution.py:706
  7.7 1.6 %collective-permute-start.1 = (bf16[1,56,512]{2,1,0:T(8,128)(2,1)}, bf16[1,56,512]{2,1,0:T(8,128)(2,1)S(1)}, u32[]{:S(2)}, u32[]{:S(2)}) collective-permute-start(bf16[1,56,512]{2,1,0:T(8,128)(2,1)} %bitcast.104), channel_id=1, source_target_pairs={{0,2},{1,3},{2,0},{3,1},{4,6},{5,7},{6,4},{7,5},{8,10},{9,11},{10,... | collective-permute-start | bytes 172040 | tf_op jit(solution)/shard_map/ppermute | solution.py:706
  9.3 1.9 %collective-permute-start = (bf16[1,144,512]{2,1,0:T(8,128)(2,1)}, bf16[1,144,512]{2,1,0:T(8,128)(2,1)S(1)}, u32[]{:S(2)}, u32[]{:S(2)}) collective-permute-start(bf16[1,144,512]{2,1,0:T(8,128)(2,1)} %bitcast.102), channel_id=1, source_target_pairs={{0,4},{1,5},{2,6},{3,7},{4,0},{5,1},{6,2},{7,3},{8,12},{9,13},{10,... | collective-permute-start | bytes 442376 | tf_op jit(solution)/shard_map/ppermute | solution.py:706
  12.2 3.9 %collective-permute-done.3 = bf16[1,56,512]{2,1,0:T(8,128)(2,1)S(1)} collective-permute-done((bf16[1,56,512]{2,1,0:T(8,128)(2,1)}, bf16[1,56,512]{2,1,0:T(8,128)(2,1)S(1)}, u32[]{:S(2)}, u32[]{:S(2)}) %collective-permute-start.3) | collective-permute-done | bytes 57376 | tf_op jit(solution)/shard_map/ppermute | solution.py:706
  16.1 2.5 %collective-permute-start.12 = (bf16[4,56,512]{2,1,0:T(8,128)(2,1)S(1)}, bf16[4,56,512]{2,1,0:T(8,128)(2,1)S(1)}, u32[]{:S(2)}, u32[]{:S(2)}) collective-permute-start(bf16[4,56,512]{2,1,0:T(8,128)(2,1)S(1)} %constant_dynamic-update-slice_fusion.refs_0_), channel_id=1, source_target_pairs={{0,24},{1,25},{2,26},{3,27},{4,28},{5,29},{6,30},{7,31},{8,16},{9,... | collective-permute-start | bytes 688136 | tf_op jit(solution)/shard_map/ppermute | solution.py:706
  21.2 3.0 %collective-permute-start.5 = (bf16[2,144,512]{2,1,0:T(8,128)(2,1)S(1)}, bf16[2,144,512]{2,1,0:T(8,128)(2,1)S(1)}, u32[]{:S(2)}, u32[]{:S(2)}) collective-permute-start(bf16[2,144,512]{2,1,0:T(8,128)(2,1)S(1)} %constant_dynamic-update-slice_fusion.4), channel_id=1, source_target_pairs={{0,2},{1,3},{2,0},{3,1},{4,6},{5,7},{6,4},{7,5},{8,10},{9,11},{10,... | collective-permute-start | bytes 884744 | tf_op jit(solution)/shard_map/ppermute | solution.py:706
  24.8 2.3 %collective-permute-done.11.refs_2_ = bf16[4,56,512]{2,1,0:T(8,128)(2,1)S(1)} collective-permute-done((bf16[4,56,512]{2,1,0:T(8,128)(2,1)S(1)}, bf16[4,56,512]{2,1,0:T(8,128)(2,1)S(1)}, u32[]{:S(2)}, u32[]{:S(2)}) %collective-permute-start.11) | collective-permute-done | bytes 229408 | tf_op jit(solution)/shard_map/ppermute | solution.py:706
  27.8 3.7 %collective-permute-done.5 = bf16[2,144,512]{2,1,0:T(8,128)(2,1)S(1)} collective-permute-done((bf16[2,144,512]{2,1,0:T(8,128)(2,1)S(1)}, bf16[2,144,512]{2,1,0:T(8,128)(2,1)S(1)}, u32[]{:S(2)}, u32[]{:S(2)}) %collective-permute-start.5) | collective-permute-done | bytes 294944 | tf_op jit(solution)/shard_map/ppermute | solution.py:706
  31.5 1.6 %collective-permute-start.9 = (bf16[2,144,512]{2,1,0:T(8,128)(2,1)S(1)}, bf16[2,144,512]{2,1,0:T(8,128)(2,1)S(1)}, u32[]{:S(2)}, u32[]{:S(2)}) collective-permute-start(bf16[2,144,512]{2,1,0:T(8,128)(2,1)S(1)} %get-tuple-element.210), channel_id=1, source_target_pairs={{0,16},{1,17},{2,18},{3,19},{4,20},{5,21},{6,22},{7,23},{8,24},{9,... | collective-permute-start | bytes 884744 | tf_op jit(solution)/shard_map/ppermute | solution.py:706
  33.1 1.5 %collective-permute-start.7 = (bf16[2,144,512]{2,1,0:T(8,128)(2,1)S(1)}, bf16[2,144,512]{2,1,0:T(8,128)(2,1)S(1)}, u32[]{:S(2)}, u32[]{:S(2)}) collective-permute-start(bf16[2,144,512]{2,1,0:T(8,128)(2,1)S(1)} %get-tuple-element.210), channel_id=1, source_target_pairs={{0,8},{1,9},{2,10},{3,11},{4,12},{5,13},{6,14},{7,15},{8,0},{9,1},... | collective-permute-start | bytes 884744 | tf_op jit(solution)/shard_map/ppermute | solution.py:706
  35.8 10.5 %attend.2 = (bf16[1024,512]{1,0:T(8,128)(2,1)S(1)}, bf16[1024,512]{1,0:T(8,128)(2,1)S(1)}, bf16[1024,512]{1,0:T(8,128)(2,1)S(1)}, bf16[1024,512]{1,0:T(8,128)(2,1)S(1)}, f32[24,512]{1,0:T(8,128)S(1)}) custom-call(s32[2]{0:T(128)S(1)} %pad_add_fusion.1.ids_ref, s32[1,16]{1,0:T(1,128)S(1)} %copy-done.2, bf16[1024,512]{1,0:T(8,128)(2,1)S(1)} %copy-done, ...), custom_call_target="tpu_custom_call" | custom-call | flops 3000000000 | bytes 1024 | tf_op jit(solution)/shard_map/attend/pallas_call | solution.py:259
  46.5 1.2 collective-permute-done.6.refs_1_
  48.2 1.5 %collective-permute-start.17 = (bf16[2,144,512]{2,1,0:T(8,128)(2,1)S(1)}, bf16[2,144,512]{2,1,0:T(8,128)(2,1)S(1)}, u32[]{:S(2)}, u32[]{:S(2)}) collective-permute-start(bf16[2,144,512]{2,1,0:T(8,128)(2,1)S(1)} %collective-permute-done.9.refs_4_), channel_id=1, source_target_pairs={{0,8},{1,9},{2,10},{3,11},{4,12},{5,13},{6,14},{7,15},{8,0},{9,1},... | collective-permute-start | bytes 884744 | tf_op jit(solution)/shard_map/ppermute | solution.py:706
  49.7 5.1 %attend.3 = (bf16[1024,512]{1,0:T(8,128)(2,1)S(1)}, bf16[1024,512]{1,0:T(8,128)(2,1)S(1)}, bf16[1024,512]{1,0:T(8,128)(2,1)S(1)}, bf16[1024,512]{1,0:T(8,128)(2,1)S(1)}, f32[24,512]{1,0:T(8,128)}) custom-call(s32[2]{0:T(128)S(1)} %pad_add_fusion.1.ids_ref, ...), custom_call_target="tpu_custom_call", output_to_operand_aliasing={{0}: (11, {}), {1}: (12, {}), {2}: (13, {}), {3}: (14, {})} | custom-call | flops 1000000000 | bytes 1024 | tf_op jit(solution)/shard_map/attend/pallas_call | solution.py:259
  59.1 25.5 %middle.1 = (bf16[1024,512]{1,0:T(8,128)(2,1)}, f32[1024,512]{1,0:T(8,128)}, f32[1024,512]{1,0:T(8,128)}, bf16[1024,512]{1,0:T(8,128)(2,1)S(1)}, f32[16,512]{1,0...) custom-call(s32[2]{0:T(128)S(1)} %pad_add_fusion.1.ids_ref, ...), custom_call_target="tpu_custom_call" | custom-call | flops 7249999872 | bytes 1024 | tf_op jit(solution)/shard_map/middle/pallas_call | solution.py:650
  84.8 4.5 %first_back.1 = (bf16[1024,128]{1,0:T(8,128)(2,1)S(1)}, bf16[1024,128]{1,0:T(8,128)(2,1)S(1)}, bf16[1024,128]{1,0:T(8,128)(2,1)S(1)}) custom-call(s32[1,16]{1,0:T(1,128)S(1)} %copy-done.2, bf16[1024,512]{1,0:T(8,128)(2,1)S(1)} %get-tuple-element.138.refs_0_, bf16[1024,512]{1,0:T(8,128)(2,1)S(1)} %get-tuple-element.139.refs_1_, ...), custom_call_target="tpu_custom_call" | custom-call | flops 1500000000 | bytes 1024 | tf_op jit(solution)/shard_map/first_back/pallas_call | solution.py:333
  90.5 1.6 %collective-permute-start.26 = (bf16[2,2,144,512]{3,2,1,0:T(8,128)(2,1)S(1)}, bf16[2,2,144,512]{3,2,1,0:T(8,128)(2,1)S(1)}, u32[]{:S(2)}, u32[]{:S(2)}) collective-permute-start(bf16[2,2,144,512]{3,2,1,0:T(8,128)(2,1)S(1)} %get-tuple-element.147), channel_id=1, source_target_pairs={{0,8},{1,9},{2,10},{3,11},{4,12},{5,13},{6,14},{7,15},{8,0},{9,1},... | collective-permute-start | bytes 1769480 | tf_op jit(solution)/shard_map/ppermute | solution.py:706
  92.0 1.4 collective-permute-start.27
  93.5 13.2 %rest_back.1.grads_ref = bf16[3,1024,512]{2,1,0:T(8,128)(2,1)S(1)} custom-call(s32[1,16]{1,0:T(1,128)S(1)} %copy-done.2, bf16[1024,512]{1,0:T(8,128)(2,1)S(1)} %get-tuple-element.138.refs_0_, bf16[1024,512]{1,0:T(8,128)(2,1)S(1)} %get-tuple-element.139.refs_1_, bf16[1024,512]{1,0:T(8,128)(2,1)S(1)} %get-tuple-element.140.refs_2_, ...), custom_call_target="tpu_custom_call" | custom-call | flops 3500000000 | bytes 1024 | tf_op jit(solution)/shard_map/rest_back/pallas_call | solution.py:368
  107.7 1.5 %collective-permute-start.28 = (bf16[2,144,512]{2,1,0:T(8,128)(2,1)S(1)}, bf16[2,144,512]{2,1,0:T(8,128)(2,1)S(1)}, u32[]{:S(2)}, u32[]{:S(2)}) collective-permute-start(bf16[2,144,512]{2,1,0:T(8,128)(2,1)S(1)} %get-tuple-element.158), channel_id=1, source_target_pairs={{0,16},{1,17},{2,18},{3,19},{4,20},{5,21},{6,22},{7,23},{8,24},{9,... | collective-permute-start | bytes 884744 | tf_op jit(solution)/shard_map/ppermute | solution.py:706
  109.8 3.6 %weights.1 = (bf16[4,4,56,512]{3,2,1,0:T(8,128)(2,1)S(1)}, bf16[4,4,56,512]{3,2,1,0:T(8,128)(2,1)S(1)}) custom-call(s32[2]{0:T(128)S(1)} %pad_add_fusion.1.ids_ref, bf16[3,1024,512]{2,1,0:T(8,128)(2,1)S(1)} %rest_back.1.grads_ref, bf16[1024,512]{1,0:T(8,128)(2,1)S(1)} %copy-done, f32[16,512]{1,0:T(8,128)S(1)} %get-tuple-element.161.sums_ref), custom_call_target="tpu_custom_call" | custom-call | flops 1000000000 | bytes 1024 | tf_op jit(solution)/shard_map/weights/pallas_call | solution.py:430
  113.4 2.6 %collective-permute-done.28 = bf16[2,144,512]{2,1,0:T(8,128)(2,1)S(1)} collective-permute-done((bf16[2,144,512]{2,1,0:T(8,128)(2,1)S(1)}, bf16[2,144,512]{2,1,0:T(8,128)(2,1)S(1)}, u32[]{:S(2)}, u32[]{:S(2)}) %collective-permute-start.28) | collective-permute-done | bytes 294944 | tf_op jit(solution)/shard_map/ppermute | solution.py:706
  117.3 2.3 %collective-permute-done.30 = bf16[4,4,56,512]{3,2,1,0:T(8,128)(2,1)S(1)} collective-permute-done((bf16[4,4,56,512]{3,2,1,0:T(8,128)(2,1)S(1)}, bf16[4,4,56,512]{3,2,1,0:T(8,128)(2,1)S(1)}, u32[]{:S(2)}, u32[]{:S(2)}) %collective-permute-start.30) | collective-permute-done | bytes 917536 | tf_op jit(solution)/shard_map/ppermute | solution.py:706
  121.0 2.3 %collective-permute-start.33 = (bf16[4,56,512]{2,1,0:T(8,128)(2,1)S(1)}, bf16[4,56,512]{2,1,0:T(8,128)(2,1)S(1)}, u32[]{:S(2)}, u32[]{:S(2)}) collective-permute-start(bf16[4,56,512]{2,1,0:T(8,128)(2,1)S(1)} %get-tuple-element.168), channel_id=1, source_target_pairs={{0,24},{1,25},{2,26},{3,27},{4,28},{5,29},{6,30},{7,31},{8,16},{9,... | collective-permute-start | bytes 688136 | tf_op jit(solution)/shard_map/ppermute | solution.py:706
  123.5 1.7 %collective-permute-start.36 = (bf16[1,144,512]{2,1,0:T(8,128)(2,1)S(1)}, bf16[1,144,512]{2,1,0:T(8,128)(2,1)S(1)}, u32[]{:S(2)}, u32[]{:S(2)}) collective-permute-start(bf16[1,144,512]{2,1,0:T(8,128)(2,1)S(1)} %get-tuple-element.201), channel_id=1, source_target_pairs={{0,6},{1,7},{2,4},{3,5},{4,2},{5,3},{6,0},{7,1},{8,14},{9,15},{10,... | collective-permute-start | bytes 442376 | tf_op jit(solution)/shard_map/ppermute | solution.py:706
  126.1 4.8 %input.1 = f32[1024,512]{1,0:T(8,128)} custom-call(s32[2]{0:T(128)S(1)} %pad_add_fusion.1.ids_ref, f32[1024,512]{1,0:T(8,128)S(1)} %copy-done.1, bf16[3,1024,512]{2,1,0:T(8,128)(2,1)S(1)} %rest_back.1.grads_ref, bf16[4,56,512]{2,1,0:T(8,128)(2,1)S(1)} %constant_dynamic-update-slice_fusion.refs_0_, bf16[4,56,512]{2,1,0:T(8,128)(2,1)S(1)} %collective-permute-done.10.refs_1_, ...), custom_call_target="tpu_custom_call" | custom-call | flops 1250000000 | bytes 1024 | tf_op jit(solution)/shard_map/input/pallas_call | solution.py:472
  130.9 1.9 %collective-permute-start.34 = (bf16[1,144,512]{2,1,0:T(8,128)(2,1)S(1)}, bf16[1,144,512]{2,1,0:T(8,128)(2,1)S(1)}, u32[]{:S(2)}, u32[]{:S(2)}) collective-permute-start(bf16[1,144,512]{2,1,0:T(8,128)(2,1)S(1)} %get-tuple-element.181), channel_id=1, source_target_pairs={{0,2},{1,3},{2,0},{3,1},{4,6},{5,7},{6,4},{7,5},{8,10},{9,11},{10,... | collective-permute-start | bytes 442376 | tf_op jit(solution)/shard_map/ppermute | solution.py:706
  133.0 4.4 %collective-permute-start.37 = (bf16[1,56,512]{2,1,0:T(8,128)(2,1)S(1)}, bf16[1,56,512]{2,1,0:T(8,128)(2,1)S(1)}, u32[]{:S(2)}, u32[]{:S(2)}) collective-permute-start(bf16[1,56,512]{2,1,0:T(8,128)(2,1)S(1)} %get-tuple-element.182), channel_id=1, source_target_pairs={{0,2},{1,3},{2,0},{3,1},{4,6},{5,7},{6,4},{7,5},{8,10},{9,11},{10,... | collective-permute-start | bytes 172040 | tf_op jit(solution)/shard_map/ppermute | solution.py:706
  137.7 2.1 %collective-permute-start.39 = (bf16[1,56,512]{2,1,0:T(8,128)(2,1)S(1)}, bf16[1,56,512]{2,1,0:T(8,128)(2,1)S(1)}, u32[]{:S(2)}, u32[]{:S(2)}) collective-permute-start(bf16[1,56,512]{2,1,0:T(8,128)(2,1)S(1)} %get-tuple-element.188), channel_id=1, source_target_pairs={{0,6},{1,7},{2,4},{3,5},{4,2},{5,3},{6,0},{7,1},{8,14},{9,15},{10,... | collective-permute-start | bytes 172040 | tf_op jit(solution)/shard_map/ppermute | solution.py:706
  140.3 1.2 collective-permute-done.37
  (104 shorter events, 22.3 us)
Async XLA Ops:
  3.7 8.4 %collective-permute-start.2 = (bf16[1,56,512]{2,1,0:T(8,128)(2,1)}, bf16[1,56,512]{2,1,0:T(8,128)(2,1)S(1)}, u32[]{:S(2)}, u32[]{:S(2)}) collective-permute-start(bf16[1,56,512]{2,1,0:T(8,128)(2,1)} %bitcast.103), channel_id=1, source_target_pairs={{0,4},{1,5},{2,6},{3,7},{4,0},{5,1},{6,2},{7,3},{8,12},{9,13},{10,... | collective-permute-start | bytes 172040 | tf_op jit(solution)/shard_map/ppermute | solution.py:706
  7.7 4.4 %collective-permute-start.1 = (bf16[1,56,512]{2,1,0:T(8,128)(2,1)}, bf16[1,56,512]{2,1,0:T(8,128)(2,1)S(1)}, u32[]{:S(2)}, u32[]{:S(2)}) collective-permute-start(bf16[1,56,512]{2,1,0:T(8,128)(2,1)} %bitcast.104), channel_id=1, source_target_pairs={{0,2},{1,3},{2,0},{3,1},{4,6},{5,7},{6,4},{7,5},{8,10},{9,11},{10,... | collective-permute-start | bytes 172040 | tf_op jit(solution)/shard_map/ppermute | solution.py:706
  9.3 6.8 %collective-permute-start.3 = (bf16[1,56,512]{2,1,0:T(8,128)(2,1)}, bf16[1,56,512]{2,1,0:T(8,128)(2,1)S(1)}, u32[]{:S(2)}, u32[]{:S(2)}) collective-permute-start(bf16[1,56,512]{2,1,0:T(8,128)(2,1)} %bitcast.105), channel_id=1, source_target_pairs={{0,6},{1,7},{2,4},{3,5},{4,2},{5,3},{6,0},{7,1},{8,14},{9,15},{10,... | collective-permute-start | bytes 172040 | tf_op jit(solution)/shard_map/ppermute | solution.py:706
  9.3 11.3 %collective-permute-start = (bf16[1,144,512]{2,1,0:T(8,128)(2,1)}, bf16[1,144,512]{2,1,0:T(8,128)(2,1)S(1)}, u32[]{:S(2)}, u32[]{:S(2)}) collective-permute-start(bf16[1,144,512]{2,1,0:T(8,128)(2,1)} %bitcast.102), channel_id=1, source_target_pairs={{0,4},{1,5},{2,6},{3,7},{4,0},{5,1},{6,2},{7,3},{8,12},{9,13},{10,... | collective-permute-start | bytes 442376 | tf_op jit(solution)/shard_map/ppermute | solution.py:706
  16.1 8.7 %collective-permute-start.12 = (bf16[4,56,512]{2,1,0:T(8,128)(2,1)S(1)}, bf16[4,56,512]{2,1,0:T(8,128)(2,1)S(1)}, u32[]{:S(2)}, u32[]{:S(2)}) collective-permute-start(bf16[4,56,512]{2,1,0:T(8,128)(2,1)S(1)} %constant_dynamic-update-slice_fusion.refs_0_), channel_id=1, source_target_pairs={{0,24},{1,25},{2,26},{3,27},{4,28},{5,29},{6,30},{7,31},{8,16},{9,... | collective-permute-start | bytes 688136 | tf_op jit(solution)/shard_map/ppermute | solution.py:706
  18.6 8.5 %collective-permute-start.11 = (bf16[4,56,512]{2,1,0:T(8,128)(2,1)S(1)}, bf16[4,56,512]{2,1,0:T(8,128)(2,1)S(1)}, u32[]{:S(2)}, u32[]{:S(2)}) collective-permute-start(bf16[4,56,512]{2,1,0:T(8,128)(2,1)S(1)} %constant_dynamic-update-slice_fusion.refs_0_), channel_id=1, source_target_pairs={{0,16},{1,17},{2,18},{3,19},{4,20},{5,21},{6,22},{7,23},{8,24},{9,... | collective-permute-start | bytes 688136 | tf_op jit(solution)/shard_map/ppermute | solution.py:706
  19.1 8.1 %collective-permute-start.10 = (bf16[4,56,512]{2,1,0:T(8,128)(2,1)S(1)}, bf16[4,56,512]{2,1,0:T(8,128)(2,1)S(1)}, u32[]{:S(2)}, u32[]{:S(2)}) collective-permute-start(bf16[4,56,512]{2,1,0:T(8,128)(2,1)S(1)} %constant_dynamic-update-slice_fusion.refs_0_), channel_id=1, source_target_pairs={{0,8},{1,9},{2,10},{3,11},{4,12},{5,13},{6,14},{7,15},{8,0},{9,1},... | collective-permute-start | bytes 688136 | tf_op jit(solution)/shard_map/ppermute | solution.py:706
  21.2 10.3 %collective-permute-start.5 = (bf16[2,144,512]{2,1,0:T(8,128)(2,1)S(1)}, bf16[2,144,512]{2,1,0:T(8,128)(2,1)S(1)}, u32[]{:S(2)}, u32[]{:S(2)}) collective-permute-start(bf16[2,144,512]{2,1,0:T(8,128)(2,1)S(1)} %constant_dynamic-update-slice_fusion.4), channel_id=1, source_target_pairs={{0,2},{1,3},{2,0},{3,1},{4,6},{5,7},{6,4},{7,5},{8,10},{9,11},{10,... | collective-permute-start | bytes 884744 | tf_op jit(solution)/shard_map/ppermute | solution.py:706
  24.8 9.8 %collective-permute-start.15 = (bf16[4,56,512]{2,1,0:T(8,128)(2,1)S(1)}, bf16[4,56,512]{2,1,0:T(8,128)(2,1)S(1)}, u32[]{:S(2)}, u32[]{:S(2)}) collective-permute-start(bf16[4,56,512]{2,1,0:T(8,128)(2,1)S(1)} %collective-permute-done.12.refs_3_), channel_id=1, source_target_pairs={{0,1},{1,0},{2,3},{3,2},{4,5},{5,4},{6,7},{7,6},{8,9},{9,8},{10,11... | collective-permute-start | bytes 688136 | tf_op jit(solution)/shard_map/ppermute | solution.py:706
  27.1 8.0 %collective-permute-start.14 = (bf16[4,56,512]{2,1,0:T(8,128)(2,1)S(1)}, bf16[4,56,512]{2,1,0:T(8,128)(2,1)S(1)}, u32[]{:S(2)}, u32[]{:S(2)}) collective-permute-start(bf16[4,56,512]{2,1,0:T(8,128)(2,1)S(1)} %collective-permute-done.11.refs_2_), channel_id=1, source_target_pairs={{0,1},{1,0},{2,3},{3,2},{4,5},{5,4},{6,7},{7,6},{8,9},{9,8},{10,11... | collective-permute-start | bytes 688136 | tf_op jit(solution)/shard_map/ppermute | solution.py:706
  27.2 8.5 %collective-permute-start.13 = (bf16[4,56,512]{2,1,0:T(8,128)(2,1)S(1)}, bf16[4,56,512]{2,1,0:T(8,128)(2,1)S(1)}, u32[]{:S(2)}, u32[]{:S(2)}) collective-permute-start(bf16[4,56,512]{2,1,0:T(8,128)(2,1)S(1)} %collective-permute-done.10.refs_1_), channel_id=1, source_target_pairs={{0,1},{1,0},{2,3},{3,2},{4,5},{5,4},{6,7},{7,6},{8,9},{9,8},{10,11... | collective-permute-start | bytes 688136 | tf_op jit(solution)/shard_map/ppermute | solution.py:706
  31.5 14.7 %collective-permute-start.9 = (bf16[2,144,512]{2,1,0:T(8,128)(2,1)S(1)}, bf16[2,144,512]{2,1,0:T(8,128)(2,1)S(1)}, u32[]{:S(2)}, u32[]{:S(2)}) collective-permute-start(bf16[2,144,512]{2,1,0:T(8,128)(2,1)S(1)} %get-tuple-element.210), channel_id=1, source_target_pairs={{0,16},{1,17},{2,18},{3,19},{4,20},{5,21},{6,22},{7,23},{8,24},{9,... | collective-permute-start | bytes 884744 | tf_op jit(solution)/shard_map/ppermute | solution.py:706
  33.1 13.2 %collective-permute-start.7 = (bf16[2,144,512]{2,1,0:T(8,128)(2,1)S(1)}, bf16[2,144,512]{2,1,0:T(8,128)(2,1)S(1)}, u32[]{:S(2)}, u32[]{:S(2)}) collective-permute-start(bf16[2,144,512]{2,1,0:T(8,128)(2,1)S(1)} %get-tuple-element.210), channel_id=1, source_target_pairs={{0,8},{1,9},{2,10},{3,11},{4,12},{5,13},{6,14},{7,15},{8,0},{9,1},... | collective-permute-start | bytes 884744 | tf_op jit(solution)/shard_map/ppermute | solution.py:706
  34.6 11.8 %collective-permute-start.8 = (bf16[2,144,512]{2,1,0:T(8,128)(2,1)S(1)}, bf16[2,144,512]{2,1,0:T(8,128)(2,1)S(1)}, u32[]{:S(2)}, u32[]{:S(2)}) collective-permute-start(bf16[2,144,512]{2,1,0:T(8,128)(2,1)S(1)} %get-tuple-element.211), channel_id=1, source_target_pairs={{0,16},{1,17},{2,18},{3,19},{4,20},{5,21},{6,22},{7,23},{8,24},{9,... | collective-permute-start | bytes 884744 | tf_op jit(solution)/shard_map/ppermute | solution.py:706
  35.1 12.6 %collective-permute-start.6 = (bf16[2,144,512]{2,1,0:T(8,128)(2,1)S(1)}, bf16[2,144,512]{2,1,0:T(8,128)(2,1)S(1)}, u32[]{:S(2)}, u32[]{:S(2)}) collective-permute-start(bf16[2,144,512]{2,1,0:T(8,128)(2,1)S(1)} %get-tuple-element.211), channel_id=1, source_target_pairs={{0,8},{1,9},{2,10},{3,11},{4,12},{5,13},{6,14},{7,15},{8,0},{9,1},... | collective-permute-start | bytes 884744 | tf_op jit(solution)/shard_map/ppermute | solution.py:706
  47.7 7.3 %collective-permute-start.16 = (bf16[2,144,512]{2,1,0:T(8,128)(2,1)S(1)}, bf16[2,144,512]{2,1,0:T(8,128)(2,1)S(1)}, u32[]{:S(2)}, u32[]{:S(2)}) collective-permute-start(bf16[2,144,512]{2,1,0:T(8,128)(2,1)S(1)} %collective-permute-done.6.refs_1_), channel_id=1, source_target_pairs={{0,16},{1,17},{2,18},{3,19},{4,20},{5,21},{6,22},{7,23},{8,24},{9,... | collective-permute-start | bytes 884744 | tf_op jit(solution)/shard_map/ppermute | solution.py:706
  48.2 7.1 %collective-permute-start.17 = (bf16[2,144,512]{2,1,0:T(8,128)(2,1)S(1)}, bf16[2,144,512]{2,1,0:T(8,128)(2,1)S(1)}, u32[]{:S(2)}, u32[]{:S(2)}) collective-permute-start(bf16[2,144,512]{2,1,0:T(8,128)(2,1)S(1)} %collective-permute-done.9.refs_4_), channel_id=1, source_target_pairs={{0,8},{1,9},{2,10},{3,11},{4,12},{5,13},{6,14},{7,15},{8,0},{9,1},... | collective-permute-start | bytes 884744 | tf_op jit(solution)/shard_map/ppermute | solution.py:706
  49.7 6.7 %collective-permute-start.18 = (bf16[4,144,512]{2,1,0:T(8,128)(2,1)S(1)}, bf16[4,144,512]{2,1,0:T(8,128)(2,1)S(1)}, u32[]{:S(2)}, u32[]{:S(2)}) collective-permute-start(bf16[4,144,512]{2,1,0:T(8,128)(2,1)S(1)} %bitcast.100), channel_id=1, source_target_pairs={{0,1},{1,0},{2,3},{3,2},{4,5},{5,4},{6,7},{7,6},{8,9},{9,8},{10,11... | collective-permute-start | bytes 1769480 | tf_op jit(solution)/shard_map/ppermute | solution.py:706
  84.6 4.8 %collective-permute-start.25 = (bf16[4,4,144,512]{3,2,1,0:T(8,128)(2,1)}, bf16[4,4,144,512]{3,2,1,0:T(8,128)(2,1)S(1)}, u32[]{:S(2)}, u32[]{:S(2)}) collective-permute-start(bf16[4,4,144,512]{3,2,1,0:T(8,128)(2,1)} %get-tuple-element.137), channel_id=1, source_target_pairs={{0,1},{1,0},{2,3},{3,2},{4,5},{5,4},{6,7},{7,6},{8,9},{9,8},{10,11... | collective-permute-start | bytes 7077896 | tf_op jit(solution)/shard_map/ppermute | solution.py:706
  90.5 16.2 %collective-permute-start.26 = (bf16[2,2,144,512]{3,2,1,0:T(8,128)(2,1)S(1)}, bf16[2,2,144,512]{3,2,1,0:T(8,128)(2,1)S(1)}, u32[]{:S(2)}, u32[]{:S(2)}) collective-permute-start(bf16[2,2,144,512]{3,2,1,0:T(8,128)(2,1)S(1)} %get-tuple-element.147), channel_id=1, source_target_pairs={{0,8},{1,9},{2,10},{3,11},{4,12},{5,13},{6,14},{7,15},{8,0},{9,1},... | collective-permute-start | bytes 1769480 | tf_op jit(solution)/shard_map/ppermute | solution.py:706
  92.0 15.3 %collective-permute-start.27 = (bf16[2,2,144,512]{3,2,1,0:T(8,128)(2,1)S(1)}, bf16[2,2,144,512]{3,2,1,0:T(8,128)(2,1)S(1)}, u32[]{:S(2)}, u32[]{:S(2)}) collective-permute-start(bf16[2,2,144,512]{3,2,1,0:T(8,128)(2,1)S(1)} %get-tuple-element.148), channel_id=1, source_target_pairs={{0,16},{1,17},{2,18},{3,19},{4,20},{5,21},{6,22},{7,23},{8,24},{9,... | collective-permute-start | bytes 1769480 | tf_op jit(solution)/shard_map/ppermute | solution.py:706
  107.7 8.2 %collective-permute-start.28 = (bf16[2,144,512]{2,1,0:T(8,128)(2,1)S(1)}, bf16[2,144,512]{2,1,0:T(8,128)(2,1)S(1)}, u32[]{:S(2)}, u32[]{:S(2)}) collective-permute-start(bf16[2,144,512]{2,1,0:T(8,128)(2,1)S(1)} %get-tuple-element.158), channel_id=1, source_target_pairs={{0,16},{1,17},{2,18},{3,19},{4,20},{5,21},{6,22},{7,23},{8,24},{9,... | collective-permute-start | bytes 884744 | tf_op jit(solution)/shard_map/ppermute | solution.py:706
  109.2 7.9 %collective-permute-start.29 = (bf16[2,144,512]{2,1,0:T(8,128)(2,1)S(1)}, bf16[2,144,512]{2,1,0:T(8,128)(2,1)S(1)}, u32[]{:S(2)}, u32[]{:S(2)}) collective-permute-start(bf16[2,144,512]{2,1,0:T(8,128)(2,1)S(1)} %get-tuple-element.159), channel_id=1, source_target_pairs={{0,8},{1,9},{2,10},{3,11},{4,12},{5,13},{6,14},{7,15},{8,0},{9,1},... | collective-permute-start | bytes 884744 | tf_op jit(solution)/shard_map/ppermute | solution.py:706
  119.8 11.2 %collective-permute-start.31 = (bf16[4,56,512]{2,1,0:T(8,128)(2,1)S(1)}, bf16[4,56,512]{2,1,0:T(8,128)(2,1)S(1)}, u32[]{:S(2)}, u32[]{:S(2)}) collective-permute-start(bf16[4,56,512]{2,1,0:T(8,128)(2,1)S(1)} %get-tuple-element.166), channel_id=1, source_target_pairs={{0,8},{1,9},{2,10},{3,11},{4,12},{5,13},{6,14},{7,15},{8,0},{9,1},... | collective-permute-start | bytes 688136 | tf_op jit(solution)/shard_map/ppermute | solution.py:706
  120.4 12.4 %collective-permute-start.32 = (bf16[4,56,512]{2,1,0:T(8,128)(2,1)S(1)}, bf16[4,56,512]{2,1,0:T(8,128)(2,1)S(1)}, u32[]{:S(2)}, u32[]{:S(2)}) collective-permute-start(bf16[4,56,512]{2,1,0:T(8,128)(2,1)S(1)} %get-tuple-element.167), channel_id=1, source_target_pairs={{0,16},{1,17},{2,18},{3,19},{4,20},{5,21},{6,22},{7,23},{8,24},{9,... | collective-permute-start | bytes 688136 | tf_op jit(solution)/shard_map/ppermute | solution.py:706
  121.0 11.8 %collective-permute-start.33 = (bf16[4,56,512]{2,1,0:T(8,128)(2,1)S(1)}, bf16[4,56,512]{2,1,0:T(8,128)(2,1)S(1)}, u32[]{:S(2)}, u32[]{:S(2)}) collective-permute-start(bf16[4,56,512]{2,1,0:T(8,128)(2,1)S(1)} %get-tuple-element.168), channel_id=1, source_target_pairs={{0,24},{1,25},{2,26},{3,27},{4,28},{5,29},{6,30},{7,31},{8,16},{9,... | collective-permute-start | bytes 688136 | tf_op jit(solution)/shard_map/ppermute | solution.py:706
  123.5 9.6 %collective-permute-start.36 = (bf16[1,144,512]{2,1,0:T(8,128)(2,1)S(1)}, bf16[1,144,512]{2,1,0:T(8,128)(2,1)S(1)}, u32[]{:S(2)}, u32[]{:S(2)}) collective-permute-start(bf16[1,144,512]{2,1,0:T(8,128)(2,1)S(1)} %get-tuple-element.201), channel_id=1, source_target_pairs={{0,6},{1,7},{2,4},{3,5},{4,2},{5,3},{6,0},{7,1},{8,14},{9,15},{10,... | collective-permute-start | bytes 442376 | tf_op jit(solution)/shard_map/ppermute | solution.py:706
  125.2 14.8 %collective-permute-start.35 = (bf16[1,144,512]{2,1,0:T(8,128)(2,1)S(1)}, bf16[1,144,512]{2,1,0:T(8,128)(2,1)S(1)}, u32[]{:S(2)}, u32[]{:S(2)}) collective-permute-start(bf16[1,144,512]{2,1,0:T(8,128)(2,1)S(1)} %get-tuple-element.203), channel_id=1, source_target_pairs={{0,4},{1,5},{2,6},{3,7},{4,0},{5,1},{6,2},{7,3},{8,12},{9,13},{10,... | collective-permute-start | bytes 442376 | tf_op jit(solution)/shard_map/ppermute | solution.py:706
  130.9 9.3 %collective-permute-start.34 = (bf16[1,144,512]{2,1,0:T(8,128)(2,1)S(1)}, bf16[1,144,512]{2,1,0:T(8,128)(2,1)S(1)}, u32[]{:S(2)}, u32[]{:S(2)}) collective-permute-start(bf16[1,144,512]{2,1,0:T(8,128)(2,1)S(1)} %get-tuple-element.181), channel_id=1, source_target_pairs={{0,2},{1,3},{2,0},{3,1},{4,6},{5,7},{6,4},{7,5},{8,10},{9,11},{10,... | collective-permute-start | bytes 442376 | tf_op jit(solution)/shard_map/ppermute | solution.py:706
  133.0 8.4 %collective-permute-start.37 = (bf16[1,56,512]{2,1,0:T(8,128)(2,1)S(1)}, bf16[1,56,512]{2,1,0:T(8,128)(2,1)S(1)}, u32[]{:S(2)}, u32[]{:S(2)}) collective-permute-start(bf16[1,56,512]{2,1,0:T(8,128)(2,1)S(1)} %get-tuple-element.182), channel_id=1, source_target_pairs={{0,2},{1,3},{2,0},{3,1},{4,6},{5,7},{6,4},{7,5},{8,10},{9,11},{10,... | collective-permute-start | bytes 172040 | tf_op jit(solution)/shard_map/ppermute | solution.py:706
  137.4 6.1 %collective-permute-start.38 = (bf16[1,56,512]{2,1,0:T(8,128)(2,1)S(1)}, bf16[1,56,512]{2,1,0:T(8,128)(2,1)S(1)}, u32[]{:S(2)}, u32[]{:S(2)}) collective-permute-start(bf16[1,56,512]{2,1,0:T(8,128)(2,1)S(1)} %get-tuple-element.187), channel_id=1, source_target_pairs={{0,4},{1,5},{2,6},{3,7},{4,0},{5,1},{6,2},{7,3},{8,12},{9,13},{10,... | collective-permute-start | bytes 172040 | tf_op jit(solution)/shard_map/ppermute | solution.py:706
  137.7 6.1 %collective-permute-start.39 = (bf16[1,56,512]{2,1,0:T(8,128)(2,1)S(1)}, bf16[1,56,512]{2,1,0:T(8,128)(2,1)S(1)}, u32[]{:S(2)}, u32[]{:S(2)}) collective-permute-start(bf16[1,56,512]{2,1,0:T(8,128)(2,1)S(1)} %get-tuple-element.188), channel_id=1, source_target_pairs={{0,6},{1,7},{2,4},{3,5},{4,2},{5,3},{6,0},{7,1},{8,14},{9,15},{10,... | collective-permute-start | bytes 172040 | tf_op jit(solution)/shard_map/ppermute | solution.py:706
  (14 other events, 62.0 us)

commit v4 on v3

--- a/solution.py
+++ b/solution.py
@@ -762,12 +762,21 @@
     return [whole[k, :, 0] for k in range(4)], [whole[k, :, 1] for k in range(4)]
 
 
-def pack_kernel(query, key, value, vectors, output, up, down, early_ref, late_ref):
+def pack_kernel(query, key, value, output, up, down, *refs):
+    vectors, (early_ref, late_ref) = refs[:-2], refs[-2:]
     rows, width = query.shape
     share = down.shape[0]
     for n, array in enumerate((query, key, value)):
         early_ref[n * rows : (n + 1) * rows] = array[...]
-    early_ref[3 * rows :] = vectors[...]
+    row = lax.broadcasted_iota(jnp.int32, (VECTORS, LANES), 0)
+    groups = [jnp.zeros((VECTORS, LANES), wide) for _ in range(width // LANES)]
+    last = len(vectors) - 1
+    for n, vector in enumerate(vectors):
+        place, group = (n % VECTORS, n // VECTORS) if n < last else (0, 2)
+        line = vector[...].astype(wide).reshape(1, -1)
+        line = jnp.concatenate([line, jnp.zeros((1, LANES - line.shape[1]), wide)], axis=1)
+        groups[group] = jnp.where(row == place, line, groups[group])
+    early_ref[3 * rows :] = jnp.concatenate(groups, axis=1).astype(low)
     late_ref[:share] = down[...]
     late_ref[2 * share :] = output[...]
     for c in range(share // rows):
@@ -775,7 +784,7 @@
         late_ref[start : start + rows] = up[:, c * width : (c + 1) * width]
 
 
-def pack(query, key, value, vectors, output, up, down):
+def pack(query, key, value, output, up, down, vectors):
     rows, width = query.shape
     shapes = [(3 * rows + VECTORS, width), (2 * down.shape[0] + rows, width)]
     return call(
@@ -784,7 +793,7 @@
         1,
         60,
         out_shape=[jax.ShapeDtypeStruct(shape, low) for shape in shapes],
-    )(query, key, value, vectors, output, up, down)
+    )(query, key, value, output, up, down, *vectors)
 
 
 def body(
@@ -845,12 +854,18 @@
             for row, lane, line in places + [(0, 2 * LANES, last)]
         )
 
-    packed = pack_lines(vectors, up_bias)
     if direct:
         early, late = pack(
-            query_weight, key_weight, value_weight, packed, output_weight, up_weight, down_weight
+            query_weight,
+            key_weight,
+            value_weight,
+            output_weight,
+            up_weight,
+            down_weight,
+            vectors + [up_bias],
         )
     else:
+        packed = pack_lines(vectors, up_bias)
         early = jnp.concatenate([query_weight, key_weight, value_weight, packed], axis=0)
         ups = [up_weight[:, c * width : (c + 1) * width] for c in range(columns)]
         late = jnp.concatenate([down_weight] + ups + [output_weight], axis=0)

time: 146 us -> 144 us (0.986)
  no operation moved by 1% of the time
where the time goes in v4:
time: 144 us
  Pallas kernels  69 us (48%)
  starting transfers between devices  41.9 us (29%)
  waiting for transfers between devices  24.3 us (17%)
  local copies, waits for them, and re-layouts  5.25 us (4%)
  other arithmetic  2.72 us (2%)
    ppermute x40, starting transfers between devices, swap(): lax.ppermute(values, AXES, [(i, i ^ distance) for i in range(self.count)])  41.9 us
    pallas_call x1, Pallas kernels, middle(): call(middle_kernel, 'middle', 29, 44, grid=(length // TILE,), in_specs=[S...  25.5 us
    ppermute x40, waiting for transfers between devices, swap(): lax.ppermute(values, AXES, [(i, i ^ distance) for i in range(self.count)])  24.3 us
    pallas_call x2, Pallas kernels, attend(): call(functools.partial(attend_kernel, size, tail_size, first), 'attend',...  15.6 us
    pallas_call x1, Pallas kernels, rest_back(): call(functools.partial(rest_back_kernel, size), 'rest_back', 14, 28, grid...  13.2 us
    pallas_call x1, Pallas kernels, input_grad(): call(input_kernel, 'input', 5, 14, grid=(length // BLOCK,), in_specs=[SCA...  4.82 us
    pallas_call x1, Pallas kernels, first_back(): call(functools.partial(first_back_kernel, size), 'first_back', 6, 16, gri...  4.53 us
    pallas_call x1, Pallas kernels, weight_grads(): call(functools.partial(weights_kernel, tail), 'weights', 4, 16, grid=(3,)...  3.57 us
  transfers between devices with their start and end apart: 40, of which 25 were waited for; matrix products, arithmetic and copies ran while one was open for 3% of the time, Pallas kernels for 29%

profile of v4, /device:TPU:0, one launch (start us, length us, event | category | flops | bytes accessed | tf_op | source)
XLA Modules:
  0.0 144.2 jit_solution(3092614434936811347)
XLA Ops:
  0.7 1.7 %pack.1 = (bf16[56,512]{1,0:T(8,128)(2,1)}, bf16[144,512]{1,0:T(8,128)(2,1)}) custom-call(bf16[16,512]{1,0:T(8,128)(2,1)} %query.1, bf16[16,512]{1,0:T(8,128)(2,1)} %key.1, bf16[16,512]{1,0:T(8,128)(2,1)} %value.1, bf16[16,512]{1,0:T(8,128)(2,1)} %output.1, bf16[16,2048]{1,0:T(8,128)(2,1)} %up.1, bf16[64,512]{1,0:T(8,128)(2,1)} %down.1, ...), custom_call_target="tpu_custom_call" | custom-call | flops 250000000 | bytes 1024 | tf_op jit(solution)/shard_map/pack/pallas_call | solution.py:790
  2.4 4.0 %collective-permute-start.2 = (bf16[1,56,512]{2,1,0:T(8,128)(2,1)}, bf16[1,56,512]{2,1,0:T(8,128)(2,1)S(1)}, u32[]{:S(2)}, u32[]{:S(2)}) collective-permute-start(bf16[1,56,512]{2,1,0:T(8,128)(2,1)} %bitcast.92), channel_id=1, source_target_pairs={{0,4},{1,5},{2,6},{3,7},{4,0},{5,1},{6,2},{7,3},{8,12},{9,13},{10,... | collective-permute-start | bytes 172040 | tf_op jit(solution)/shard_map/ppermute | solution.py:706
  6.4 1.6 %collective-permute-start.1 = (bf16[1,56,512]{2,1,0:T(8,128)(2,1)}, bf16[1,56,512]{2,1,0:T(8,128)(2,1)S(1)}, u32[]{:S(2)}, u32[]{:S(2)}) collective-permute-start(bf16[1,56,512]{2,1,0:T(8,128)(2,1)} %bitcast.93), channel_id=1, source_target_pairs={{0,2},{1,3},{2,0},{3,1},{4,6},{5,7},{6,4},{7,5},{8,10},{9,11},{10,... | collective-permute-start | bytes 172040 | tf_op jit(solution)/shard_map/ppermute | solution.py:706
  8.0 1.9 %collective-permute-start = (bf16[1,144,512]{2,1,0:T(8,128)(2,1)}, bf16[1,144,512]{2,1,0:T(8,128)(2,1)S(1)}, u32[]{:S(2)}, u32[]{:S(2)}) collective-permute-start(bf16[1,144,512]{2,1,0:T(8,128)(2,1)} %bitcast.91), channel_id=1, source_target_pairs={{0,4},{1,5},{2,6},{3,7},{4,0},{5,1},{6,2},{7,3},{8,12},{9,13},{10,... | collective-permute-start | bytes 442376 | tf_op jit(solution)/shard_map/ppermute | solution.py:706
  10.8 3.9 %collective-permute-done.3 = bf16[1,56,512]{2,1,0:T(8,128)(2,1)S(1)} collective-permute-done((bf16[1,56,512]{2,1,0:T(8,128)(2,1)}, bf16[1,56,512]{2,1,0:T(8,128)(2,1)S(1)}, u32[]{:S(2)}, u32[]{:S(2)}) %collective-permute-start.3) | collective-permute-done | bytes 57376 | tf_op jit(solution)/shard_map/ppermute | solution.py:706
  14.8 2.5 %collective-permute-start.12 = (bf16[4,56,512]{2,1,0:T(8,128)(2,1)S(1)}, bf16[4,56,512]{2,1,0:T(8,128)(2,1)S(1)}, u32[]{:S(2)}, u32[]{:S(2)}) collective-permute-start(bf16[4,56,512]{2,1,0:T(8,128)(2,1)S(1)} %constant_dynamic-update-slice_fusion.refs_0_), channel_id=1, source_target_pairs={{0,24},{1,25},{2,26},{3,27},{4,28},{5,29},{6,30},{7,31},{8,16},{9,... | collective-permute-start | bytes 688136 | tf_op jit(solution)/shard_map/ppermute | solution.py:706
  19.8 3.0 %collective-permute-start.5 = (bf16[2,144,512]{2,1,0:T(8,128)(2,1)S(1)}, bf16[2,144,512]{2,1,0:T(8,128)(2,1)S(1)}, u32[]{:S(2)}, u32[]{:S(2)}) collective-permute-start(bf16[2,144,512]{2,1,0:T(8,128)(2,1)S(1)} %constant_dynamic-update-slice_fusion.4), channel_id=1, source_target_pairs={{0,2},{1,3},{2,0},{3,1},{4,6},{5,7},{6,4},{7,5},{8,10},{9,11},{10,... | collective-permute-start | bytes 884744 | tf_op jit(solution)/shard_map/ppermute | solution.py:706
  23.4 2.3 %collective-permute-done.11.refs_2_ = bf16[4,56,512]{2,1,0:T(8,128)(2,1)S(1)} collective-permute-done((bf16[4,56,512]{2,1,0:T(8,128)(2,1)S(1)}, bf16[4,56,512]{2,1,0:T(8,128)(2,1)S(1)}, u32[]{:S(2)}, u32[]{:S(2)}) %collective-permute-start.11) | collective-permute-done | bytes 229408 | tf_op jit(solution)/shard_map/ppermute | solution.py:706
  26.4 3.7 %collective-permute-done.5 = bf16[2,144,512]{2,1,0:T(8,128)(2,1)S(1)} collective-permute-done((bf16[2,144,512]{2,1,0:T(8,128)(2,1)S(1)}, bf16[2,144,512]{2,1,0:T(8,128)(2,1)S(1)}, u32[]{:S(2)}, u32[]{:S(2)}) %collective-permute-start.5) | collective-permute-done | bytes 294944 | tf_op jit(solution)/shard_map/ppermute | solution.py:706
  30.2 1.6 %collective-permute-start.9 = (bf16[2,144,512]{2,1,0:T(8,128)(2,1)S(1)}, bf16[2,144,512]{2,1,0:T(8,128)(2,1)S(1)}, u32[]{:S(2)}, u32[]{:S(2)}) collective-permute-start(bf16[2,144,512]{2,1,0:T(8,128)(2,1)S(1)} %get-tuple-element.210), channel_id=1, source_target_pairs={{0,16},{1,17},{2,18},{3,19},{4,20},{5,21},{6,22},{7,23},{8,24},{9,... | collective-permute-start | bytes 884744 | tf_op jit(solution)/shard_map/ppermute | solution.py:706
  31.8 1.5 %collective-permute-start.7 = (bf16[2,144,512]{2,1,0:T(8,128)(2,1)S(1)}, bf16[2,144,512]{2,1,0:T(8,128)(2,1)S(1)}, u32[]{:S(2)}, u32[]{:S(2)}) collective-permute-start(bf16[2,144,512]{2,1,0:T(8,128)(2,1)S(1)} %get-tuple-element.210), channel_id=1, source_target_pairs={{0,8},{1,9},{2,10},{3,11},{4,12},{5,13},{6,14},{7,15},{8,0},{9,1},... | collective-permute-start | bytes 884744 | tf_op jit(solution)/shard_map/ppermute | solution.py:706
  34.4 10.5 %attend.2 = (bf16[1024,512]{1,0:T(8,128)(2,1)S(1)}, bf16[1024,512]{1,0:T(8,128)(2,1)S(1)}, bf16[1024,512]{1,0:T(8,128)(2,1)S(1)}, bf16[1024,512]{1,0:T(8,128)(2,1)S(1)}, f32[24,512]{1,0:T(8,128)S(1)}) custom-call(s32[2]{0:T(128)S(1)} %pad_add_fusion.ids_ref, s32[1,16]{1,0:T(1,128)S(1)} %copy-done.2, bf16[1024,512]{1,0:T(8,128)(2,1)S(1)} %copy-done, ...), custom_call_target="tpu_custom_call" | custom-call | flops 3000000000 | bytes 1024 | tf_op jit(solution)/shard_map/attend/pallas_call | solution.py:259
  45.1 1.2 collective-permute-done.6.refs_1_
  46.9 1.5 %collective-permute-start.17 = (bf16[2,144,512]{2,1,0:T(8,128)(2,1)S(1)}, bf16[2,144,512]{2,1,0:T(8,128)(2,1)S(1)}, u32[]{:S(2)}, u32[]{:S(2)}) collective-permute-start(bf16[2,144,512]{2,1,0:T(8,128)(2,1)S(1)} %collective-permute-done.9.refs_4_), channel_id=1, source_target_pairs={{0,8},{1,9},{2,10},{3,11},{4,12},{5,13},{6,14},{7,15},{8,0},{9,1},... | collective-permute-start | bytes 884744 | tf_op jit(solution)/shard_map/ppermute | solution.py:706
  48.4 5.1 %attend.3 = (bf16[1024,512]{1,0:T(8,128)(2,1)S(1)}, bf16[1024,512]{1,0:T(8,128)(2,1)S(1)}, bf16[1024,512]{1,0:T(8,128)(2,1)S(1)}, bf16[1024,512]{1,0:T(8,128)(2,1)S(1)}, f32[24,512]{1,0:T(8,128)}) custom-call(s32[2]{0:T(128)S(1)} %pad_add_fusion.ids_ref, ...), custom_call_target="tpu_custom_call", output_to_operand_aliasing={{0}: (11, {}), {1}: (12, {}), {2}: (13, {}), {3}: (14, {})} | custom-call | flops 1000000000 | bytes 1024 | tf_op jit(solution)/shard_map/attend/pallas_call | solution.py:259
  57.7 25.5 %middle.1 = (bf16[1024,512]{1,0:T(8,128)(2,1)}, f32[1024,512]{1,0:T(8,128)}, f32[1024,512]{1,0:T(8,128)}, bf16[1024,512]{1,0:T(8,128)(2,1)S(1)}, f32[16,512]{1,0...) custom-call(s32[2]{0:T(128)S(1)} %pad_add_fusion.ids_ref, ...), custom_call_target="tpu_custom_call" | custom-call | flops 7249999872 | bytes 1024 | tf_op jit(solution)/shard_map/middle/pallas_call | solution.py:650
  83.4 4.5 %first_back.1 = (bf16[1024,128]{1,0:T(8,128)(2,1)S(1)}, bf16[1024,128]{1,0:T(8,128)(2,1)S(1)}, bf16[1024,128]{1,0:T(8,128)(2,1)S(1)}) custom-call(s32[1,16]{1,0:T(1,128)S(1)} %copy-done.2, bf16[1024,512]{1,0:T(8,128)(2,1)S(1)} %get-tuple-element.138.refs_0_, bf16[1024,512]{1,0:T(8,128)(2,1)S(1)} %get-tuple-element.139.refs_1_, ...), custom_call_target="tpu_custom_call" | custom-call | flops 1500000000 | bytes 1024 | tf_op jit(solution)/shard_map/first_back/pallas_call | solution.py:333
  89.1 1.6 %collective-permute-start.26 = (bf16[2,2,144,512]{3,2,1,0:T(8,128)(2,1)S(1)}, bf16[2,2,144,512]{3,2,1,0:T(8,128)(2,1)S(1)}, u32[]{:S(2)}, u32[]{:S(2)}) collective-permute-start(bf16[2,2,144,512]{3,2,1,0:T(8,128)(2,1)S(1)} %get-tuple-element.147), channel_id=1, source_target_pairs={{0,8},{1,9},{2,10},{3,11},{4,12},{5,13},{6,14},{7,15},{8,0},{9,1},... | collective-permute-start | bytes 1769480 | tf_op jit(solution)/shard_map/ppermute | solution.py:706
  90.7 1.4 %collective-permute-start.27 = (bf16[2,2,144,512]{3,2,1,0:T(8,128)(2,1)S(1)}, bf16[2,2,144,512]{3,2,1,0:T(8,128)(2,1)S(1)}, u32[]{:S(2)}, u32[]{:S(2)}) collective-permute-start(bf16[2,2,144,512]{3,2,1,0:T(8,128)(2,1)S(1)} %get-tuple-element.148), channel_id=1, source_target_pairs={{0,16},{1,17},{2,18},{3,19},{4,20},{5,21},{6,22},{7,23},{8,24},{9,... | collective-permute-start | bytes 1769480 | tf_op jit(solution)/shard_map/ppermute | solution.py:706
  92.1 13.2 %rest_back.1.grads_ref = bf16[3,1024,512]{2,1,0:T(8,128)(2,1)S(1)} custom-call(s32[1,16]{1,0:T(1,128)S(1)} %copy-done.2, bf16[1024,512]{1,0:T(8,128)(2,1)S(1)} %get-tuple-element.138.refs_0_, bf16[1024,512]{1,0:T(8,128)(2,1)S(1)} %get-tuple-element.139.refs_1_, bf16[1024,512]{1,0:T(8,128)(2,1)S(1)} %get-tuple-element.140.refs_2_, ...), custom_call_target="tpu_custom_call" | custom-call | flops 3500000000 | bytes 1024 | tf_op jit(solution)/shard_map/rest_back/pallas_call | solution.py:368
  106.4 1.5 %collective-permute-start.28 = (bf16[2,144,512]{2,1,0:T(8,128)(2,1)S(1)}, bf16[2,144,512]{2,1,0:T(8,128)(2,1)S(1)}, u32[]{:S(2)}, u32[]{:S(2)}) collective-permute-start(bf16[2,144,512]{2,1,0:T(8,128)(2,1)S(1)} %get-tuple-element.158), channel_id=1, source_target_pairs={{0,16},{1,17},{2,18},{3,19},{4,20},{5,21},{6,22},{7,23},{8,24},{9,... | collective-permute-start | bytes 884744 | tf_op jit(solution)/shard_map/ppermute | solution.py:706
  108.4 3.6 %weights.1 = (bf16[4,4,56,512]{3,2,1,0:T(8,128)(2,1)S(1)}, bf16[4,4,56,512]{3,2,1,0:T(8,128)(2,1)S(1)}) custom-call(s32[2]{0:T(128)S(1)} %pad_add_fusion.ids_ref, bf16[3,1024,512]{2,1,0:T(8,128)(2,1)S(1)} %rest_back.1.grads_ref, bf16[1024,512]{1,0:T(8,128)(2,1)S(1)} %copy-done, f32[16,512]{1,0:T(8,128)S(1)} %get-tuple-element.161.sums_ref), custom_call_target="tpu_custom_call" | custom-call | flops 1000000000 | bytes 1024 | tf_op jit(solution)/shard_map/weights/pallas_call | solution.py:430
  112.0 2.6 %collective-permute-done.28 = bf16[2,144,512]{2,1,0:T(8,128)(2,1)S(1)} collective-permute-done((bf16[2,144,512]{2,1,0:T(8,128)(2,1)S(1)}, bf16[2,144,512]{2,1,0:T(8,128)(2,1)S(1)}, u32[]{:S(2)}, u32[]{:S(2)}) %collective-permute-start.28) | collective-permute-done | bytes 294944 | tf_op jit(solution)/shard_map/ppermute | solution.py:706
  114.6 1.1 collective-permute-done.29
  115.9 2.3 %collective-permute-done.30 = bf16[4,4,56,512]{3,2,1,0:T(8,128)(2,1)S(1)} collective-permute-done((bf16[4,4,56,512]{3,2,1,0:T(8,128)(2,1)S(1)}, bf16[4,4,56,512]{3,2,1,0:T(8,128)(2,1)S(1)}, u32[]{:S(2)}, u32[]{:S(2)}) %collective-permute-start.30) | collective-permute-done | bytes 917536 | tf_op jit(solution)/shard_map/ppermute | solution.py:706
  119.7 2.3 %collective-permute-start.33 = (bf16[4,56,512]{2,1,0:T(8,128)(2,1)S(1)}, bf16[4,56,512]{2,1,0:T(8,128)(2,1)S(1)}, u32[]{:S(2)}, u32[]{:S(2)}) collective-permute-start(bf16[4,56,512]{2,1,0:T(8,128)(2,1)S(1)} %get-tuple-element.168), channel_id=1, source_target_pairs={{0,24},{1,25},{2,26},{3,27},{4,28},{5,29},{6,30},{7,31},{8,16},{9,... | collective-permute-start | bytes 688136 | tf_op jit(solution)/shard_map/ppermute | solution.py:706
  122.1 1.8 %collective-permute-start.36 = (bf16[1,144,512]{2,1,0:T(8,128)(2,1)S(1)}, bf16[1,144,512]{2,1,0:T(8,128)(2,1)S(1)}, u32[]{:S(2)}, u32[]{:S(2)}) collective-permute-start(bf16[1,144,512]{2,1,0:T(8,128)(2,1)S(1)} %get-tuple-element.201), channel_id=1, source_target_pairs={{0,6},{1,7},{2,4},{3,5},{4,2},{5,3},{6,0},{7,1},{8,14},{9,15},{10,... | collective-permute-start | bytes 442376 | tf_op jit(solution)/shard_map/ppermute | solution.py:706
  124.7 4.8 %input.1 = f32[1024,512]{1,0:T(8,128)} custom-call(s32[2]{0:T(128)S(1)} %pad_add_fusion.ids_ref, f32[1024,512]{1,0:T(8,128)S(1)} %copy-done.1, bf16[3,1024,512]{2,1,0:T(8,128)(2,1)S(1)} %rest_back.1.grads_ref, bf16[4,56,512]{2,1,0:T(8,128)(2,1)S(1)} %constant_dynamic-update-slice_fusion.refs_0_, bf16[4,56,512]{2,1,0:T(8,128)(2,1)S(1)} %collective-permute-done.10.refs_1_, ...), custom_call_target="tpu_custom_call" | custom-call | flops 1250000000 | bytes 1024 | tf_op jit(solution)/shard_map/input/pallas_call | solution.py:472
  129.6 1.9 %collective-permute-start.34 = (bf16[1,144,512]{2,1,0:T(8,128)(2,1)S(1)}, bf16[1,144,512]{2,1,0:T(8,128)(2,1)S(1)}, u32[]{:S(2)}, u32[]{:S(2)}) collective-permute-start(bf16[1,144,512]{2,1,0:T(8,128)(2,1)S(1)} %get-tuple-element.181), channel_id=1, source_target_pairs={{0,2},{1,3},{2,0},{3,1},{4,6},{5,7},{6,4},{7,5},{8,10},{9,11},{10,... | collective-permute-start | bytes 442376 | tf_op jit(solution)/shard_map/ppermute | solution.py:706
  131.7 4.4 %collective-permute-start.37 = (bf16[1,56,512]{2,1,0:T(8,128)(2,1)S(1)}, bf16[1,56,512]{2,1,0:T(8,128)(2,1)S(1)}, u32[]{:S(2)}, u32[]{:S(2)}) collective-permute-start(bf16[1,56,512]{2,1,0:T(8,128)(2,1)S(1)} %get-tuple-element.182), channel_id=1, source_target_pairs={{0,2},{1,3},{2,0},{3,1},{4,6},{5,7},{6,4},{7,5},{8,10},{9,11},{10,... | collective-permute-start | bytes 172040 | tf_op jit(solution)/shard_map/ppermute | solution.py:706
  136.4 2.1 %collective-permute-start.39 = (bf16[1,56,512]{2,1,0:T(8,128)(2,1)S(1)}, bf16[1,56,512]{2,1,0:T(8,128)(2,1)S(1)}, u32[]{:S(2)}, u32[]{:S(2)}) collective-permute-start(bf16[1,56,512]{2,1,0:T(8,128)(2,1)S(1)} %get-tuple-element.188), channel_id=1, source_target_pairs={{0,6},{1,7},{2,4},{3,5},{4,2},{5,3},{6,0},{7,1},{8,14},{9,15},{10,... | collective-permute-start | bytes 172040 | tf_op jit(solution)/shard_map/ppermute | solution.py:706
  138.9 1.2 collective-permute-done.37
  (103 shorter events, 21.2 us)
Async XLA Ops:
  2.4 8.4 %collective-permute-start.2 = (bf16[1,56,512]{2,1,0:T(8,128)(2,1)}, bf16[1,56,512]{2,1,0:T(8,128)(2,1)S(1)}, u32[]{:S(2)}, u32[]{:S(2)}) collective-permute-start(bf16[1,56,512]{2,1,0:T(8,128)(2,1)} %bitcast.92), channel_id=1, source_target_pairs={{0,4},{1,5},{2,6},{3,7},{4,0},{5,1},{6,2},{7,3},{8,12},{9,13},{10,... | collective-permute-start | bytes 172040 | tf_op jit(solution)/shard_map/ppermute | solution.py:706
  6.4 4.4 %collective-permute-start.1 = (bf16[1,56,512]{2,1,0:T(8,128)(2,1)}, bf16[1,56,512]{2,1,0:T(8,128)(2,1)S(1)}, u32[]{:S(2)}, u32[]{:S(2)}) collective-permute-start(bf16[1,56,512]{2,1,0:T(8,128)(2,1)} %bitcast.93), channel_id=1, source_target_pairs={{0,2},{1,3},{2,0},{3,1},{4,6},{5,7},{6,4},{7,5},{8,10},{9,11},{10,... | collective-permute-start | bytes 172040 | tf_op jit(solution)/shard_map/ppermute | solution.py:706
  8.0 6.8 %collective-permute-start.3 = (bf16[1,56,512]{2,1,0:T(8,128)(2,1)}, bf16[1,56,512]{2,1,0:T(8,128)(2,1)S(1)}, u32[]{:S(2)}, u32[]{:S(2)}) collective-permute-start(bf16[1,56,512]{2,1,0:T(8,128)(2,1)} %bitcast.94), channel_id=1, source_target_pairs={{0,6},{1,7},{2,4},{3,5},{4,2},{5,3},{6,0},{7,1},{8,14},{9,15},{10,... | collective-permute-start | bytes 172040 | tf_op jit(solution)/shard_map/ppermute | solution.py:706
  8.0 11.3 %collective-permute-start = (bf16[1,144,512]{2,1,0:T(8,128)(2,1)}, bf16[1,144,512]{2,1,0:T(8,128)(2,1)S(1)}, u32[]{:S(2)}, u32[]{:S(2)}) collective-permute-start(bf16[1,144,512]{2,1,0:T(8,128)(2,1)} %bitcast.91), channel_id=1, source_target_pairs={{0,4},{1,5},{2,6},{3,7},{4,0},{5,1},{6,2},{7,3},{8,12},{9,13},{10,... | collective-permute-start | bytes 442376 | tf_op jit(solution)/shard_map/ppermute | solution.py:706
  14.8 8.7 %collective-permute-start.12 = (bf16[4,56,512]{2,1,0:T(8,128)(2,1)S(1)}, bf16[4,56,512]{2,1,0:T(8,128)(2,1)S(1)}, u32[]{:S(2)}, u32[]{:S(2)}) collective-permute-start(bf16[4,56,512]{2,1,0:T(8,128)(2,1)S(1)} %constant_dynamic-update-slice_fusion.refs_0_), channel_id=1, source_target_pairs={{0,24},{1,25},{2,26},{3,27},{4,28},{5,29},{6,30},{7,31},{8,16},{9,... | collective-permute-start | bytes 688136 | tf_op jit(solution)/shard_map/ppermute | solution.py:706
  17.3 8.5 %collective-permute-start.11 = (bf16[4,56,512]{2,1,0:T(8,128)(2,1)S(1)}, bf16[4,56,512]{2,1,0:T(8,128)(2,1)S(1)}, u32[]{:S(2)}, u32[]{:S(2)}) collective-permute-start(bf16[4,56,512]{2,1,0:T(8,128)(2,1)S(1)} %constant_dynamic-update-slice_fusion.refs_0_), channel_id=1, source_target_pairs={{0,16},{1,17},{2,18},{3,19},{4,20},{5,21},{6,22},{7,23},{8,24},{9,... | collective-permute-start | bytes 688136 | tf_op jit(solution)/shard_map/ppermute | solution.py:706
  17.8 8.1 %collective-permute-start.10 = (bf16[4,56,512]{2,1,0:T(8,128)(2,1)S(1)}, bf16[4,56,512]{2,1,0:T(8,128)(2,1)S(1)}, u32[]{:S(2)}, u32[]{:S(2)}) collective-permute-start(bf16[4,56,512]{2,1,0:T(8,128)(2,1)S(1)} %constant_dynamic-update-slice_fusion.refs_0_), channel_id=1, source_target_pairs={{0,8},{1,9},{2,10},{3,11},{4,12},{5,13},{6,14},{7,15},{8,0},{9,1},... | collective-permute-start | bytes 688136 | tf_op jit(solution)/shard_map/ppermute | solution.py:706
  19.8 10.3 %collective-permute-start.5 = (bf16[2,144,512]{2,1,0:T(8,128)(2,1)S(1)}, bf16[2,144,512]{2,1,0:T(8,128)(2,1)S(1)}, u32[]{:S(2)}, u32[]{:S(2)}) collective-permute-start(bf16[2,144,512]{2,1,0:T(8,128)(2,1)S(1)} %constant_dynamic-update-slice_fusion.4), channel_id=1, source_target_pairs={{0,2},{1,3},{2,0},{3,1},{4,6},{5,7},{6,4},{7,5},{8,10},{9,11},{10,... | collective-permute-start | bytes 884744 | tf_op jit(solution)/shard_map/ppermute | solution.py:706
  23.4 9.8 %collective-permute-start.15 = (bf16[4,56,512]{2,1,0:T(8,128)(2,1)S(1)}, bf16[4,56,512]{2,1,0:T(8,128)(2,1)S(1)}, u32[]{:S(2)}, u32[]{:S(2)}) collective-permute-start(bf16[4,56,512]{2,1,0:T(8,128)(2,1)S(1)} %collective-permute-done.12.refs_3_), channel_id=1, source_target_pairs={{0,1},{1,0},{2,3},{3,2},{4,5},{5,4},{6,7},{7,6},{8,9},{9,8},{10,11... | collective-permute-start | bytes 688136 | tf_op jit(solution)/shard_map/ppermute | solution.py:706
  25.8 8.0 %collective-permute-start.14 = (bf16[4,56,512]{2,1,0:T(8,128)(2,1)S(1)}, bf16[4,56,512]{2,1,0:T(8,128)(2,1)S(1)}, u32[]{:S(2)}, u32[]{:S(2)}) collective-permute-start(bf16[4,56,512]{2,1,0:T(8,128)(2,1)S(1)} %collective-permute-done.11.refs_2_), channel_id=1, source_target_pairs={{0,1},{1,0},{2,3},{3,2},{4,5},{5,4},{6,7},{7,6},{8,9},{9,8},{10,11... | collective-permute-start | bytes 688136 | tf_op jit(solution)/shard_map/ppermute | solution.py:706
  25.9 8.5 %collective-permute-start.13 = (bf16[4,56,512]{2,1,0:T(8,128)(2,1)S(1)}, bf16[4,56,512]{2,1,0:T(8,128)(2,1)S(1)}, u32[]{:S(2)}, u32[]{:S(2)}) collective-permute-start(bf16[4,56,512]{2,1,0:T(8,128)(2,1)S(1)} %collective-permute-done.10.refs_1_), channel_id=1, source_target_pairs={{0,1},{1,0},{2,3},{3,2},{4,5},{5,4},{6,7},{7,6},{8,9},{9,8},{10,11... | collective-permute-start | bytes 688136 | tf_op jit(solution)/shard_map/ppermute | solution.py:706
  30.2 14.7 %collective-permute-start.9 = (bf16[2,144,512]{2,1,0:T(8,128)(2,1)S(1)}, bf16[2,144,512]{2,1,0:T(8,128)(2,1)S(1)}, u32[]{:S(2)}, u32[]{:S(2)}) collective-permute-start(bf16[2,144,512]{2,1,0:T(8,128)(2,1)S(1)} %get-tuple-element.210), channel_id=1, source_target_pairs={{0,16},{1,17},{2,18},{3,19},{4,20},{5,21},{6,22},{7,23},{8,24},{9,... | collective-permute-start | bytes 884744 | tf_op jit(solution)/shard_map/ppermute | solution.py:706
  31.8 13.2 %collective-permute-start.7 = (bf16[2,144,512]{2,1,0:T(8,128)(2,1)S(1)}, bf16[2,144,512]{2,1,0:T(8,128)(2,1)S(1)}, u32[]{:S(2)}, u32[]{:S(2)}) collective-permute-start(bf16[2,144,512]{2,1,0:T(8,128)(2,1)S(1)} %get-tuple-element.210), channel_id=1, source_target_pairs={{0,8},{1,9},{2,10},{3,11},{4,12},{5,13},{6,14},{7,15},{8,0},{9,1},... | collective-permute-start | bytes 884744 | tf_op jit(solution)/shard_map/ppermute | solution.py:706
  33.3 11.8 %collective-permute-start.8 = (bf16[2,144,512]{2,1,0:T(8,128)(2,1)S(1)}, bf16[2,144,512]{2,1,0:T(8,128)(2,1)S(1)}, u32[]{:S(2)}, u32[]{:S(2)}) collective-permute-start(bf16[2,144,512]{2,1,0:T(8,128)(2,1)S(1)} %get-tuple-element.211), channel_id=1, source_target_pairs={{0,16},{1,17},{2,18},{3,19},{4,20},{5,21},{6,22},{7,23},{8,24},{9,... | collective-permute-start | bytes 884744 | tf_op jit(solution)/shard_map/ppermute | solution.py:706
  33.8 12.6 %collective-permute-start.6 = (bf16[2,144,512]{2,1,0:T(8,128)(2,1)S(1)}, bf16[2,144,512]{2,1,0:T(8,128)(2,1)S(1)}, u32[]{:S(2)}, u32[]{:S(2)}) collective-permute-start(bf16[2,144,512]{2,1,0:T(8,128)(2,1)S(1)} %get-tuple-element.211), channel_id=1, source_target_pairs={{0,8},{1,9},{2,10},{3,11},{4,12},{5,13},{6,14},{7,15},{8,0},{9,1},... | collective-permute-start | bytes 884744 | tf_op jit(solution)/shard_map/ppermute | solution.py:706
  46.4 7.3 %collective-permute-start.16 = (bf16[2,144,512]{2,1,0:T(8,128)(2,1)S(1)}, bf16[2,144,512]{2,1,0:T(8,128)(2,1)S(1)}, u32[]{:S(2)}, u32[]{:S(2)}) collective-permute-start(bf16[2,144,512]{2,1,0:T(8,128)(2,1)S(1)} %collective-permute-done.6.refs_1_), channel_id=1, source_target_pairs={{0,16},{1,17},{2,18},{3,19},{4,20},{5,21},{6,22},{7,23},{8,24},{9,... | collective-permute-start | bytes 884744 | tf_op jit(solution)/shard_map/ppermute | solution.py:706
  46.9 7.1 %collective-permute-start.17 = (bf16[2,144,512]{2,1,0:T(8,128)(2,1)S(1)}, bf16[2,144,512]{2,1,0:T(8,128)(2,1)S(1)}, u32[]{:S(2)}, u32[]{:S(2)}) collective-permute-start(bf16[2,144,512]{2,1,0:T(8,128)(2,1)S(1)} %collective-permute-done.9.refs_4_), channel_id=1, source_target_pairs={{0,8},{1,9},{2,10},{3,11},{4,12},{5,13},{6,14},{7,15},{8,0},{9,1},... | collective-permute-start | bytes 884744 | tf_op jit(solution)/shard_map/ppermute | solution.py:706
  48.4 6.7 %collective-permute-start.18 = (bf16[4,144,512]{2,1,0:T(8,128)(2,1)S(1)}, bf16[4,144,512]{2,1,0:T(8,128)(2,1)S(1)}, u32[]{:S(2)}, u32[]{:S(2)}) collective-permute-start(bf16[4,144,512]{2,1,0:T(8,128)(2,1)S(1)} %bitcast.89), channel_id=1, source_target_pairs={{0,1},{1,0},{2,3},{3,2},{4,5},{5,4},{6,7},{7,6},{8,9},{9,8},{10,11... | collective-permute-start | bytes 1769480 | tf_op jit(solution)/shard_map/ppermute | solution.py:706
  83.2 4.8 %collective-permute-start.25 = (bf16[4,4,144,512]{3,2,1,0:T(8,128)(2,1)}, bf16[4,4,144,512]{3,2,1,0:T(8,128)(2,1)S(1)}, u32[]{:S(2)}, u32[]{:S(2)}) collective-permute-start(bf16[4,4,144,512]{3,2,1,0:T(8,128)(2,1)} %get-tuple-element.137), channel_id=1, source_target_pairs={{0,1},{1,0},{2,3},{3,2},{4,5},{5,4},{6,7},{7,6},{8,9},{9,8},{10,11... | collective-permute-start | bytes 7077896 | tf_op jit(solution)/shard_map/ppermute | solution.py:706
  89.1 16.2 %collective-permute-start.26 = (bf16[2,2,144,512]{3,2,1,0:T(8,128)(2,1)S(1)}, bf16[2,2,144,512]{3,2,1,0:T(8,128)(2,1)S(1)}, u32[]{:S(2)}, u32[]{:S(2)}) collective-permute-start(bf16[2,2,144,512]{3,2,1,0:T(8,128)(2,1)S(1)} %get-tuple-element.147), channel_id=1, source_target_pairs={{0,8},{1,9},{2,10},{3,11},{4,12},{5,13},{6,14},{7,15},{8,0},{9,1},... | collective-permute-start | bytes 1769480 | tf_op jit(solution)/shard_map/ppermute | solution.py:706
  90.7 15.3 %collective-permute-start.27 = (bf16[2,2,144,512]{3,2,1,0:T(8,128)(2,1)S(1)}, bf16[2,2,144,512]{3,2,1,0:T(8,128)(2,1)S(1)}, u32[]{:S(2)}, u32[]{:S(2)}) collective-permute-start(bf16[2,2,144,512]{3,2,1,0:T(8,128)(2,1)S(1)} %get-tuple-element.148), channel_id=1, source_target_pairs={{0,16},{1,17},{2,18},{3,19},{4,20},{5,21},{6,22},{7,23},{8,24},{9,... | collective-permute-start | bytes 1769480 | tf_op jit(solution)/shard_map/ppermute | solution.py:706
  106.4 8.2 %collective-permute-start.28 = (bf16[2,144,512]{2,1,0:T(8,128)(2,1)S(1)}, bf16[2,144,512]{2,1,0:T(8,128)(2,1)S(1)}, u32[]{:S(2)}, u32[]{:S(2)}) collective-permute-start(bf16[2,144,512]{2,1,0:T(8,128)(2,1)S(1)} %get-tuple-element.158), channel_id=1, source_target_pairs={{0,16},{1,17},{2,18},{3,19},{4,20},{5,21},{6,22},{7,23},{8,24},{9,... | collective-permute-start | bytes 884744 | tf_op jit(solution)/shard_map/ppermute | solution.py:706
  107.9 7.8 %collective-permute-start.29 = (bf16[2,144,512]{2,1,0:T(8,128)(2,1)S(1)}, bf16[2,144,512]{2,1,0:T(8,128)(2,1)S(1)}, u32[]{:S(2)}, u32[]{:S(2)}) collective-permute-start(bf16[2,144,512]{2,1,0:T(8,128)(2,1)S(1)} %get-tuple-element.159), channel_id=1, source_target_pairs={{0,8},{1,9},{2,10},{3,11},{4,12},{5,13},{6,14},{7,15},{8,0},{9,1},... | collective-permute-start | bytes 884744 | tf_op jit(solution)/shard_map/ppermute | solution.py:706
  118.4 11.2 %collective-permute-start.31 = (bf16[4,56,512]{2,1,0:T(8,128)(2,1)S(1)}, bf16[4,56,512]{2,1,0:T(8,128)(2,1)S(1)}, u32[]{:S(2)}, u32[]{:S(2)}) collective-permute-start(bf16[4,56,512]{2,1,0:T(8,128)(2,1)S(1)} %get-tuple-element.166), channel_id=1, source_target_pairs={{0,8},{1,9},{2,10},{3,11},{4,12},{5,13},{6,14},{7,15},{8,0},{9,1},... | collective-permute-start | bytes 688136 | tf_op jit(solution)/shard_map/ppermute | solution.py:706
  119.1 12.4 %collective-permute-start.32 = (bf16[4,56,512]{2,1,0:T(8,128)(2,1)S(1)}, bf16[4,56,512]{2,1,0:T(8,128)(2,1)S(1)}, u32[]{:S(2)}, u32[]{:S(2)}) collective-permute-start(bf16[4,56,512]{2,1,0:T(8,128)(2,1)S(1)} %get-tuple-element.167), channel_id=1, source_target_pairs={{0,16},{1,17},{2,18},{3,19},{4,20},{5,21},{6,22},{7,23},{8,24},{9,... | collective-permute-start | bytes 688136 | tf_op jit(solution)/shard_map/ppermute | solution.py:706
  119.7 11.8 %collective-permute-start.33 = (bf16[4,56,512]{2,1,0:T(8,128)(2,1)S(1)}, bf16[4,56,512]{2,1,0:T(8,128)(2,1)S(1)}, u32[]{:S(2)}, u32[]{:S(2)}) collective-permute-start(bf16[4,56,512]{2,1,0:T(8,128)(2,1)S(1)} %get-tuple-element.168), channel_id=1, source_target_pairs={{0,24},{1,25},{2,26},{3,27},{4,28},{5,29},{6,30},{7,31},{8,16},{9,... | collective-permute-start | bytes 688136 | tf_op jit(solution)/shard_map/ppermute | solution.py:706
  122.1 9.6 %collective-permute-start.36 = (bf16[1,144,512]{2,1,0:T(8,128)(2,1)S(1)}, bf16[1,144,512]{2,1,0:T(8,128)(2,1)S(1)}, u32[]{:S(2)}, u32[]{:S(2)}) collective-permute-start(bf16[1,144,512]{2,1,0:T(8,128)(2,1)S(1)} %get-tuple-element.201), channel_id=1, source_target_pairs={{0,6},{1,7},{2,4},{3,5},{4,2},{5,3},{6,0},{7,1},{8,14},{9,15},{10,... | collective-permute-start | bytes 442376 | tf_op jit(solution)/shard_map/ppermute | solution.py:706
  123.9 14.7 %collective-permute-start.35 = (bf16[1,144,512]{2,1,0:T(8,128)(2,1)S(1)}, bf16[1,144,512]{2,1,0:T(8,128)(2,1)S(1)}, u32[]{:S(2)}, u32[]{:S(2)}) collective-permute-start(bf16[1,144,512]{2,1,0:T(8,128)(2,1)S(1)} %get-tuple-element.203), channel_id=1, source_target_pairs={{0,4},{1,5},{2,6},{3,7},{4,0},{5,1},{6,2},{7,3},{8,12},{9,13},{10,... | collective-permute-start | bytes 442376 | tf_op jit(solution)/shard_map/ppermute | solution.py:706
  129.6 9.3 %collective-permute-start.34 = (bf16[1,144,512]{2,1,0:T(8,128)(2,1)S(1)}, bf16[1,144,512]{2,1,0:T(8,128)(2,1)S(1)}, u32[]{:S(2)}, u32[]{:S(2)}) collective-permute-start(bf16[1,144,512]{2,1,0:T(8,128)(2,1)S(1)} %get-tuple-element.181), channel_id=1, source_target_pairs={{0,2},{1,3},{2,0},{3,1},{4,6},{5,7},{6,4},{7,5},{8,10},{9,11},{10,... | collective-permute-start | bytes 442376 | tf_op jit(solution)/shard_map/ppermute | solution.py:706
  131.7 8.4 %collective-permute-start.37 = (bf16[1,56,512]{2,1,0:T(8,128)(2,1)S(1)}, bf16[1,56,512]{2,1,0:T(8,128)(2,1)S(1)}, u32[]{:S(2)}, u32[]{:S(2)}) collective-permute-start(bf16[1,56,512]{2,1,0:T(8,128)(2,1)S(1)} %get-tuple-element.182), channel_id=1, source_target_pairs={{0,2},{1,3},{2,0},{3,1},{4,6},{5,7},{6,4},{7,5},{8,10},{9,11},{10,... | collective-permute-start | bytes 172040 | tf_op jit(solution)/shard_map/ppermute | solution.py:706
  136.1 6.1 %collective-permute-start.38 = (bf16[1,56,512]{2,1,0:T(8,128)(2,1)S(1)}, bf16[1,56,512]{2,1,0:T(8,128)(2,1)S(1)}, u32[]{:S(2)}, u32[]{:S(2)}) collective-permute-start(bf16[1,56,512]{2,1,0:T(8,128)(2,1)S(1)} %get-tuple-element.187), channel_id=1, source_target_pairs={{0,4},{1,5},{2,6},{3,7},{4,0},{5,1},{6,2},{7,3},{8,12},{9,13},{10,... | collective-permute-start | bytes 172040 | tf_op jit(solution)/shard_map/ppermute | solution.py:706
  136.4 6.1 %collective-permute-start.39 = (bf16[1,56,512]{2,1,0:T(8,128)(2,1)S(1)}, bf16[1,56,512]{2,1,0:T(8,128)(2,1)S(1)}, u32[]{:S(2)}, u32[]{:S(2)}) collective-permute-start(bf16[1,56,512]{2,1,0:T(8,128)(2,1)S(1)} %get-tuple-element.188), channel_id=1, source_target_pairs={{0,6},{1,7},{2,4},{3,5},{4,2},{5,3},{6,0},{7,1},{8,14},{9,15},{10,... | collective-permute-start | bytes 172040 | tf_op jit(solution)/shard_map/ppermute | solution.py:706
  (14 other events, 62.0 us)

commit v5 on v4

--- a/solution.py
+++ b/solution.py
@@ -920,9 +920,14 @@
             (1, 1): links.swap(halves[1], across),
         }
         *attended, table = attending(0, pairs - 1)
-        received, attended = lax.optimization_barrier((received, attended))
-        received[3, 0] = links.swap(received[1, 0], along)
-        received[3, 1] = links.swap(received[2, 1], across)
+        passing = received[1, 0], received[2, 1]
+        passing, attended = lax.optimization_barrier((passing, attended))
+        received[1, 0], received[2, 1] = passing
+        received[3, 0] = links.swap(passing[0], along)
+        received[3, 1] = links.swap(passing[1], across)
+        direct_ones = received[2, 0], received[1, 1]
+        direct_ones, attended = lax.optimization_barrier((direct_ones, attended))
+        received[2, 0], received[1, 1] = direct_ones
         *attended, _ = attending(pairs - 1, 1, attended)
         received, attended = lax.optimization_barrier((received, attended))
         late_parts = [late] + [received[k, half] for k in (1, 2, 3) for half in (0, 1)]

time: 144 us -> 144 us (level)
  transfers between devices with their start and end apart: 40 -> 40, of which waited for: 25 -> 23; matrix products, arithmetic and copies ran while one was open for 3% -> 3% of each run, Pallas kernels for 29% -> 29%
where the time goes in v5:
time: 144 us; the launch traced here: 143 us
  Pallas kernels  69 us (48%)
  starting transfers between devices  40.7 us (28%)
  waiting for transfers between devices  24.6 us (17%)
  local copies, waits for them, and re-layouts  5.25 us (4%)
  other arithmetic  2.72 us (2%)
    ppermute x40, starting transfers between devices, swap(): lax.ppermute(values, AXES, [(i, i ^ distance) for i in range(self.count)])  40.7 us
    pallas_call x1, Pallas kernels, middle(): call(middle_kernel, 'middle', 29, 44, grid=(length // TILE,), in_specs=[S...  25.5 us
    ppermute x40, waiting for transfers between devices, swap(): lax.ppermute(values, AXES, [(i, i ^ distance) for i in range(self.count)])  24.6 us
    pallas_call x2, Pallas kernels, attend(): call(functools.partial(attend_kernel, size, tail_size, first), 'attend',...  15.6 us
    pallas_call x1, Pallas kernels, rest_back(): call(functools.partial(rest_back_kernel, size), 'rest_back', 14, 28, grid...  13.2 us
    pallas_call x1, Pallas kernels, input_grad(): call(input_kernel, 'input', 5, 14, grid=(length // BLOCK,), in_specs=[SCA...  4.82 us
    pallas_call x1, Pallas kernels, first_back(): call(functools.partial(first_back_kernel, size), 'first_back', 6, 16, gri...  4.53 us
    pallas_call x1, Pallas kernels, weight_grads(): call(functools.partial(weights_kernel, tail), 'weights', 4, 16, grid=(3,)...  3.57 us
  transfers between devices with their start and end apart: 40, of which 23 were waited for; matrix products, arithmetic and copies ran while one was open for 3% of the time, Pallas kernels for 29%

profile of v5, /device:TPU:0, one launch (start us, length us, event | category | flops | bytes accessed | tf_op | source)
XLA Modules:
  0.0 143.3 jit_solution(18096360466762642100)
XLA Ops:
  0.7 1.7 %pack.1 = (bf16[56,512]{1,0:T(8,128)(2,1)}, bf16[144,512]{1,0:T(8,128)(2,1)}) custom-call(bf16[16,512]{1,0:T(8,128)(2,1)} %query.1, bf16[16,512]{1,0:T(8,128)(2,1)} %key.1, bf16[16,512]{1,0:T(8,128)(2,1)} %value.1, bf16[16,512]{1,0:T(8,128)(2,1)} %output.1, bf16[16,2048]{1,0:T(8,128)(2,1)} %up.1, bf16[64,512]{1,0:T(8,128)(2,1)} %down.1, ...), custom_call_target="tpu_custom_call" | custom-call | flops 250000000 | bytes 1024 | tf_op jit(solution)/shard_map/pack/pallas_call | solution.py:790
  2.4 4.0 %collective-permute-start.2 = (bf16[1,56,512]{2,1,0:T(8,128)(2,1)}, bf16[1,56,512]{2,1,0:T(8,128)(2,1)S(1)}, u32[]{:S(2)}, u32[]{:S(2)}) collective-permute-start(bf16[1,56,512]{2,1,0:T(8,128)(2,1)} %bitcast.92), channel_id=1, source_target_pairs={{0,4},{1,5},{2,6},{3,7},{4,0},{5,1},{6,2},{7,3},{8,12},{9,13},{10,... | collective-permute-start | bytes 172040 | tf_op jit(solution)/shard_map/ppermute | solution.py:706
  6.4 1.6 %collective-permute-start.1 = (bf16[1,56,512]{2,1,0:T(8,128)(2,1)}, bf16[1,56,512]{2,1,0:T(8,128)(2,1)S(1)}, u32[]{:S(2)}, u32[]{:S(2)}) collective-permute-start(bf16[1,56,512]{2,1,0:T(8,128)(2,1)} %bitcast.93), channel_id=1, source_target_pairs={{0,2},{1,3},{2,0},{3,1},{4,6},{5,7},{6,4},{7,5},{8,10},{9,11},{10,... | collective-permute-start | bytes 172040 | tf_op jit(solution)/shard_map/ppermute | solution.py:706
  8.0 1.9 %collective-permute-start = (bf16[1,144,512]{2,1,0:T(8,128)(2,1)}, bf16[1,144,512]{2,1,0:T(8,128)(2,1)S(1)}, u32[]{:S(2)}, u32[]{:S(2)}) collective-permute-start(bf16[1,144,512]{2,1,0:T(8,128)(2,1)} %bitcast.91), channel_id=1, source_target_pairs={{0,4},{1,5},{2,6},{3,7},{4,0},{5,1},{6,2},{7,3},{8,12},{9,13},{10,... | collective-permute-start | bytes 442376 | tf_op jit(solution)/shard_map/ppermute | solution.py:706
  10.8 3.9 %collective-permute-done.3 = bf16[1,56,512]{2,1,0:T(8,128)(2,1)S(1)} collective-permute-done((bf16[1,56,512]{2,1,0:T(8,128)(2,1)}, bf16[1,56,512]{2,1,0:T(8,128)(2,1)S(1)}, u32[]{:S(2)}, u32[]{:S(2)}) %collective-permute-start.3) | collective-permute-done | bytes 57376 | tf_op jit(solution)/shard_map/ppermute | solution.py:706
  14.8 2.5 %collective-permute-start.10 = (bf16[4,56,512]{2,1,0:T(8,128)(2,1)S(1)}, bf16[4,56,512]{2,1,0:T(8,128)(2,1)S(1)}, u32[]{:S(2)}, u32[]{:S(2)}) collective-permute-start(bf16[4,56,512]{2,1,0:T(8,128)(2,1)S(1)} %constant_dynamic-update-slice_fusion.refs_0_), channel_id=1, source_target_pairs={{0,24},{1,25},{2,26},{3,27},{4,28},{5,29},{6,30},{7,31},{8,16},{9,... | collective-permute-start | bytes 688136 | tf_op jit(solution)/shard_map/ppermute | solution.py:706
  18.3 0.9 constant_dynamic-update-slice_fusion.5
  19.8 3.0 %collective-permute-start.5 = (bf16[2,144,512]{2,1,0:T(8,128)(2,1)S(1)}, bf16[2,144,512]{2,1,0:T(8,128)(2,1)S(1)}, u32[]{:S(2)}, u32[]{:S(2)}) collective-permute-start(bf16[2,144,512]{2,1,0:T(8,128)(2,1)S(1)} %constant_dynamic-update-slice_fusion.4), channel_id=1, source_target_pairs={{0,2},{1,3},{2,0},{3,1},{4,6},{5,7},{6,4},{7,5},{8,10},{9,11},{10,... | collective-permute-start | bytes 884744 | tf_op jit(solution)/shard_map/ppermute | solution.py:706
  23.4 2.3 %collective-permute-done.9.refs_2_ = bf16[4,56,512]{2,1,0:T(8,128)(2,1)S(1)} collective-permute-done((bf16[4,56,512]{2,1,0:T(8,128)(2,1)S(1)}, bf16[4,56,512]{2,1,0:T(8,128)(2,1)S(1)}, u32[]{:S(2)}, u32[]{:S(2)}) %collective-permute-start.9) | collective-permute-done | bytes 229408 | tf_op jit(solution)/shard_map/ppermute | solution.py:706
  26.4 3.7 %collective-permute-done.5 = bf16[2,144,512]{2,1,0:T(8,128)(2,1)S(1)} collective-permute-done((bf16[2,144,512]{2,1,0:T(8,128)(2,1)S(1)}, bf16[2,144,512]{2,1,0:T(8,128)(2,1)S(1)}, u32[]{:S(2)}, u32[]{:S(2)}) %collective-permute-start.5) | collective-permute-done | bytes 294944 | tf_op jit(solution)/shard_map/ppermute | solution.py:706
  30.2 1.6 %collective-permute-start.7 = (bf16[2,144,512]{2,1,0:T(8,128)(2,1)S(1)}, bf16[2,144,512]{2,1,0:T(8,128)(2,1)S(1)}, u32[]{:S(2)}, u32[]{:S(2)}) collective-permute-start(bf16[2,144,512]{2,1,0:T(8,128)(2,1)S(1)} %get-tuple-element.218), channel_id=1, source_target_pairs={{0,16},{1,17},{2,18},{3,19},{4,20},{5,21},{6,22},{7,23},{8,24},{9,... | collective-permute-start | bytes 884744 | tf_op jit(solution)/shard_map/ppermute | solution.py:706
  31.8 1.5 %collective-permute-start.6 = (bf16[2,144,512]{2,1,0:T(8,128)(2,1)S(1)}, bf16[2,144,512]{2,1,0:T(8,128)(2,1)S(1)}, u32[]{:S(2)}, u32[]{:S(2)}) collective-permute-start(bf16[2,144,512]{2,1,0:T(8,128)(2,1)S(1)} %get-tuple-element.219), channel_id=1, source_target_pairs={{0,8},{1,9},{2,10},{3,11},{4,12},{5,13},{6,14},{7,15},{8,0},{9,1},... | collective-permute-start | bytes 884744 | tf_op jit(solution)/shard_map/ppermute | solution.py:706
  34.4 10.5 %attend.2 = (bf16[1024,512]{1,0:T(8,128)(2,1)S(1)}, bf16[1024,512]{1,0:T(8,128)(2,1)S(1)}, bf16[1024,512]{1,0:T(8,128)(2,1)S(1)}, bf16[1024,512]{1,0:T(8,128)(2,1)S(1)}, f32[24,512]{1,0:T(8,128)S(1)}) custom-call(s32[2]{0:T(128)S(1)} %pad_add_fusion.ids_ref, s32[1,16]{1,0:T(1,128)S(1)} %copy-done.2, bf16[1024,512]{1,0:T(8,128)(2,1)S(1)} %copy-done, ...), custom_call_target="tpu_custom_call" | custom-call | flops 3000000000 | bytes 1024 | tf_op jit(solution)/shard_map/attend/pallas_call | solution.py:259
  44.9 1.6 %collective-permute-start.16 = (bf16[2,144,512]{2,1,0:T(8,128)(2,1)S(1)}, bf16[2,144,512]{2,1,0:T(8,128)(2,1)S(1)}, u32[]{:S(2)}, u32[]{:S(2)}) collective-permute-start(bf16[2,144,512]{2,1,0:T(8,128)(2,1)S(1)} %collective-permute-done.6.refs_1_), channel_id=1, source_target_pairs={{0,16},{1,17},{2,18},{3,19},{4,20},{5,21},{6,22},{7,23},{8,24},{9,... | collective-permute-start | bytes 884744 | tf_op jit(solution)/shard_map/ppermute | solution.py:706
  46.5 1.5 %collective-permute-start.17 = (bf16[2,144,512]{2,1,0:T(8,128)(2,1)S(1)}, bf16[2,144,512]{2,1,0:T(8,128)(2,1)S(1)}, u32[]{:S(2)}, u32[]{:S(2)}) collective-permute-start(bf16[2,144,512]{2,1,0:T(8,128)(2,1)S(1)} %collective-permute-done.7.refs_4_), channel_id=1, source_target_pairs={{0,8},{1,9},{2,10},{3,11},{4,12},{5,13},{6,14},{7,15},{8,0},{9,1},... | collective-permute-start | bytes 884744 | tf_op jit(solution)/shard_map/ppermute | solution.py:706
  48.0 5.1 %attend.3 = (bf16[1024,512]{1,0:T(8,128)(2,1)S(1)}, bf16[1024,512]{1,0:T(8,128)(2,1)S(1)}, bf16[1024,512]{1,0:T(8,128)(2,1)S(1)}, bf16[1024,512]{1,0:T(8,128)(2,1)S(1)}, f32[24,512]{1,0:T(8,128)}) custom-call(s32[2]{0:T(128)S(1)} %pad_add_fusion.ids_ref, ...), custom_call_target="tpu_custom_call", output_to_operand_aliasing={{0}: (11, {}), {1}: (12, {}), {2}: (13, {}), {3}: (14, {})} | custom-call | flops 1000000000 | bytes 1024 | tf_op jit(solution)/shard_map/attend/pallas_call | solution.py:259
  57.4 25.5 %middle.1 = (bf16[1024,512]{1,0:T(8,128)(2,1)}, f32[1024,512]{1,0:T(8,128)}, f32[1024,512]{1,0:T(8,128)}, bf16[1024,512]{1,0:T(8,128)(2,1)S(1)}, f32[16,512]{1,0...) custom-call(s32[2]{0:T(128)S(1)} %pad_add_fusion.ids_ref, ...), custom_call_target="tpu_custom_call" | custom-call | flops 7249999872 | bytes 1024 | tf_op jit(solution)/shard_map/middle/pallas_call | solution.py:650
  83.1 4.5 %first_back.1 = (bf16[1024,128]{1,0:T(8,128)(2,1)S(1)}, bf16[1024,128]{1,0:T(8,128)(2,1)S(1)}, bf16[1024,128]{1,0:T(8,128)(2,1)S(1)}) custom-call(s32[1,16]{1,0:T(1,128)S(1)} %copy-done.2, bf16[1024,512]{1,0:T(8,128)(2,1)S(1)} %get-tuple-element.146.refs_0_, bf16[1024,512]{1,0:T(8,128)(2,1)S(1)} %get-tuple-element.147.refs_1_, ...), custom_call_target="tpu_custom_call" | custom-call | flops 1500000000 | bytes 1024 | tf_op jit(solution)/shard_map/first_back/pallas_call | solution.py:333
  88.8 1.6 %collective-permute-start.26 = (bf16[2,2,144,512]{3,2,1,0:T(8,128)(2,1)S(1)}, bf16[2,2,144,512]{3,2,1,0:T(8,128)(2,1)S(1)}, u32[]{:S(2)}, u32[]{:S(2)}) collective-permute-start(bf16[2,2,144,512]{3,2,1,0:T(8,128)(2,1)S(1)} %get-tuple-element.155), channel_id=1, source_target_pairs={{0,8},{1,9},{2,10},{3,11},{4,12},{5,13},{6,14},{7,15},{8,0},{9,1},... | collective-permute-start | bytes 1769480 | tf_op jit(solution)/shard_map/ppermute | solution.py:706
  90.9 13.2 %rest_back.1.grads_ref = bf16[3,1024,512]{2,1,0:T(8,128)(2,1)S(1)} custom-call(s32[1,16]{1,0:T(1,128)S(1)} %copy-done.2, bf16[1024,512]{1,0:T(8,128)(2,1)S(1)} %get-tuple-element.146.refs_0_, bf16[1024,512]{1,0:T(8,128)(2,1)S(1)} %get-tuple-element.147.refs_1_, bf16[1024,512]{1,0:T(8,128)(2,1)S(1)} %get-tuple-element.148.refs_2_, ...), custom_call_target="tpu_custom_call" | custom-call | flops 3500000000 | bytes 1024 | tf_op jit(solution)/shard_map/rest_back/pallas_call | solution.py:368
  104.4 1.2 collective-permute-done.27
  107.2 3.6 %weights.1 = (bf16[4,4,56,512]{3,2,1,0:T(8,128)(2,1)S(1)}, bf16[4,4,56,512]{3,2,1,0:T(8,128)(2,1)S(1)}) custom-call(s32[2]{0:T(128)S(1)} %pad_add_fusion.ids_ref, bf16[3,1024,512]{2,1,0:T(8,128)(2,1)S(1)} %rest_back.1.grads_ref, bf16[1024,512]{1,0:T(8,128)(2,1)S(1)} %copy-done, f32[16,512]{1,0:T(8,128)S(1)} %get-tuple-element.169.sums_ref), custom_call_target="tpu_custom_call" | custom-call | flops 1000000000 | bytes 1024 | tf_op jit(solution)/shard_map/weights/pallas_call | solution.py:430
  110.8 3.5 %collective-permute-done.28 = bf16[2,144,512]{2,1,0:T(8,128)(2,1)S(1)} collective-permute-done((bf16[2,144,512]{2,1,0:T(8,128)(2,1)S(1)}, bf16[2,144,512]{2,1,0:T(8,128)(2,1)S(1)}, u32[]{:S(2)}, u32[]{:S(2)}) %collective-permute-start.28) | collective-permute-done | bytes 294944 | tf_op jit(solution)/shard_map/ppermute | solution.py:706
  114.7 2.3 %collective-permute-done.30 = bf16[4,4,56,512]{3,2,1,0:T(8,128)(2,1)S(1)} collective-permute-done((bf16[4,4,56,512]{3,2,1,0:T(8,128)(2,1)S(1)}, bf16[4,4,56,512]{3,2,1,0:T(8,128)(2,1)S(1)}, u32[]{:S(2)}, u32[]{:S(2)}) %collective-permute-start.30) | collective-permute-done | bytes 917536 | tf_op jit(solution)/shard_map/ppermute | solution.py:706
  117.8 1.5 %collective-permute-start.32 = (bf16[4,56,512]{2,1,0:T(8,128)(2,1)S(1)}, bf16[4,56,512]{2,1,0:T(8,128)(2,1)S(1)}, u32[]{:S(2)}, u32[]{:S(2)}) collective-permute-start(bf16[4,56,512]{2,1,0:T(8,128)(2,1)S(1)} %get-tuple-element.175), channel_id=1, source_target_pairs={{0,16},{1,17},{2,18},{3,19},{4,20},{5,21},{6,22},{7,23},{8,24},{9,... | collective-permute-start | bytes 688136 | tf_op jit(solution)/shard_map/ppermute | solution.py:706
  119.3 1.4 collective-permute-start.33
  120.9 2.1 %collective-permute-start.36 = (bf16[1,144,512]{2,1,0:T(8,128)(2,1)S(1)}, bf16[1,144,512]{2,1,0:T(8,128)(2,1)S(1)}, u32[]{:S(2)}, u32[]{:S(2)}) collective-permute-start(bf16[1,144,512]{2,1,0:T(8,128)(2,1)S(1)} %get-tuple-element.209), channel_id=1, source_target_pairs={{0,6},{1,7},{2,4},{3,5},{4,2},{5,3},{6,0},{7,1},{8,14},{9,15},{10,... | collective-permute-start | bytes 442376 | tf_op jit(solution)/shard_map/ppermute | solution.py:706
  123.8 4.8 %input.1 = f32[1024,512]{1,0:T(8,128)} custom-call(s32[2]{0:T(128)S(1)} %pad_add_fusion.ids_ref, f32[1024,512]{1,0:T(8,128)S(1)} %copy-done.1, bf16[3,1024,512]{2,1,0:T(8,128)(2,1)S(1)} %rest_back.1.grads_ref, bf16[4,56,512]{2,1,0:T(8,128)(2,1)S(1)} %constant_dynamic-update-slice_fusion.refs_0_, bf16[4,56,512]{2,1,0:T(8,128)(2,1)S(1)} %collective-permute-done.8.refs_1_, ...), custom_call_target="tpu_custom_call" | custom-call | flops 1250000000 | bytes 1024 | tf_op jit(solution)/shard_map/input/pallas_call | solution.py:472
  128.7 1.6 %collective-permute-start.34 = (bf16[1,144,512]{2,1,0:T(8,128)(2,1)S(1)}, bf16[1,144,512]{2,1,0:T(8,128)(2,1)S(1)}, u32[]{:S(2)}, u32[]{:S(2)}) collective-permute-start(bf16[1,144,512]{2,1,0:T(8,128)(2,1)S(1)} %get-tuple-element.189), channel_id=1, source_target_pairs={{0,2},{1,3},{2,0},{3,1},{4,6},{5,7},{6,4},{7,5},{8,10},{9,11},{10,... | collective-permute-start | bytes 442376 | tf_op jit(solution)/shard_map/ppermute | solution.py:706
  130.9 3.9 %collective-permute-start.37 = (bf16[1,56,512]{2,1,0:T(8,128)(2,1)S(1)}, bf16[1,56,512]{2,1,0:T(8,128)(2,1)S(1)}, u32[]{:S(2)}, u32[]{:S(2)}) collective-permute-start(bf16[1,56,512]{2,1,0:T(8,128)(2,1)S(1)} %get-tuple-element.190), channel_id=1, source_target_pairs={{0,2},{1,3},{2,0},{3,1},{4,6},{5,7},{6,4},{7,5},{8,10},{9,11},{10,... | collective-permute-start | bytes 172040 | tf_op jit(solution)/shard_map/ppermute | solution.py:706
  135.4 1.8 %collective-permute-start.39 = (bf16[1,56,512]{2,1,0:T(8,128)(2,1)S(1)}, bf16[1,56,512]{2,1,0:T(8,128)(2,1)S(1)}, u32[]{:S(2)}, u32[]{:S(2)}) collective-permute-start(bf16[1,56,512]{2,1,0:T(8,128)(2,1)S(1)} %get-tuple-element.196), channel_id=1, source_target_pairs={{0,6},{1,7},{2,4},{3,5},{4,2},{5,3},{6,0},{7,1},{8,14},{9,15},{10,... | collective-permute-start | bytes 172040 | tf_op jit(solution)/shard_map/ppermute | solution.py:706
  138.2 1.2 collective-permute-done.37
  (103 shorter events, 21.0 us)
Async XLA Ops:
  2.4 8.4 %collective-permute-start.2 = (bf16[1,56,512]{2,1,0:T(8,128)(2,1)}, bf16[1,56,512]{2,1,0:T(8,128)(2,1)S(1)}, u32[]{:S(2)}, u32[]{:S(2)}) collective-permute-start(bf16[1,56,512]{2,1,0:T(8,128)(2,1)} %bitcast.92), channel_id=1, source_target_pairs={{0,4},{1,5},{2,6},{3,7},{4,0},{5,1},{6,2},{7,3},{8,12},{9,13},{10,... | collective-permute-start | bytes 172040 | tf_op jit(solution)/shard_map/ppermute | solution.py:706
  6.4 4.4 %collective-permute-start.1 = (bf16[1,56,512]{2,1,0:T(8,128)(2,1)}, bf16[1,56,512]{2,1,0:T(8,128)(2,1)S(1)}, u32[]{:S(2)}, u32[]{:S(2)}) collective-permute-start(bf16[1,56,512]{2,1,0:T(8,128)(2,1)} %bitcast.93), channel_id=1, source_target_pairs={{0,2},{1,3},{2,0},{3,1},{4,6},{5,7},{6,4},{7,5},{8,10},{9,11},{10,... | collective-permute-start | bytes 172040 | tf_op jit(solution)/shard_map/ppermute | solution.py:706
  8.0 6.8 %collective-permute-start.3 = (bf16[1,56,512]{2,1,0:T(8,128)(2,1)}, bf16[1,56,512]{2,1,0:T(8,128)(2,1)S(1)}, u32[]{:S(2)}, u32[]{:S(2)}) collective-permute-start(bf16[1,56,512]{2,1,0:T(8,128)(2,1)} %bitcast.94), channel_id=1, source_target_pairs={{0,6},{1,7},{2,4},{3,5},{4,2},{5,3},{6,0},{7,1},{8,14},{9,15},{10,... | collective-permute-start | bytes 172040 | tf_op jit(solution)/shard_map/ppermute | solution.py:706
  8.0 11.3 %collective-permute-start = (bf16[1,144,512]{2,1,0:T(8,128)(2,1)}, bf16[1,144,512]{2,1,0:T(8,128)(2,1)S(1)}, u32[]{:S(2)}, u32[]{:S(2)}) collective-permute-start(bf16[1,144,512]{2,1,0:T(8,128)(2,1)} %bitcast.91), channel_id=1, source_target_pairs={{0,4},{1,5},{2,6},{3,7},{4,0},{5,1},{6,2},{7,3},{8,12},{9,13},{10,... | collective-permute-start | bytes 442376 | tf_op jit(solution)/shard_map/ppermute | solution.py:706
  14.8 8.7 %collective-permute-start.10 = (bf16[4,56,512]{2,1,0:T(8,128)(2,1)S(1)}, bf16[4,56,512]{2,1,0:T(8,128)(2,1)S(1)}, u32[]{:S(2)}, u32[]{:S(2)}) collective-permute-start(bf16[4,56,512]{2,1,0:T(8,128)(2,1)S(1)} %constant_dynamic-update-slice_fusion.refs_0_), channel_id=1, source_target_pairs={{0,24},{1,25},{2,26},{3,27},{4,28},{5,29},{6,30},{7,31},{8,16},{9,... | collective-permute-start | bytes 688136 | tf_op jit(solution)/shard_map/ppermute | solution.py:706
  17.3 8.5 %collective-permute-start.9 = (bf16[4,56,512]{2,1,0:T(8,128)(2,1)S(1)}, bf16[4,56,512]{2,1,0:T(8,128)(2,1)S(1)}, u32[]{:S(2)}, u32[]{:S(2)}) collective-permute-start(bf16[4,56,512]{2,1,0:T(8,128)(2,1)S(1)} %constant_dynamic-update-slice_fusion.refs_0_), channel_id=1, source_target_pairs={{0,16},{1,17},{2,18},{3,19},{4,20},{5,21},{6,22},{7,23},{8,24},{9,... | collective-permute-start | bytes 688136 | tf_op jit(solution)/shard_map/ppermute | solution.py:706
  17.8 8.1 %collective-permute-start.8 = (bf16[4,56,512]{2,1,0:T(8,128)(2,1)S(1)}, bf16[4,56,512]{2,1,0:T(8,128)(2,1)S(1)}, u32[]{:S(2)}, u32[]{:S(2)}) collective-permute-start(bf16[4,56,512]{2,1,0:T(8,128)(2,1)S(1)} %constant_dynamic-update-slice_fusion.refs_0_), channel_id=1, source_target_pairs={{0,8},{1,9},{2,10},{3,11},{4,12},{5,13},{6,14},{7,15},{8,0},{9,1},... | collective-permute-start | bytes 688136 | tf_op jit(solution)/shard_map/ppermute | solution.py:706
  19.8 10.3 %collective-permute-start.5 = (bf16[2,144,512]{2,1,0:T(8,128)(2,1)S(1)}, bf16[2,144,512]{2,1,0:T(8,128)(2,1)S(1)}, u32[]{:S(2)}, u32[]{:S(2)}) collective-permute-start(bf16[2,144,512]{2,1,0:T(8,128)(2,1)S(1)} %constant_dynamic-update-slice_fusion.4), channel_id=1, source_target_pairs={{0,2},{1,3},{2,0},{3,1},{4,6},{5,7},{6,4},{7,5},{8,10},{9,11},{10,... | collective-permute-start | bytes 884744 | tf_op jit(solution)/shard_map/ppermute | solution.py:706
  23.4 9.9 %collective-permute-start.13 = (bf16[4,56,512]{2,1,0:T(8,128)(2,1)S(1)}, bf16[4,56,512]{2,1,0:T(8,128)(2,1)S(1)}, u32[]{:S(2)}, u32[]{:S(2)}) collective-permute-start(bf16[4,56,512]{2,1,0:T(8,128)(2,1)S(1)} %collective-permute-done.10.refs_3_), channel_id=1, source_target_pairs={{0,1},{1,0},{2,3},{3,2},{4,5},{5,4},{6,7},{7,6},{8,9},{9,8},{10,11... | collective-permute-start | bytes 688136 | tf_op jit(solution)/shard_map/ppermute | solution.py:706
  25.8 8.1 %collective-permute-start.12 = (bf16[4,56,512]{2,1,0:T(8,128)(2,1)S(1)}, bf16[4,56,512]{2,1,0:T(8,128)(2,1)S(1)}, u32[]{:S(2)}, u32[]{:S(2)}) collective-permute-start(bf16[4,56,512]{2,1,0:T(8,128)(2,1)S(1)} %collective-permute-done.9.refs_2_), channel_id=1, source_target_pairs={{0,1},{1,0},{2,3},{3,2},{4,5},{5,4},{6,7},{7,6},{8,9},{9,8},{10,11... | collective-permute-start | bytes 688136 | tf_op jit(solution)/shard_map/ppermute | solution.py:706
  25.9 8.5 %collective-permute-start.11 = (bf16[4,56,512]{2,1,0:T(8,128)(2,1)S(1)}, bf16[4,56,512]{2,1,0:T(8,128)(2,1)S(1)}, u32[]{:S(2)}, u32[]{:S(2)}) collective-permute-start(bf16[4,56,512]{2,1,0:T(8,128)(2,1)S(1)} %collective-permute-done.8.refs_1_), channel_id=1, source_target_pairs={{0,1},{1,0},{2,3},{3,2},{4,5},{5,4},{6,7},{7,6},{8,9},{9,8},{10,11... | collective-permute-start | bytes 688136 | tf_op jit(solution)/shard_map/ppermute | solution.py:706
  30.2 14.7 %collective-permute-start.7 = (bf16[2,144,512]{2,1,0:T(8,128)(2,1)S(1)}, bf16[2,144,512]{2,1,0:T(8,128)(2,1)S(1)}, u32[]{:S(2)}, u32[]{:S(2)}) collective-permute-start(bf16[2,144,512]{2,1,0:T(8,128)(2,1)S(1)} %get-tuple-element.218), channel_id=1, source_target_pairs={{0,16},{1,17},{2,18},{3,19},{4,20},{5,21},{6,22},{7,23},{8,24},{9,... | collective-permute-start | bytes 884744 | tf_op jit(solution)/shard_map/ppermute | solution.py:706
  31.8 13.2 %collective-permute-start.6 = (bf16[2,144,512]{2,1,0:T(8,128)(2,1)S(1)}, bf16[2,144,512]{2,1,0:T(8,128)(2,1)S(1)}, u32[]{:S(2)}, u32[]{:S(2)}) collective-permute-start(bf16[2,144,512]{2,1,0:T(8,128)(2,1)S(1)} %get-tuple-element.219), channel_id=1, source_target_pairs={{0,8},{1,9},{2,10},{3,11},{4,12},{5,13},{6,14},{7,15},{8,0},{9,1},... | collective-permute-start | bytes 884744 | tf_op jit(solution)/shard_map/ppermute | solution.py:706
  33.3 14.7 %collective-permute-start.15 = (bf16[2,144,512]{2,1,0:T(8,128)(2,1)S(1)}, bf16[2,144,512]{2,1,0:T(8,128)(2,1)S(1)}, u32[]{:S(2)}, u32[]{:S(2)}) collective-permute-start(bf16[2,144,512]{2,1,0:T(8,128)(2,1)S(1)} %get-tuple-element.218), channel_id=1, source_target_pairs={{0,8},{1,9},{2,10},{3,11},{4,12},{5,13},{6,14},{7,15},{8,0},{9,1},... | collective-permute-start | bytes 884744 | tf_op jit(solution)/shard_map/ppermute | solution.py:706
  33.9 14.2 %collective-permute-start.14 = (bf16[2,144,512]{2,1,0:T(8,128)(2,1)S(1)}, bf16[2,144,512]{2,1,0:T(8,128)(2,1)S(1)}, u32[]{:S(2)}, u32[]{:S(2)}) collective-permute-start(bf16[2,144,512]{2,1,0:T(8,128)(2,1)S(1)} %get-tuple-element.219), channel_id=1, source_target_pairs={{0,16},{1,17},{2,18},{3,19},{4,20},{5,21},{6,22},{7,23},{8,24},{9,... | collective-permute-start | bytes 884744 | tf_op jit(solution)/shard_map/ppermute | solution.py:706
  44.9 8.2 %collective-permute-start.16 = (bf16[2,144,512]{2,1,0:T(8,128)(2,1)S(1)}, bf16[2,144,512]{2,1,0:T(8,128)(2,1)S(1)}, u32[]{:S(2)}, u32[]{:S(2)}) collective-permute-start(bf16[2,144,512]{2,1,0:T(8,128)(2,1)S(1)} %collective-permute-done.6.refs_1_), channel_id=1, source_target_pairs={{0,16},{1,17},{2,18},{3,19},{4,20},{5,21},{6,22},{7,23},{8,24},{9,... | collective-permute-start | bytes 884744 | tf_op jit(solution)/shard_map/ppermute | solution.py:706
  46.5 7.1 %collective-permute-start.17 = (bf16[2,144,512]{2,1,0:T(8,128)(2,1)S(1)}, bf16[2,144,512]{2,1,0:T(8,128)(2,1)S(1)}, u32[]{:S(2)}, u32[]{:S(2)}) collective-permute-start(bf16[2,144,512]{2,1,0:T(8,128)(2,1)S(1)} %collective-permute-done.7.refs_4_), channel_id=1, source_target_pairs={{0,8},{1,9},{2,10},{3,11},{4,12},{5,13},{6,14},{7,15},{8,0},{9,1},... | collective-permute-start | bytes 884744 | tf_op jit(solution)/shard_map/ppermute | solution.py:706
  48.0 6.7 %collective-permute-start.18 = (bf16[4,144,512]{2,1,0:T(8,128)(2,1)S(1)}, bf16[4,144,512]{2,1,0:T(8,128)(2,1)S(1)}, u32[]{:S(2)}, u32[]{:S(2)}) collective-permute-start(bf16[4,144,512]{2,1,0:T(8,128)(2,1)S(1)} %bitcast.89), channel_id=1, source_target_pairs={{0,1},{1,0},{2,3},{3,2},{4,5},{5,4},{6,7},{7,6},{8,9},{9,8},{10,11... | collective-permute-start | bytes 1769480 | tf_op jit(solution)/shard_map/ppermute | solution.py:706
  82.9 4.8 %collective-permute-start.25 = (bf16[4,4,144,512]{3,2,1,0:T(8,128)(2,1)}, bf16[4,4,144,512]{3,2,1,0:T(8,128)(2,1)S(1)}, u32[]{:S(2)}, u32[]{:S(2)}) collective-permute-start(bf16[4,4,144,512]{3,2,1,0:T(8,128)(2,1)} %get-tuple-element.145), channel_id=1, source_target_pairs={{0,1},{1,0},{2,3},{3,2},{4,5},{5,4},{6,7},{7,6},{8,9},{9,8},{10,11... | collective-permute-start | bytes 7077896 | tf_op jit(solution)/shard_map/ppermute | solution.py:706
  88.8 15.6 %collective-permute-start.26 = (bf16[2,2,144,512]{3,2,1,0:T(8,128)(2,1)S(1)}, bf16[2,2,144,512]{3,2,1,0:T(8,128)(2,1)S(1)}, u32[]{:S(2)}, u32[]{:S(2)}) collective-permute-start(bf16[2,2,144,512]{3,2,1,0:T(8,128)(2,1)S(1)} %get-tuple-element.155), channel_id=1, source_target_pairs={{0,8},{1,9},{2,10},{3,11},{4,12},{5,13},{6,14},{7,15},{8,0},{9,1},... | collective-permute-start | bytes 1769480 | tf_op jit(solution)/shard_map/ppermute | solution.py:706
  90.4 15.3 %collective-permute-start.27 = (bf16[2,2,144,512]{3,2,1,0:T(8,128)(2,1)S(1)}, bf16[2,2,144,512]{3,2,1,0:T(8,128)(2,1)S(1)}, u32[]{:S(2)}, u32[]{:S(2)}) collective-permute-start(bf16[2,2,144,512]{3,2,1,0:T(8,128)(2,1)S(1)} %get-tuple-element.156), channel_id=1, source_target_pairs={{0,16},{1,17},{2,18},{3,19},{4,20},{5,21},{6,22},{7,23},{8,24},{9,... | collective-permute-start | bytes 1769480 | tf_op jit(solution)/shard_map/ppermute | solution.py:706
  106.0 8.2 %collective-permute-start.28 = (bf16[2,144,512]{2,1,0:T(8,128)(2,1)S(1)}, bf16[2,144,512]{2,1,0:T(8,128)(2,1)S(1)}, u32[]{:S(2)}, u32[]{:S(2)}) collective-permute-start(bf16[2,144,512]{2,1,0:T(8,128)(2,1)S(1)} %get-tuple-element.166), channel_id=1, source_target_pairs={{0,16},{1,17},{2,18},{3,19},{4,20},{5,21},{6,22},{7,23},{8,24},{9,... | collective-permute-start | bytes 884744 | tf_op jit(solution)/shard_map/ppermute | solution.py:706
  106.6 7.9 %collective-permute-start.29 = (bf16[2,144,512]{2,1,0:T(8,128)(2,1)S(1)}, bf16[2,144,512]{2,1,0:T(8,128)(2,1)S(1)}, u32[]{:S(2)}, u32[]{:S(2)}) collective-permute-start(bf16[2,144,512]{2,1,0:T(8,128)(2,1)S(1)} %get-tuple-element.167), channel_id=1, source_target_pairs={{0,8},{1,9},{2,10},{3,11},{4,12},{5,13},{6,14},{7,15},{8,0},{9,1},... | collective-permute-start | bytes 884744 | tf_op jit(solution)/shard_map/ppermute | solution.py:706
  117.2 11.5 %collective-permute-start.31 = (bf16[4,56,512]{2,1,0:T(8,128)(2,1)S(1)}, bf16[4,56,512]{2,1,0:T(8,128)(2,1)S(1)}, u32[]{:S(2)}, u32[]{:S(2)}) collective-permute-start(bf16[4,56,512]{2,1,0:T(8,128)(2,1)S(1)} %get-tuple-element.174), channel_id=1, source_target_pairs={{0,8},{1,9},{2,10},{3,11},{4,12},{5,13},{6,14},{7,15},{8,0},{9,1},... | collective-permute-start | bytes 688136 | tf_op jit(solution)/shard_map/ppermute | solution.py:706
  117.8 12.5 %collective-permute-start.32 = (bf16[4,56,512]{2,1,0:T(8,128)(2,1)S(1)}, bf16[4,56,512]{2,1,0:T(8,128)(2,1)S(1)}, u32[]{:S(2)}, u32[]{:S(2)}) collective-permute-start(bf16[4,56,512]{2,1,0:T(8,128)(2,1)S(1)} %get-tuple-element.175), channel_id=1, source_target_pairs={{0,16},{1,17},{2,18},{3,19},{4,20},{5,21},{6,22},{7,23},{8,24},{9,... | collective-permute-start | bytes 688136 | tf_op jit(solution)/shard_map/ppermute | solution.py:706
  119.3 11.4 %collective-permute-start.33 = (bf16[4,56,512]{2,1,0:T(8,128)(2,1)S(1)}, bf16[4,56,512]{2,1,0:T(8,128)(2,1)S(1)}, u32[]{:S(2)}, u32[]{:S(2)}) collective-permute-start(bf16[4,56,512]{2,1,0:T(8,128)(2,1)S(1)} %get-tuple-element.176), channel_id=1, source_target_pairs={{0,24},{1,25},{2,26},{3,27},{4,28},{5,29},{6,30},{7,31},{8,16},{9,... | collective-permute-start | bytes 688136 | tf_op jit(solution)/shard_map/ppermute | solution.py:706
  120.9 10.0 %collective-permute-start.36 = (bf16[1,144,512]{2,1,0:T(8,128)(2,1)S(1)}, bf16[1,144,512]{2,1,0:T(8,128)(2,1)S(1)}, u32[]{:S(2)}, u32[]{:S(2)}) collective-permute-start(bf16[1,144,512]{2,1,0:T(8,128)(2,1)S(1)} %get-tuple-element.209), channel_id=1, source_target_pairs={{0,6},{1,7},{2,4},{3,5},{4,2},{5,3},{6,0},{7,1},{8,14},{9,15},{10,... | collective-permute-start | bytes 442376 | tf_op jit(solution)/shard_map/ppermute | solution.py:706
  123.0 14.5 %collective-permute-start.35 = (bf16[1,144,512]{2,1,0:T(8,128)(2,1)S(1)}, bf16[1,144,512]{2,1,0:T(8,128)(2,1)S(1)}, u32[]{:S(2)}, u32[]{:S(2)}) collective-permute-start(bf16[1,144,512]{2,1,0:T(8,128)(2,1)S(1)} %get-tuple-element.211), channel_id=1, source_target_pairs={{0,4},{1,5},{2,6},{3,7},{4,0},{5,1},{6,2},{7,3},{8,12},{9,13},{10,... | collective-permute-start | bytes 442376 | tf_op jit(solution)/shard_map/ppermute | solution.py:706
  128.7 9.5 %collective-permute-start.34 = (bf16[1,144,512]{2,1,0:T(8,128)(2,1)S(1)}, bf16[1,144,512]{2,1,0:T(8,128)(2,1)S(1)}, u32[]{:S(2)}, u32[]{:S(2)}) collective-permute-start(bf16[1,144,512]{2,1,0:T(8,128)(2,1)S(1)} %get-tuple-element.189), channel_id=1, source_target_pairs={{0,2},{1,3},{2,0},{3,1},{4,6},{5,7},{6,4},{7,5},{8,10},{9,11},{10,... | collective-permute-start | bytes 442376 | tf_op jit(solution)/shard_map/ppermute | solution.py:706
  130.9 8.5 %collective-permute-start.37 = (bf16[1,56,512]{2,1,0:T(8,128)(2,1)S(1)}, bf16[1,56,512]{2,1,0:T(8,128)(2,1)S(1)}, u32[]{:S(2)}, u32[]{:S(2)}) collective-permute-start(bf16[1,56,512]{2,1,0:T(8,128)(2,1)S(1)} %get-tuple-element.190), channel_id=1, source_target_pairs={{0,2},{1,3},{2,0},{3,1},{4,6},{5,7},{6,4},{7,5},{8,10},{9,11},{10,... | collective-permute-start | bytes 172040 | tf_op jit(solution)/shard_map/ppermute | solution.py:706
  134.9 6.6 %collective-permute-start.38 = (bf16[1,56,512]{2,1,0:T(8,128)(2,1)S(1)}, bf16[1,56,512]{2,1,0:T(8,128)(2,1)S(1)}, u32[]{:S(2)}, u32[]{:S(2)}) collective-permute-start(bf16[1,56,512]{2,1,0:T(8,128)(2,1)S(1)} %get-tuple-element.195), channel_id=1, source_target_pairs={{0,4},{1,5},{2,6},{3,7},{4,0},{5,1},{6,2},{7,3},{8,12},{9,13},{10,... | collective-permute-start | bytes 172040 | tf_op jit(solution)/shard_map/ppermute | solution.py:706
  135.4 6.1 %collective-permute-start.39 = (bf16[1,56,512]{2,1,0:T(8,128)(2,1)S(1)}, bf16[1,56,512]{2,1,0:T(8,128)(2,1)S(1)}, u32[]{:S(2)}, u32[]{:S(2)}) collective-permute-start(bf16[1,56,512]{2,1,0:T(8,128)(2,1)S(1)} %get-tuple-element.196), channel_id=1, source_target_pairs={{0,6},{1,7},{2,4},{3,5},{4,2},{5,3},{6,0},{7,1},{8,14},{9,15},{10,... | collective-permute-start | bytes 172040 | tf_op jit(solution)/shard_map/ppermute | solution.py:706
  (14 other events, 62.3 us)
